TPU v7x, 32 devices: a whole 2x2x4 slice. The times are simulated.
32 devices in a mesh: groups: 2 (over y), pts: 4 (over z), freq: 2 (over x), sub: 2 (over core).
Axes of the slice: x: 2, y: 2, z: 4, core: 2. Of those that a mesh axis runs over, the one named last changes fastest.
Arguments:
- series: bfloat16 [2048, 8, 16384], P(('pts', 'sub'), 'freq', 'groups'), parts along dimension 2, may hold values from -256 to 256, as said below
- block_start: int32 [15], replicated, may hold values from 0 to 1792, as said below
- freq_index: int32 [64], replicated, may hold values from 0 to 128, as said below
Outputs:
- modes: float32 [2, 64, 16, 8192], P(None, 'freq', 'groups', ('pts', 'sub')), parts along dimension 2
- spectrum: float32 [128], P(('groups', 'freq')), parts along dimension 0
There are 2 independent parts, one for each index of `groups`. A program takes and returns all parts, laid end to end along the dimension named above; an argument that names none is the same for every part. Nothing has to cross between parts.
Inputs may be any that keep to these rules, and one draw needn't show every extreme that they name: series is finite. block_start rises with the block; its first entry is 0 and its last is 1792; every other entry lies within 32 of its block number times 128. freq_index holds 64 different bins, 0 and 128 among them.
All inputs are finite; a program needn't handle non-finite values.
Results may differ from a plain program's by a relative error of at most 0.0041.
Values may be sent and summed in bfloat16 or wider, within the bound.
No kernel may reach another device: no remote copies, remote signals or barrier semaphores. Data moves between devices by JAX's collectives and lax.ppermute only.
A program may use at most 128 MiB of HBM per device.

v0:
```python
import math

import jax
import jax.numpy as jnp
from jax import lax
from jax.sharding import PartitionSpec as P

NFFT = 256
ITERS = 3


def dft_basis(freq_index, window_len):
    steps_int = jnp.arange(window_len, dtype=jnp.int32)
    phase_int = freq_index[:, None] * steps_int[None, :] % window_len
    angle = 2.0 * math.pi / window_len * phase_int.astype(jnp.float32)
    window = 0.5 - 0.5 * jnp.cos(2.0 * math.pi / window_len * steps_int.astype(jnp.float32))
    weighting = window / jnp.sqrt(jnp.sum(window * window))
    table = jnp.stack([jnp.cos(angle), -jnp.sin(angle)], axis=1) * weighting[None, None, :]
    return table.reshape(-1, window_len).astype(jnp.bfloat16)


def apply_cross(cross_real, cross_imag, vec_real, vec_imag):
    highest = lax.Precision.HIGHEST
    out_real = jnp.einsum("kbd,kd->kb", cross_real, vec_real, precision=highest) - jnp.einsum(
        "kbd,kd->kb", cross_imag, vec_imag, precision=highest
    )
    out_imag = jnp.einsum("kbd,kd->kb", cross_real, vec_imag, precision=highest) + jnp.einsum(
        "kbd,kd->kb", cross_imag, vec_real, precision=highest
    )
    return (out_real, out_imag)


def leading_vector(cross_real, cross_imag, sweeps):
    initial = jnp.full(cross_real.shape[:2], 1.0 / math.sqrt(cross_real.shape[1]), jnp.float32)
    vec_real = initial
    vec_imag = jnp.zeros_like(initial)
    for sweep_index in range(sweeps):
        out_real, out_imag = apply_cross(cross_real, cross_imag, vec_real, vec_imag)
        length = jnp.sqrt(jnp.sum(out_real * out_real + out_imag * out_imag, axis=1, keepdims=True))
        vec_real = out_real / length
        vec_imag = out_imag / length
    out_real, out_imag = apply_cross(cross_real, cross_imag, vec_real, vec_imag)
    spectrum = jnp.sum(vec_real * out_real + vec_imag * out_imag, axis=1)
    return (vec_real, vec_imag, spectrum)


def cross_spectra(coefficients):
    product = jnp.einsum(
        "bkcxr,dkexr->kcebd", coefficients, coefficients, preferred_element_type=jnp.float32
    )
    return (product[:, 0, 0] + product[:, 1, 1], product[:, 0, 1] - product[:, 1, 0])


def project_modes(coefficients, vec_real, vec_imag):
    low_real = vec_real.astype(jnp.bfloat16)
    low_imag = vec_imag.astype(jnp.bfloat16)
    mixing = jnp.stack(
        [jnp.stack([low_real, low_imag], axis=1), jnp.stack([-low_imag, low_real], axis=1)], axis=1
    )
    raw_modes = jnp.einsum(
        "bkcxr,kceb->ekxr", coefficients, mixing, preferred_element_type=jnp.float32
    )
    return (low_real, low_imag, raw_modes)


def shards(series, block_start, freq_index):
    snap_rows, slab_rows, plane = series.shape
    group_count = lax.axis_size(("pts", "sub"))
    width = plane // group_count
    tiles_in = series.reshape(1, snap_rows, slab_rows, group_count, width)
    regrouped = lax.all_to_all(tiles_in, ("pts", "sub"), split_axis=3, concat_axis=0, tiled=True)
    history = regrouped.reshape(-1, slab_rows * width)
    basis = dft_basis(freq_index, NFFT)

    def one_block(carried, offset):
        segment = lax.dynamic_slice_in_dim(history, offset, NFFT, 0)
        return (
            carried,
            jnp.dot(basis, segment, preferred_element_type=jnp.float32).astype(jnp.bfloat16),
        )

    unused, tiles = lax.scan(one_block, jnp.int32(0), block_start)
    blocks = block_start.shape[0]
    retained = freq_index.shape[0]
    coefficients = tiles.reshape(blocks, retained, 2, slab_rows, width)
    total_points = slab_rows * lax.axis_size("freq") * plane
    norm_scale = 1.0 / (blocks * total_points)
    moved = lax.all_to_all(coefficients, "freq", split_axis=1, concat_axis=3, tiled=True)
    cross_real, cross_imag = cross_spectra(moved)
    cross_real, cross_imag = lax.psum((cross_real, cross_imag), ("pts", "sub"))
    cross_real = cross_real * norm_scale
    cross_imag = cross_imag * norm_scale
    vec_real, vec_imag, spectrum = leading_vector(cross_real, cross_imag, ITERS)
    low_real, low_imag, raw_modes = project_modes(moved, vec_real, vec_imag)
    partial_energy = jnp.sum(raw_modes[0] * raw_modes[0] + raw_modes[1] * raw_modes[1], axis=(1, 2))
    energy = lax.psum(partial_energy, ("pts", "sub")) / total_points
    modes = raw_modes * lax.rsqrt(energy + 1e-06)[None, :, None, None]
    return (modes, spectrum)


def solution(mesh):
    in_specs = (P(("pts", "sub"), "freq", "groups"), P(), P())
    out_specs = (P(None, "freq", "groups", ("pts", "sub")), P(("groups", "freq")))
    return jax.shard_map(shards, mesh=mesh, in_specs=in_specs, out_specs=out_specs, check_vma=False)
```

profile of v0, /device:TPU:0, one launch (start us, length us, event | category | flops | bytes accessed | tf_op | source)
XLA Modules:
  0.0 892.3 jit_solution(4202417993309503555)
XLA Ops:
  0.6 26.1 %copy.95 = bf16[256,4,8192]{0,2,1:T(8,128)(2,1)} copy(bf16[256,4,8192]{2,1,0:T(4,128)(2,1)} %param.5) | data formatting | bytes 33554432 | tf_op args[0]
  26.8 28.1 %copy.96 = bf16[1,256,4,8,1024]{4,2,1,0,3:T(4,128)(2,1)} copy(bf16[1,256,4,8,1024]{1,4,3,2,0:T(8,128)(2,1)} %bitcast.127) | data formatting | bytes 33554432 | tf_op jit(solution)/shard_map/reshape | solution.py:70
  54.8 6.5 all-to-all-start
  63.3 361.8 %all-to-all-done = bf16[1,256,4,8,1024]{4,2,1,0,3:T(4,128)(2,1)} async-done(((bf16[1,256,4,8,1024]{4,2,1,0,3:T(4,128)(2,1)}), bf16[1,256,4,8,1024]{4,2,1,0,3:T(4,128)(2,1)}, u32[]{:S(2)}, u32[]{:S(2)}) %all-to-all-start) | async-done | bytes 16777248 | tf_op jit(solution)/shard_map/all_to_all | solution.py:71
  425.1 17.0 %copy.198 = bf16[256,8,4,1024]{3,1,2,0:T(8,128)(2,1)} copy(bf16[256,8,4,1024]{3,2,1,0:T(4,128)(2,1)} %bitcast.56) | data formatting | bytes 33554432
  442.2 97.7 %while.10 = (s32[]{:T(128)}, bf16[15,128,4096]{2,1,0:T(8,128)(2,1)}, s32[15]{0:T(128)S(1)}, bf16[2048,4096]{1,0:T(8,128)(2,1)}, bf16[128,256]{1,0:T(8,128)(2,1)S(1)}, /*index=5*/s32[]{:T(128)}, s32[]{:T(128)}, s32[]{:T(128)}) while((s32[]{:T(128)}, bf16[15,128,4096]{2,1,0:T(8,128)(2,1)}, s32[15]{0:T(128)S(1)}, bf16[2048,4096]{1,0:T(8,128)(2,1)}, ...), condition=%wide.region_2.3_spmd, body=%wide.region_1.2_spmd.sunk | while | flops 268959744 | bytes 7406215 | solution.py:82
  444.7 2.4 fusion.52
  470.8 2.4 fusion.52
  477.3 2.4 fusion.52
  483.7 2.4 fusion.52
  490.3 2.4 fusion.52
  503.3 2.4 fusion.52
  509.8 2.4 fusion.52
  516.4 2.4 fusion.52
  529.4 2.4 fusion.52
  539.9 26.2 %reshape.139 = bf16[15,64,2,4,1024]{4,3,2,1,0:T(4,128)(2,1)} reshape(bf16[15,128,4096]{2,1,0:T(8,128)(2,1)} %get-tuple-element.29) | data formatting | bytes 31457280 | tf_op jit(solution)/shard_map/reshape | solution.py:85
  566.1 8.3 copy.99
  574.4 175.4 %all_to_all.33 = bf16[15,64,2,4,1024]{4,3,2,0,1:T(4,128)(2,1)S(1)} all-to-all(bf16[15,64,2,4,1024]{4,3,2,0,1:T(4,128)(2,1)S(1)} %copy.99), channel_id=1, replica_groups=mesh['groups'=2,'pts'=4,'freq'=2,'sub'=2] {'freq'}, dimensions={1} | all-to-all | bytes 31457280 | tf_op jit(solution)/shard_map/all_to_all | solution.py:88
  749.8 21.2 %copy.100 = bf16[15,64,2,4,1024]{4,1,3,2,0:T(8,128)(2,1)S(1)} copy(bf16[15,64,2,4,1024]{4,3,2,0,1:T(4,128)(2,1)S(1)} %all_to_all.33) | data formatting | bytes 31457280 | tf_op jit(solution)/shard_map/all_to_all | solution.py:88
  771.0 20.8 %copy.101 = bf16[15,32,2,2,4,1024]{5,0,4,3,2,1:T(8,128)(2,1)} copy(bf16[15,32,2,2,4,1024]{5,1,3,4,2,0:T(8,128)(2,1)S(1)} %bitcast.128) | data formatting | bytes 31457280 | tf_op jit(solution)/shard_map/all_to_all | solution.py:88
  791.8 34.2 %convolution_bitcast_fusion = f32[32,2,2,15,15]{3,4,1,2,0:T(8,128)S(1)} fusion(bf16[15,32,2,8,1024,1]{4,0,3,5,2,1:T(8,128)(2,1)} %bitcast.130, bf16[15,32,2,8,1024,1]{4,0,3,2,5,1:T(8,128)(2,1)} %bitcast.131), kind=kOutput, calls=%fused_computation.8 | convolution fusion | flops 471859200 | bytes 31572480 | tf_op jit(solution)/shard_map/bkcxr,dkexr->kcebd/dot_general | solution.py:48
  826.1 33.5 %all-reduce = (f32[32,15,15]{1,2,0:T(8,128)S(1)}, f32[32,15,15]{1,2,0:T(8,128)S(1)}) all-reduce(f32[32,15,15]{1,2,0:T(8,128)S(1)} %fusion.12, f32[32,15,15]{1,2,0:T(8,128)S(1)} %fusion.10), channel_id=1, replica_groups=mesh['groups'=2,'pts'=4,'freq'=2,'sub'=2] {'pts','sub'}, use_global_device_ids=true, to_apply=%region_3.4 | all-reduce | flops 14400 | bytes 115200 | tf_op jit(solution)/shard_map/psum | solution.py:90
  864.6 8.1 fusion.5
  874.9 13.6 %psum.23 = f32[32]{0:T(128)S(1)} all-reduce(f32[32]{0:T(128)S(1)} %fusion.9), channel_id=1, replica_groups=mesh['groups'=2,'pts'=4,'freq'=2,'sub'=2] {'pts','sub'}, use_global_device_ids=true, to_apply=%region_9.10 | all-reduce | flops 32 | bytes 256 | tf_op jit(solution)/shard_map/psum | solution.py:96
  (117 shorter events, 59.0 us)
Async XLA Ops:
  54.8 6.5 copy-start
  54.8 370.3 %all-to-all-start = ((bf16[1,256,4,8,1024]{4,2,1,0,3:T(4,128)(2,1)}), bf16[1,256,4,8,1024]{4,2,1,0,3:T(4,128)(2,1)}, u32[]{:S(2)}, u32[]{:S(2)}) async-start(bf16[1,256,4,8,1024]{4,2,1,0,3:T(4,128)(2,1)} %copy.96), calls=%async_computation | async-start | bytes 33554432 | tf_op jit(solution)/shard_map/all_to_all | solution.py:71
  425.1 17.0 %copy-start.1 = (s32[15]{0:T(128)S(1)}, s32[15]{0:T(128)}, u32[]{:S(2)}) copy-start(s32[15]{0:T(128)} %param.6) | copy-start | bytes 184
where the time goes:
time: 896 us; the launch traced here: 892 us
  waiting for transfers between devices  362 us (40%)
  blocking collectives  223 us (25%)
  local copies, waits for them, and re-layouts  184 us (21%)
  matrix products  79.6 us (9%)
  loops' own time  29.4 us (3%)
    all_to_all x1, waiting for transfers between devices, shards(): lax.all_to_all(tiles_in, ('pts', 'sub'), split_axis=3, concat_axis=0, til...  362 us
    all_to_all x1, blocking collectives, shards(): lax.all_to_all(coefficients, 'freq', split_axis=1, concat_axis=3, tiled=T...  175 us
    unnamed x13, local copies, waits for them, and re-layouts  45.6 us
    all_to_all x2, local copies, waits for them, and re-layouts, shards(): lax.all_to_all(coefficients, 'freq', split_axis=1, concat_axis=3, tiled=T...  42 us
    dot_general x15, matrix products, one_block(): jnp.dot(basis, segment, preferred_element_type=jnp.float32)  35.7 us
    reshape x2, local copies, waits for them, and re-layouts, shards(): coefficients = tiles.reshape(blocks, retained, 2, slab_rows, width)  34.5 us
    dot_general x1, matrix products, cross_spectra(): jnp.einsum('bkcxr,dkexr->kcebd', coefficients, coefficients, preferred_el...  34.2 us
    psum x1, blocking collectives, shards(): cross_real, cross_imag = lax.psum((cross_real, cross_imag), ('pts', 'sub'))  33.5 us
  transfers between devices with their start and end apart: 1, of which 1 were waited for; matrix products, arithmetic and copies ran while one was open for 0% of the time, Pallas kernels for 0%

commit v1 on v0

v1 whole, which is shorter than its diff:
```python
import functools
import math

import jax
import jax.numpy as jnp
from jax import lax
from jax.experimental import pallas as pl
from jax.experimental.pallas import tpu as pltpu
from jax.sharding import PartitionSpec as P

NFFT = 256
ITERS = 3
SPAN = 2 * NFFT
LANES = 128
SUBLANES = 8
GROUP_ROWS = 2 * SUBLANES
MIB = 1 << 20


def shifted_basis(freq_order, offsets, blocks):
    steps = jnp.arange(SPAN, dtype=jnp.int32)[None, :] - offsets[:, None]
    inside = (steps >= 0) & (steps < NFFT) & (jnp.arange(offsets.shape[0]) < blocks)[:, None]
    steps = jnp.where(inside, steps, 0)
    unit = 2.0 * math.pi / NFFT
    window = 0.5 - 0.5 * jnp.cos(unit * jnp.arange(NFFT, dtype=jnp.int32).astype(jnp.float32))
    shifted_window = 0.5 - 0.5 * jnp.cos(unit * steps.astype(jnp.float32))
    weighting = jnp.where(inside, shifted_window / jnp.sqrt(jnp.sum(window * window)), 0.0)
    freq = freq_order.reshape(1, -1, SUBLANES, 1)
    phase_int = freq * steps[:, None, None, :] % NFFT
    angle = unit * phase_int.astype(jnp.float32)
    table = jnp.stack([jnp.cos(angle), -jnp.sin(angle)], axis=2) * weighting[:, None, None, None, :]
    return table.astype(jnp.bfloat16).reshape(offsets.shape[0] // 2, -1, SPAN)


def spectra_kernel(window_start, history, basis, total_in, *outs, members):
    coefs = outs[:members]
    total_out = outs[members]
    rows = coefs[0].shape[1]
    pairs = basis.shape[0]
    width = history.shape[1]
    for pair in range(pairs):
        start = pl.multiple_of(window_start[pair], 16)
        segment = history[pl.ds(start, SPAN), :]
        both = jnp.dot(basis[pair], segment, preferred_element_type=jnp.float32)
        both = both.astype(jnp.bfloat16)
        for half in range(2):
            for member in range(members):
                first = (half * members + member) * rows
                coefs[member][2 * pair + half] = both[first : first + rows]
    lane = lax.broadcasted_iota(jnp.int32, (2 * pairs * SUBLANES, LANES), 1)
    sub = lax.broadcasted_iota(jnp.int32, (2 * pairs * SUBLANES, LANES), 0) % SUBLANES
    place = (lane - sub) & (LANES - 1)
    for member in range(members):
        packed = [jnp.zeros((2 * pairs * SUBLANES, LANES), jnp.float32) for _ in range(2)]
        for group in range(rows // GROUP_ROWS):
            tile = coefs[member][:, group * GROUP_ROWS : (group + 1) * GROUP_ROWS, :]
            tile = tile.reshape(2 * pairs * GROUP_ROWS, width)
            gram = lax.dot_general(
                tile, tile, (((1,), (1,)), ((), ())), preferred_element_type=jnp.float32
            )
            gram = gram.reshape(2 * pairs, 2, SUBLANES, 2 * LANES)
            for c in range(2):
                for high in range(2):
                    shift = group + 4 * high
                    part = gram[:, c, :, high * LANES : (high + 1) * LANES]
                    part = part.reshape(2 * pairs * SUBLANES, LANES)
                    part = pltpu.roll(part, shift, 1) if shift else part
                    packed[c] = jnp.where(place % 8 == shift, part, packed[c])
        swapped = jnp.where(
            (place // 8) % 2 == 0,
            pltpu.roll(packed[1], LANES - 8, 1),
            -pltpu.roll(packed[1], 8, 1),
        )
        total_out[member] = total_in[member] + (packed[0] + swapped)


def spectra(window_start, history, basis, total, members):
    width = history.shape[1]
    blocks = 2 * basis.shape[0]
    rows = basis.shape[1] // 2 // members
    vmem = pl.BlockSpec(memory_space=pltpu.VMEM)
    outs = [jax.ShapeDtypeStruct((blocks, rows, width), jnp.bfloat16)] * members
    return pl.pallas_call(
        functools.partial(spectra_kernel, members=members),
        out_shape=outs + [jax.ShapeDtypeStruct(total.shape, jnp.float32)],
        in_specs=[pl.BlockSpec(memory_space=pltpu.SMEM), vmem, vmem, vmem],
        out_specs=[vmem] * (members + 1),
        compiler_params=pltpu.CompilerParams(vmem_limit_bytes=40 * MIB),
        cost_estimate=pl.CostEstimate(
            flops=2 * blocks * members * rows * width * (SPAN + 256),
            bytes_accessed=2 * (history.size + basis.size + blocks * members * rows * width),
            transcendentals=0,
        ),
        name="spectra",
    )(window_start, history, basis, total)


def power_kernel(total, mix, scale, spectrum, *, blocks, norm_scale):
    padded = total.shape[0] // SUBLANES
    cross = total[...].reshape(padded, SUBLANES, LANES) * norm_scale
    shape = (SUBLANES, LANES)
    lane = lax.broadcasted_iota(jnp.int32, shape, 1)
    sub = lax.broadcasted_iota(jnp.int32, shape, 0)
    place = (lane - sub) & (LANES - 1)
    number = place // 16 + 8 * ((place // 4) % 2)
    is_real = (place // 8) % 2 == 0

    def lane_sum(value):
        for shift in (64, 32, 16, 8, 4):
            value = value + pltpu.roll(value, shift, value.ndim - 1)
        return value

    def turned(vec):
        for_real = jnp.where(is_real, vec, -vec)
        for_imag = jnp.where(is_real, pltpu.roll(vec, LANES - 8, 1), pltpu.roll(vec, 8, 1))
        return for_real, for_imag

    def apply(vec):
        for_real, for_imag = turned(vec)
        out_real = lane_sum(cross * for_real[None])
        out_imag = lane_sum(cross * for_imag[None])
        out = jnp.zeros(shape, jnp.float32)
        for block in range(padded):
            out = jnp.where(number == block, jnp.where(is_real, out_real[block], out_imag[block]), out)
        return out

    vec = jnp.where(is_real & (number < blocks), 1.0 / math.sqrt(blocks), 0.0)
    for _ in range(ITERS):
        out = apply(vec)
        vec = out / jnp.sqrt(lane_sum(out * out))
    value = lane_sum(vec * apply(vec))
    low = vec.astype(jnp.bfloat16).astype(jnp.float32)
    energy = lane_sum(low * apply(low)) * blocks
    factor = lax.rsqrt(jnp.maximum(energy, 0.0) + 1e-06)

    def spread(values, group):
        picked = jnp.where(place % 4 == group, values, 0.0)
        picked = picked + pltpu.roll(picked, 1, 1)
        return picked + pltpu.roll(picked, 2, 1)

    for_real, for_imag = turned(low)
    diagonal = lane % SUBLANES == sub
    for group in range(mix.shape[0]):
        parts = []
        for vec_part in (for_real, for_imag):
            row = []
            for high in range(2):
                shift = (LANES - group - 4 * high) % LANES
                moved = pltpu.roll(vec_part, shift, 1) if shift else vec_part
                row.append(jnp.where(diagonal, moved, 0.0))
            parts.append(jnp.concatenate(row, axis=1))
        mix[group] = jnp.concatenate(parts, axis=0).astype(jnp.bfloat16)
        scale[group] = spread(factor, group)
        spectrum[group] = spread(value, group)


def leading_vectors(total, groups, blocks, norm_scale):
    vmem = pl.BlockSpec(memory_space=pltpu.VMEM)
    return pl.pallas_call(
        functools.partial(power_kernel, blocks=blocks, norm_scale=norm_scale),
        out_shape=[
            jax.ShapeDtypeStruct((groups, GROUP_ROWS, 2 * LANES), jnp.bfloat16),
            jax.ShapeDtypeStruct((groups, SUBLANES, LANES), jnp.float32),
            jax.ShapeDtypeStruct((groups, SUBLANES, LANES), jnp.float32),
        ],
        in_specs=[vmem],
        out_specs=[vmem] * 3,
        name="power",
    )(total)


def modes_kernel(member_ref, mix, scale, *refs, chunks, members):
    coefs = refs[: chunks * members]
    out, buffer, sems = refs[chunks * members :]
    member = member_ref[0]
    copies = []
    for chunk in range(chunks):
        for turn in range(members):
            slot = lax.rem(member + members - turn, members)
            copy = pltpu.make_async_copy(
                coefs[chunk * members + turn], buffer.at[chunk, slot], sems.at[chunk, turn]
            )
            copy.start()
            copies.append(copy)
    width = coefs[0].shape[2]
    padded = coefs[0].shape[0]
    planes = out.shape[2] // members
    points = width // planes
    for chunk in range(chunks):
        for turn in range(members):
            copies[chunk * members + turn].wait()
        for slot in range(members):
            for group in range(mix.shape[0]):
                tile = buffer[chunk, slot, :, group * GROUP_ROWS : (group + 1) * GROUP_ROWS, :]
                tile = tile.reshape(padded * GROUP_ROWS, width)
                raw = jnp.dot(mix[group], tile, preferred_element_type=jnp.float32)
                for e in range(2):
                    for plane in range(planes):
                        part = raw[
                            e * SUBLANES : (e + 1) * SUBLANES, plane * points : (plane + 1) * points
                        ]
                        out[
                            e,
                            group * SUBLANES : (group + 1) * SUBLANES,
                            slot * planes + plane,
                            chunk * points : (chunk + 1) * points,
                        ] = part * jnp.tile(scale[group], (1, points // LANES))


def project(member, mix, scale, coefs, members, planes, points):
    chunks = len(coefs) // members
    groups = mix.shape[0]
    vmem = pl.BlockSpec(memory_space=pltpu.VMEM)
    return pl.pallas_call(
        functools.partial(modes_kernel, chunks=chunks, members=members),
        out_shape=jax.ShapeDtypeStruct(
            (2, groups * SUBLANES, members * planes, points), jnp.float32
        ),
        in_specs=[pl.BlockSpec(memory_space=pltpu.SMEM), vmem, vmem]
        + [pl.BlockSpec(memory_space=pl.ANY)] * len(coefs),
        out_specs=vmem,
        scratch_shapes=[
            pltpu.VMEM((chunks, members) + coefs[0].shape, jnp.bfloat16),
            pltpu.SemaphoreType.DMA((chunks, members)),
        ],
        compiler_params=pltpu.CompilerParams(vmem_limit_bytes=48 * MIB),
        name="modes",
    )(member, mix, scale, *coefs)


def butterfly_sum(value, axes, count):
    step = 1
    while step < count:
        pairs = [(i, i ^ step) for i in range(count)]
        value = value + lax.ppermute(value, axes, pairs)
        step *= 2
    return value


def shards(series, block_start, freq_index):
    snap_rows, slab_rows, plane = series.shape
    line = ("pts", "sub")
    group_count = lax.axis_size(line)
    members = lax.axis_size("freq")
    member = lax.axis_index("freq")
    width = plane // group_count
    chunk_points = LANES
    chunks = width // chunk_points
    blocks = block_start.shape[0]
    pairs = (blocks + 1) // 2
    frames = snap_rows * group_count

    order = (member + jnp.arange(members, dtype=jnp.int32)) % members
    freq_order = freq_index.reshape(members, -1)[order].reshape(-1)
    starts = jnp.pad(block_start, (0, 2 * pairs - blocks), mode="edge")
    window_start = jnp.minimum(starts[::2] // 16 * 16, frames - SPAN)
    basis = shifted_basis(freq_order, starts - jnp.repeat(window_start, 2), blocks)

    tiles = series.reshape(snap_rows, slab_rows, group_count, chunks, chunk_points)
    total = jnp.zeros((members, 2 * pairs * SUBLANES, LANES), jnp.float32)
    coefs = []
    for chunk in range(chunks):
        piece = jnp.transpose(tiles[:, :, :, chunk, :], (2, 0, 1, 3))
        piece = piece.reshape(group_count, snap_rows, slab_rows * chunk_points)
        history = lax.all_to_all(piece, line, split_axis=0, concat_axis=0, tiled=True)
        history = history.reshape(frames, slab_rows * chunk_points)
        *sent, total = spectra(window_start, history, basis, total, members)
        coefs.append(sent[0])
        for turn in range(1, members):
            ring = [(i, (i + turn) % members) for i in range(members)]
            coefs.append(lax.ppermute(sent[turn], "freq", ring))

    mine = total[0]
    for turn in range(1, members):
        ring = [(i, (i + turn) % members) for i in range(members)]
        mine = mine + lax.ppermute(total[turn], "freq", ring)
    mine = butterfly_sum(mine, line, group_count)

    groups = freq_index.shape[0] // members // SUBLANES
    norm_scale = 1.0 / (blocks * slab_rows * members * plane)
    mix, scale, spectrum = leading_vectors(mine, groups, blocks, norm_scale)
    modes = project(member.reshape(1), mix, scale, coefs, members, slab_rows, width)
    return (modes, spectrum[:, :, 0].reshape(-1))


def solution(mesh):
    in_specs = (P(("pts", "sub"), "freq", "groups"), P(), P())
    out_specs = (P(None, "freq", "groups", ("pts", "sub")), P(("groups", "freq")))
    return jax.shard_map(shards, mesh=mesh, in_specs=in_specs, out_specs=out_specs, check_vma=False)
```

time: 896 us -> 651 us (0.73)
  blocking collectives: 223 us -> 0 us
  matrix products: 79.6 us -> 0 us
  local copies, waits for them, and re-layouts: 184 us -> 111 us
  waiting for transfers between devices: 362 us -> 433 us
  starting transfers between devices: 6.46 us -> 50.4 us
  Pallas kernels: 0 us -> 40.4 us
  loops' own time: 29.4 us -> 0 us
    all_to_all x1 -> x0, blocking collectives: 175 us -> none  [shards(): lax.all_to_all(coefficients, 'freq', split_axis=1, concat_axis=3, tiled=T...]
    ppermute x0 -> x12, waiting for transfers between devices: none -> 110 us  [the longest x8 100 us: shards(): coefs.append(lax.ppermute(sent[turn], 'freq', ring))]
    dot_general x21 -> x0, matrix products: 79.6 us -> none  [the longest x15 35.7 us: one_block(): jnp.dot(basis, segment, preferred_element_type=jnp.float32)]
    reshape x3 -> x2, local copies, waits for them, and re-layouts: 62.6 us -> 0.16 us  [the longest x1 0.08 us: shards(): jnp.repeat(window_start, 2)]
    psum x2 -> x0, blocking collectives: 47.1 us -> none  [the longest x1 33.5 us: shards(): cross_real, cross_imag = lax.psum((cross_real, cross_imag), ('pts', 'sub'))]
    pallas_call x0 -> x10, Pallas kernels: none -> 40.4 us  [the longest x8 28.7 us: spectra(): pl.pallas_call(functools.partial(spectra_kernel, members=members), out_sh...]
    all_to_all x1 -> x8, waiting for transfers between devices: 362 us -> 323 us  [shards(): lax.all_to_all(piece, line, split_axis=0, concat_axis=0, tiled=True)]
    transpose x0 -> x9, local copies, waits for them, and re-layouts: none -> 33 us  [shards(): piece = jnp.transpose(tiles[:, :, :, chunk, :], (2, 0, 1, 3))]
  transfers between devices with their start and end apart: 1 -> 20, of which waited for: 1 -> 16; matrix products, arithmetic and copies ran while one was open for 0% -> 10% of each run, Pallas kernels for 0% -> 5%
where the time goes in v1:
time: 651 us; the launch traced here: 649 us
  waiting for transfers between devices  433 us (67%)
  local copies, waits for them, and re-layouts  111 us (17%)
  starting transfers between devices  50.4 us (8%)
  Pallas kernels  40.4 us (6%)
  other arithmetic  11.9 us (2%)
    all_to_all x8, waiting for transfers between devices, shards(): lax.all_to_all(piece, line, split_axis=0, concat_axis=0, tiled=True)  323 us
    ppermute x8, waiting for transfers between devices, shards(): coefs.append(lax.ppermute(sent[turn], 'freq', ring))  100 us
    unnamed x47, local copies, waits for them, and re-layouts  43.9 us
    all_to_all x8, starting transfers between devices, shards(): lax.all_to_all(piece, line, split_axis=0, concat_axis=0, tiled=True)  37.1 us
    transpose x9, local copies, waits for them, and re-layouts, shards(): piece = jnp.transpose(tiles[:, :, :, chunk, :], (2, 0, 1, 3))  33 us
    all_to_all x8, local copies, waits for them, and re-layouts, shards(): lax.all_to_all(piece, line, split_axis=0, concat_axis=0, tiled=True)  31.4 us
    pallas_call x8, Pallas kernels, spectra(): pl.pallas_call(functools.partial(spectra_kernel, members=members), out_sh...  28.7 us
  transfers between devices with their start and end apart: 20, of which 16 were waited for; matrix products, arithmetic and copies ran while one was open for 10% of the time, Pallas kernels for 5%

profile of v1, /device:TPU:0, one launch (start us, length us, event | category | flops | bytes accessed | tf_op | source)
XLA Modules:
  0.0 648.6 jit_solution(16017089259548796804)
XLA Ops:
  0.6 26.1 %copy.13 = bf16[256,4,8192]{0,2,1:T(8,128)(2,1)} copy(bf16[256,4,8192]{2,1,0:T(4,128)(2,1)} %param.3) | data formatting | bytes 33554432 | tf_op args[0]
  26.8 10.9 %slice_bitcast_fusion = (bf16[8,256,4,128]{1,3,0,2:T(8,128)(2,1)}, bf16[8,256,4,128]{1,3,0,2:T(8,128)(2,1)}, bf16[8,256,4,128]{1,3,0,2:T(8,128)(2,1)}, bf16[8,25...) fusion(bf16[256,4,8,8,128]{0,4,3,2,1:T(8,128)(2,1)} %bitcast.73), kind=kLoop, calls=%fused_computation.11 | loop fusion | bytes 33554432 | tf_op jit(solution)/shard_map/transpose | solution.py:263
  39.1 6.3 all-to-all-start
  48.6 46.0 %all-to-all-done = bf16[8,256,512]{1,2,0:T(8,128)(2,1)} async-done(((bf16[8,256,512]{1,2,0:T(8,128)(2,1)}), bf16[8,256,512]{1,2,0:T(8,128)(2,1)}, u32[]{:S(2)}, u32[]{:S(2)}) %all-to-all-start) | async-done | bytes 2097184 | tf_op jit(solution)/shard_map/all_to_all | solution.py:265
  94.6 4.4 all-to-all-start.2
  102.2 45.9 %all-to-all-done.2 = bf16[8,256,512]{1,2,0:T(8,128)(2,1)} async-done(((bf16[8,256,512]{1,2,0:T(8,128)(2,1)}), bf16[8,256,512]{1,2,0:T(8,128)(2,1)}, u32[]{:S(2)}, u32[]{:S(2)}) %all-to-all-start.2) | async-done | bytes 2097184 | tf_op jit(solution)/shard_map/all_to_all | solution.py:265
  155.6 45.9 %all-to-all-done.3 = bf16[8,256,512]{1,2,0:T(8,128)(2,1)} async-done(((bf16[8,256,512]{1,2,0:T(8,128)(2,1)}), bf16[8,256,512]{1,2,0:T(8,128)(2,1)}, u32[]{:S(2)}, u32[]{:S(2)}) %all-to-all-start.3) | async-done | bytes 2097184 | tf_op jit(solution)/shard_map/all_to_all | solution.py:265
  201.5 4.4 all-to-all-start.4
  209.1 45.8 %all-to-all-done.4 = bf16[8,256,512]{1,2,0:T(8,128)(2,1)} async-done(((bf16[8,256,512]{1,2,0:T(8,128)(2,1)}), bf16[8,256,512]{1,2,0:T(8,128)(2,1)}, u32[]{:S(2)}, u32[]{:S(2)}) %all-to-all-start.4) | async-done | bytes 2097184 | tf_op jit(solution)/shard_map/all_to_all | solution.py:265
  254.9 4.4 all-to-all-start.5
  262.4 45.9 %all-to-all-done.5 = bf16[8,256,512]{1,2,0:T(8,128)(2,1)} async-done(((bf16[8,256,512]{1,2,0:T(8,128)(2,1)}), bf16[8,256,512]{1,2,0:T(8,128)(2,1)}, u32[]{:S(2)}, u32[]{:S(2)}) %all-to-all-start.5) | async-done | bytes 2097184 | tf_op jit(solution)/shard_map/all_to_all | solution.py:265
  308.4 4.3 all-to-all-start.6
  315.9 45.9 %all-to-all-done.6 = bf16[8,256,512]{1,2,0:T(8,128)(2,1)} async-done(((bf16[8,256,512]{1,2,0:T(8,128)(2,1)}), bf16[8,256,512]{1,2,0:T(8,128)(2,1)}, u32[]{:S(2)}, u32[]{:S(2)}) %all-to-all-start.6) | async-done | bytes 2097184 | tf_op jit(solution)/shard_map/all_to_all | solution.py:265
  361.8 4.3 all-to-all-start.7
  367.7 47.5 %all-to-all-done.7 = bf16[8,256,512]{1,2,0:T(8,128)(2,1)} async-done(((bf16[8,256,512]{1,2,0:T(8,128)(2,1)}), bf16[8,256,512]{1,2,0:T(8,128)(2,1)}, u32[]{:S(2)}, u32[]{:S(2)}) %all-to-all-start.7) | async-done | bytes 2097184 | tf_op jit(solution)/shard_map/all_to_all | solution.py:265
  415.2 4.7 all-to-all-start.1
  424.6 8.2 %fusion.4 = (f32[16,8,1,8,512]{4,3,2,1,0:T(8,128)S(1)}, f32[16,8,1,8,512]{4,3,2,1,0:T(8,128)S(1)}) fusion(s32[16,512]{1,0:T(8,128)S(1)} %fusion.5, s32[8,8]{1,0:T(8,128)S(1)} %mul.86), kind=kLoop, calls=%fused_computation.20 | loop fusion | flops 7864320 | bytes 4227328 | tf_op jit(solution)/shard_map/cos | solution.py:31
  530.8 4.8 power.1
  537.1 12.8 %collective-permute-done.7.refs_7_ = bf16[16,64,512]{2,1,0:T(8,128)(2,1)S(1)} collective-permute-done((bf16[16,64,512]{2,1,0:T(8,128)(2,1)}, bf16[16,64,512]{2,1,0:T(8,128)(2,1)S(1)}, u32[]{:S(2)}, u32[]{:S(2)}) %collective-permute-start.7) | collective-permute-done | bytes 1048608 | tf_op jit(solution)/shard_map/ppermute | solution.py:271
  549.9 22.5 %collective-permute-done.8.refs_9_ = bf16[16,64,512]{2,1,0:T(8,128)(2,1)S(1)} collective-permute-done((bf16[16,64,512]{2,1,0:T(8,128)(2,1)}, bf16[16,64,512]{2,1,0:T(8,128)(2,1)S(1)}, u32[]{:S(2)}, u32[]{:S(2)}) %collective-permute-start.8) | collective-permute-done | bytes 1048608 | tf_op jit(solution)/shard_map/ppermute | solution.py:271
  572.4 22.6 %collective-permute-done.9.refs_11_ = bf16[16,64,512]{2,1,0:T(8,128)(2,1)} collective-permute-done((bf16[16,64,512]{2,1,0:T(8,128)(2,1)}, bf16[16,64,512]{2,1,0:T(8,128)(2,1)}, u32[]{:S(2)}, u32[]{:S(2)}) %collective-permute-start.9) | collective-permute-done | bytes 1048608 | tf_op jit(solution)/shard_map/ppermute | solution.py:271
  594.9 22.5 %collective-permute-done.10.refs_13_ = bf16[16,64,512]{2,1,0:T(8,128)(2,1)} collective-permute-done((bf16[16,64,512]{2,1,0:T(8,128)(2,1)}, bf16[16,64,512]{2,1,0:T(8,128)(2,1)}, u32[]{:S(2)}, u32[]{:S(2)}) %collective-permute-start.10) | collective-permute-done | bytes 1048608 | tf_op jit(solution)/shard_map/ppermute | solution.py:271
  617.4 20.2 %collective-permute-done.11.refs_15_ = bf16[16,64,512]{2,1,0:T(8,128)(2,1)} collective-permute-done((bf16[16,64,512]{2,1,0:T(8,128)(2,1)}, bf16[16,64,512]{2,1,0:T(8,128)(2,1)}, u32[]{:S(2)}, u32[]{:S(2)}) %collective-permute-start.11) | collective-permute-done | bytes 1048608 | tf_op jit(solution)/shard_map/ppermute | solution.py:271
  641.5 6.9 %modes.1 = f32[2,32,8,1024]{3,2,1,0:T(8,128)} custom-call(s32[1]{0:T(128)} %bitcast.member_ref, bf16[4,16,256]{2,1,0:T(8,128)(2,1)S(1)} %copy-done.17, f32[4,8,128]{2,1,0:T(8,128)S(1)} %copy-done.18, bf16[16,64,512]{2,1,0:T(8,128)(2,1)S(1)} %get-tuple-element.39.refs_0_, bf16[16,64,512]{2,1,0:T(8,128)(2,1)} %collective-permute-done.4.refs_1_, ...), custom_call_target="tpu_custom_call" | custom-call | tf_op jit(solution)/shard_map/modes/pallas_call | solution.py:214
  (116 shorter events, 133.6 us)
Async XLA Ops:
  39.1 55.5 %all-to-all-start = ((bf16[8,256,512]{1,2,0:T(8,128)(2,1)}), bf16[8,256,512]{1,2,0:T(8,128)(2,1)}, u32[]{:S(2)}, u32[]{:S(2)}) async-start(bf16[8,256,512]{1,2,0:T(8,128)(2,1)} %bitcast.81), calls=%async_computation | async-start | bytes 4194304 | tf_op jit(solution)/shard_map/all_to_all | solution.py:265
  94.6 53.4 %all-to-all-start.2 = ((bf16[8,256,512]{1,2,0:T(8,128)(2,1)}), bf16[8,256,512]{1,2,0:T(8,128)(2,1)}, u32[]{:S(2)}, u32[]{:S(2)}) async-start(bf16[8,256,512]{1,2,0:T(8,128)(2,1)} %bitcast.76), calls=%async_computation.2 | async-start | bytes 4194304 | tf_op jit(solution)/shard_map/all_to_all | solution.py:265
  148.1 53.4 %all-to-all-start.3 = ((bf16[8,256,512]{1,2,0:T(8,128)(2,1)}), bf16[8,256,512]{1,2,0:T(8,128)(2,1)}, u32[]{:S(2)}, u32[]{:S(2)}) async-start(bf16[8,256,512]{1,2,0:T(8,128)(2,1)} %bitcast.77), calls=%async_computation.3 | async-start | bytes 4194304 | tf_op jit(solution)/shard_map/all_to_all | solution.py:265
  201.5 53.4 %all-to-all-start.4 = ((bf16[8,256,512]{1,2,0:T(8,128)(2,1)}), bf16[8,256,512]{1,2,0:T(8,128)(2,1)}, u32[]{:S(2)}, u32[]{:S(2)}) async-start(bf16[8,256,512]{1,2,0:T(8,128)(2,1)} %bitcast.78), calls=%async_computation.4 | async-start | bytes 4194304 | tf_op jit(solution)/shard_map/all_to_all | solution.py:265
  254.9 53.4 %all-to-all-start.5 = ((bf16[8,256,512]{1,2,0:T(8,128)(2,1)}), bf16[8,256,512]{1,2,0:T(8,128)(2,1)}, u32[]{:S(2)}, u32[]{:S(2)}) async-start(bf16[8,256,512]{1,2,0:T(8,128)(2,1)} %bitcast.79), calls=%async_computation.5 | async-start | bytes 4194304 | tf_op jit(solution)/shard_map/all_to_all | solution.py:265
  308.4 53.4 %all-to-all-start.6 = ((bf16[8,256,512]{1,2,0:T(8,128)(2,1)}), bf16[8,256,512]{1,2,0:T(8,128)(2,1)}, u32[]{:S(2)}, u32[]{:S(2)}) async-start(bf16[8,256,512]{1,2,0:T(8,128)(2,1)} %bitcast.80), calls=%async_computation.6 | async-start | bytes 4194304 | tf_op jit(solution)/shard_map/all_to_all | solution.py:265
  361.8 53.4 %all-to-all-start.7 = ((bf16[8,256,512]{1,2,0:T(8,128)(2,1)}), bf16[8,256,512]{1,2,0:T(8,128)(2,1)}, u32[]{:S(2)}, u32[]{:S(2)}) async-start(bf16[8,256,512]{1,2,0:T(8,128)(2,1)} %bitcast.75), calls=%async_computation.7 | async-start | bytes 4194304 | tf_op jit(solution)/shard_map/all_to_all | solution.py:265
  415.2 4.7 copy-start.21
  415.2 6.3 copy-start.22
  415.2 81.1 %all-to-all-start.1 = ((bf16[8,256,512]{1,2,0:T(8,128)(2,1)}), bf16[8,256,512]{1,2,0:T(8,128)(2,1)}, u32[]{:S(2)}, u32[]{:S(2)}) async-start(bf16[8,256,512]{1,2,0:T(8,128)(2,1)} %bitcast.74), calls=%async_computation.1 | async-start | bytes 4194304 | tf_op jit(solution)/shard_map/all_to_all | solution.py:265
  442.6 84.2 %collective-permute-start.4 = (bf16[16,64,512]{2,1,0:T(8,128)(2,1)}, bf16[16,64,512]{2,1,0:T(8,128)(2,1)}, u32[]{:S(2)}, u32[]{:S(2)}) collective-permute-start(bf16[16,64,512]{2,1,0:T(8,128)(2,1)} %get-tuple-element.40), channel_id=1, source_target_pairs={{0,2},{2,0},{1,3},{3,1},{4,6},{6,4},{5,7},{7,5},{8,10},{10,8},{9,1... | collective-permute-start | bytes 3145736 | tf_op jit(solution)/shard_map/ppermute | solution.py:271
  454.1 74.0 %collective-permute-start.5 = (bf16[16,64,512]{2,1,0:T(8,128)(2,1)}, bf16[16,64,512]{2,1,0:T(8,128)(2,1)}, u32[]{:S(2)}, u32[]{:S(2)}) collective-permute-start(bf16[16,64,512]{2,1,0:T(8,128)(2,1)} %get-tuple-element.42), channel_id=1, source_target_pairs={{0,2},{2,0},{1,3},{3,1},{4,6},{6,4},{5,7},{7,5},{8,10},{10,8},{9,1... | collective-permute-start | bytes 3145736 | tf_op jit(solution)/shard_map/ppermute | solution.py:271
  464.8 64.1 %collective-permute-start.6 = (bf16[16,64,512]{2,1,0:T(8,128)(2,1)}, bf16[16,64,512]{2,1,0:T(8,128)(2,1)}, u32[]{:S(2)}, u32[]{:S(2)}) collective-permute-start(bf16[16,64,512]{2,1,0:T(8,128)(2,1)} %get-tuple-element.44), channel_id=1, source_target_pairs={{0,2},{2,0},{1,3},{3,1},{4,6},{6,4},{5,7},{7,5},{8,10},{10,8},{9,1... | collective-permute-start | bytes 3145736 | tf_op jit(solution)/shard_map/ppermute | solution.py:271
  510.9 4.3 collective-permute-start
  515.2 1.3 collective-permute-start.1
  516.5 4.3 collective-permute-start.2
  520.9 5.2 collective-permute-start.3
  523.6 26.3 %collective-permute-start.7 = (bf16[16,64,512]{2,1,0:T(8,128)(2,1)}, bf16[16,64,512]{2,1,0:T(8,128)(2,1)S(1)}, u32[]{:S(2)}, u32[]{:S(2)}) collective-permute-start(bf16[16,64,512]{2,1,0:T(8,128)(2,1)} %get-tuple-element.46), channel_id=1, source_target_pairs={{0,2},{2,0},{1,3},{3,1},{4,6},{6,4},{5,7},{7,5},{8,10},{10,8},{9,1... | collective-permute-start | bytes 3145736 | tf_op jit(solution)/shard_map/ppermute | solution.py:271
  526.1 46.2 %collective-permute-start.8 = (bf16[16,64,512]{2,1,0:T(8,128)(2,1)}, bf16[16,64,512]{2,1,0:T(8,128)(2,1)S(1)}, u32[]{:S(2)}, u32[]{:S(2)}) collective-permute-start(bf16[16,64,512]{2,1,0:T(8,128)(2,1)} %get-tuple-element.48), channel_id=1, source_target_pairs={{0,2},{2,0},{1,3},{3,1},{4,6},{6,4},{5,7},{7,5},{8,10},{10,8},{9,1... | collective-permute-start | bytes 3145736 | tf_op jit(solution)/shard_map/ppermute | solution.py:271
  526.8 68.1 %collective-permute-start.9 = (bf16[16,64,512]{2,1,0:T(8,128)(2,1)}, bf16[16,64,512]{2,1,0:T(8,128)(2,1)}, u32[]{:S(2)}, u32[]{:S(2)}) collective-permute-start(bf16[16,64,512]{2,1,0:T(8,128)(2,1)} %get-tuple-element.50), channel_id=1, source_target_pairs={{0,2},{2,0},{1,3},{3,1},{4,6},{6,4},{5,7},{7,5},{8,10},{10,8},{9,1... | collective-permute-start | bytes 3145736 | tf_op jit(solution)/shard_map/ppermute | solution.py:271
  528.2 89.2 %collective-permute-start.10 = (bf16[16,64,512]{2,1,0:T(8,128)(2,1)}, bf16[16,64,512]{2,1,0:T(8,128)(2,1)}, u32[]{:S(2)}, u32[]{:S(2)}) collective-permute-start(bf16[16,64,512]{2,1,0:T(8,128)(2,1)} %get-tuple-element.52), channel_id=1, source_target_pairs={{0,2},{2,0},{1,3},{3,1},{4,6},{6,4},{5,7},{7,5},{8,10},{10,8},{9,1... | collective-permute-start | bytes 3145736 | tf_op jit(solution)/shard_map/ppermute | solution.py:271
  528.8 108.7 %collective-permute-start.11 = (bf16[16,64,512]{2,1,0:T(8,128)(2,1)}, bf16[16,64,512]{2,1,0:T(8,128)(2,1)}, u32[]{:S(2)}, u32[]{:S(2)}) collective-permute-start(bf16[16,64,512]{2,1,0:T(8,128)(2,1)} %get-tuple-element.54), channel_id=1, source_target_pairs={{0,2},{2,0},{1,3},{3,1},{4,6},{6,4},{5,7},{7,5},{8,10},{10,8},{9,1... | collective-permute-start | bytes 3145736 | tf_op jit(solution)/shard_map/ppermute | solution.py:271
  549.9 87.7 %copy-start.19 = (bf16[16,64,512]{2,1,0:T(8,128)(2,1)}, bf16[16,64,512]{2,1,0:T(8,128)(2,1)S(1)}, u32[]{:S(2)}) copy-start(bf16[16,64,512]{2,1,0:T(8,128)(2,1)S(1)} %collective-permute-done.7.refs_7_) | copy-start | bytes 3145732
  572.4 65.2 %copy-start.20 = (bf16[16,64,512]{2,1,0:T(8,128)(2,1)}, bf16[16,64,512]{2,1,0:T(8,128)(2,1)S(1)}, u32[]{:S(2)}) copy-start(bf16[16,64,512]{2,1,0:T(8,128)(2,1)S(1)} %collective-permute-done.8.refs_9_) | copy-start | bytes 3145732
  (19 other events, 34.2 us)

commit v2 on v1

--- a/solution.py
+++ b/solution.py
@@ -13,6 +13,7 @@
 SPAN = 2 * NFFT
 LANES = 128
 SUBLANES = 8
+AHEAD = 2
 GROUP_ROWS = 2 * SUBLANES
 MIB = 1 << 20
 
@@ -32,9 +33,59 @@
     return table.astype(jnp.bfloat16).reshape(offsets.shape[0] // 2, -1, SPAN)
 
 
-def spectra_kernel(window_start, history, basis, total_in, *outs, members):
-    coefs = outs[:members]
-    total_out = outs[members]
+def prepare_kernel(line_ref, *refs, count):
+    del line_ref
+    for piece in range(count):
+        source, target = refs[piece], refs[count + piece]
+        points = source.shape[2]
+        for plane in range(source.shape[1]):
+            target[:, plane * points : (plane + 1) * points] = source[:, plane, :]
+
+
+def prepare(line_index, series, offset, points, count):
+    snap_rows, slab_rows, plane = series.shape
+    first, stride = offset // points, plane // count // points
+
+    def source_map(piece):
+        return lambda step, line_ref: (0, 0, (line_ref[0] ^ piece) * stride + first)
+
+    return pl.pallas_call(
+        functools.partial(prepare_kernel, count=count),
+        grid_spec=pltpu.PrefetchScalarGridSpec(
+            num_scalar_prefetch=1,
+            grid=(1,),
+            in_specs=[
+                pl.BlockSpec((snap_rows, slab_rows, points), source_map(piece))
+                for piece in range(count)
+            ],
+            out_specs=[
+                pl.BlockSpec((snap_rows, slab_rows * points), lambda step, line_ref: (0, 0))
+                for piece in range(count)
+            ],
+        ),
+        out_shape=[jax.ShapeDtypeStruct((snap_rows, slab_rows * points), series.dtype)] * count,
+        compiler_params=pltpu.CompilerParams(vmem_limit_bytes=40 * MIB),
+        cost_estimate=pl.CostEstimate(
+            flops=0, bytes_accessed=4 * count * snap_rows * slab_rows * points, transcendentals=0
+        ),
+        name="prepare",
+    )(line_index, *([series] * count))
+
+
+def spectra_kernel(line_ref, window_start, basis, total_in, *refs, count, members):
+    pieces = refs[:count]
+    coefs = refs[count : count + members]
+    total_out, history, sems = refs[count + members :]
+    copies = []
+    for piece in range(count):
+        length = pieces[piece].shape[0]
+        first = pl.multiple_of((line_ref[0] ^ piece) * length if count > 1 else 0, 16)
+        copies.append(
+            pltpu.make_async_copy(pieces[piece], history.at[pl.ds(first, length)], sems.at[piece])
+        )
+        copies[-1].start()
+    for copy in copies:
+        copy.wait()
     rows = coefs[0].shape[1]
     pairs = basis.shape[0]
     width = history.shape[1]
@@ -74,25 +125,32 @@
         total_out[member] = total_in[member] + (packed[0] + swapped)
 
 
-def spectra(window_start, history, basis, total, members):
-    width = history.shape[1]
+def spectra(line_index, window_start, pieces, basis, total, members):
+    count = len(pieces)
+    length, width = pieces[0].shape
     blocks = 2 * basis.shape[0]
     rows = basis.shape[1] // 2 // members
+    smem = pl.BlockSpec(memory_space=pltpu.SMEM)
     vmem = pl.BlockSpec(memory_space=pltpu.VMEM)
     outs = [jax.ShapeDtypeStruct((blocks, rows, width), jnp.bfloat16)] * members
     return pl.pallas_call(
-        functools.partial(spectra_kernel, members=members),
+        functools.partial(spectra_kernel, count=count, members=members),
         out_shape=outs + [jax.ShapeDtypeStruct(total.shape, jnp.float32)],
-        in_specs=[pl.BlockSpec(memory_space=pltpu.SMEM), vmem, vmem, vmem],
+        in_specs=[smem, smem, vmem, vmem] + [pl.BlockSpec(memory_space=pl.ANY)] * count,
         out_specs=[vmem] * (members + 1),
+        scratch_shapes=[
+            pltpu.VMEM((count * length, width), pieces[0].dtype),
+            pltpu.SemaphoreType.DMA((count,)),
+        ],
         compiler_params=pltpu.CompilerParams(vmem_limit_bytes=40 * MIB),
         cost_estimate=pl.CostEstimate(
             flops=2 * blocks * members * rows * width * (SPAN + 256),
-            bytes_accessed=2 * (history.size + basis.size + blocks * members * rows * width),
+            bytes_accessed=2
+            * (count * length * width + basis.size + blocks * members * rows * width),
             transcendentals=0,
         ),
         name="spectra",
-    )(window_start, history, basis, total)
+    )(line_index, window_start, basis, total, *pieces)
 
 
 def power_kernel(total, mix, scale, spectrum, *, blocks, norm_scale):
@@ -171,29 +229,32 @@
 
 def modes_kernel(member_ref, mix, scale, *refs, chunks, members):
     coefs = refs[: chunks * members]
-    out, buffer, sems = refs[chunks * members :]
+    out = refs[chunks * members]
+    buffers = refs[chunks * members + 1 : -1]
+    sems = refs[-1]
     member = member_ref[0]
     copies = []
     for chunk in range(chunks):
         for turn in range(members):
             slot = lax.rem(member + members - turn, members)
             copy = pltpu.make_async_copy(
-                coefs[chunk * members + turn], buffer.at[chunk, slot], sems.at[chunk, turn]
+                coefs[chunk * members + turn], buffers[chunk].at[slot], sems.at[chunk, turn]
             )
             copy.start()
             copies.append(copy)
-    width = coefs[0].shape[2]
-    padded = coefs[0].shape[0]
     planes = out.shape[2] // members
-    points = width // planes
+    done = 0
     for chunk in range(chunks):
         for turn in range(members):
             copies[chunk * members + turn].wait()
+        padded, width = buffers[chunk].shape[1], buffers[chunk].shape[3]
+        points = width // planes
         for slot in range(members):
             for group in range(mix.shape[0]):
-                tile = buffer[chunk, slot, :, group * GROUP_ROWS : (group + 1) * GROUP_ROWS, :]
+                tile = buffers[chunk][slot, :, group * GROUP_ROWS : (group + 1) * GROUP_ROWS, :]
                 tile = tile.reshape(padded * GROUP_ROWS, width)
                 raw = jnp.dot(mix[group], tile, preferred_element_type=jnp.float32)
+                factor = jnp.tile(scale[group], (1, points // LANES))
                 for e in range(2):
                     for plane in range(planes):
                         part = raw[
@@ -203,13 +264,15 @@
                             e,
                             group * SUBLANES : (group + 1) * SUBLANES,
                             slot * planes + plane,
-                            chunk * points : (chunk + 1) * points,
-                        ] = part * jnp.tile(scale[group], (1, points // LANES))
-
-
-def project(member, mix, scale, coefs, members, planes, points):
+                            done : done + points,
+                        ] = part * factor
+        done += points
+
+
+def project(member, mix, scale, coefs, members, planes):
     chunks = len(coefs) // members
     groups = mix.shape[0]
+    points = sum(part.shape[2] for part in coefs[::members]) // planes
     vmem = pl.BlockSpec(memory_space=pltpu.VMEM)
     return pl.pallas_call(
         functools.partial(modes_kernel, chunks=chunks, members=members),
@@ -220,12 +283,19 @@
         + [pl.BlockSpec(memory_space=pl.ANY)] * len(coefs),
         out_specs=vmem,
         scratch_shapes=[
-            pltpu.VMEM((chunks, members) + coefs[0].shape, jnp.bfloat16),
-            pltpu.SemaphoreType.DMA((chunks, members)),
-        ],
+            pltpu.VMEM((members,) + part.shape, jnp.bfloat16) for part in coefs[::members]
+        ]
+        + [pltpu.SemaphoreType.DMA((chunks, members))],
         compiler_params=pltpu.CompilerParams(vmem_limit_bytes=48 * MIB),
         name="modes",
     )(member, mix, scale, *coefs)
+
+
+def chunk_sizes(width):
+    if width < 8 * LANES:
+        return [LANES] * (width // LANES)
+    sizes = [LANES, LANES] + [2 * LANES] * ((width - 4 * LANES) // (2 * LANES)) + [LANES, LANES]
+    return sizes
 
 
 def butterfly_sum(value, axes, count):
@@ -244,11 +314,10 @@
     members = lax.axis_size("freq")
     member = lax.axis_index("freq")
     width = plane // group_count
-    chunk_points = LANES
-    chunks = width // chunk_points
     blocks = block_start.shape[0]
     pairs = (blocks + 1) // 2
     frames = snap_rows * group_count
+    line_index = lax.axis_index(line).reshape(1)
 
     order = (member + jnp.arange(members, dtype=jnp.int32)) % members
     freq_order = freq_index.reshape(members, -1)[order].reshape(-1)
@@ -256,19 +325,29 @@
     window_start = jnp.minimum(starts[::2] // 16 * 16, frames - SPAN)
     basis = shifted_basis(freq_order, starts - jnp.repeat(window_start, 2), blocks)
 
-    tiles = series.reshape(snap_rows, slab_rows, group_count, chunks, chunk_points)
     total = jnp.zeros((members, 2 * pairs * SUBLANES, LANES), jnp.float32)
-    coefs = []
-    for chunk in range(chunks):
-        piece = jnp.transpose(tiles[:, :, :, chunk, :], (2, 0, 1, 3))
-        piece = piece.reshape(group_count, snap_rows, slab_rows * chunk_points)
-        history = lax.all_to_all(piece, line, split_axis=0, concat_axis=0, tiled=True)
-        history = history.reshape(frames, slab_rows * chunk_points)
-        *sent, total = spectra(window_start, history, basis, total, members)
+    sizes = chunk_sizes(width)
+    offsets = [sum(sizes[:chunk]) for chunk in range(len(sizes))]
+    coefs, pieces, ticket = [], [], line_index
+
+    def exchange(chunk):
+        parts = list(prepare(ticket, series, offsets[chunk], sizes[chunk], group_count))
+        for piece in range(1, group_count):
+            pairs_of_piece = [(i, i ^ piece) for i in range(group_count)]
+            parts[piece] = lax.ppermute(parts[piece], line, pairs_of_piece)
+        pieces.append(parts)
+
+    for chunk in range(min(AHEAD, len(sizes))):
+        exchange(chunk)
+    for chunk in range(len(sizes)):
+        *sent, total = spectra(line_index, window_start, pieces[chunk], basis, total, members)
         coefs.append(sent[0])
         for turn in range(1, members):
             ring = [(i, (i + turn) % members) for i in range(members)]
             coefs.append(lax.ppermute(sent[turn], "freq", ring))
+        if chunk + AHEAD < len(sizes):
+            ticket, total = lax.optimization_barrier((ticket, total))
+            exchange(chunk + AHEAD)
 
     mine = total[0]
     for turn in range(1, members):
@@ -279,7 +358,7 @@
     groups = freq_index.shape[0] // members // SUBLANES
     norm_scale = 1.0 / (blocks * slab_rows * members * plane)
     mix, scale, spectrum = leading_vectors(mine, groups, blocks, norm_scale)
-    modes = project(member.reshape(1), mix, scale, coefs, members, slab_rows, width)
+    modes = project(member.reshape(1), mix, scale, coefs, members, slab_rows)
     return (modes, spectrum[:, :, 0].reshape(-1))
 
 

time: 651 us -> 619 us (0.951)
  local copies, waits for them, and re-layouts: 111 us -> 8.95 us
  starting transfers between devices: 50.4 us -> 111 us
  waiting for transfers between devices: 433 us -> 389 us
  Pallas kernels: 40.4 us -> 83.7 us
    all_to_all x8 -> x0, waiting for transfers between devices: 323 us -> none  [shards(): lax.all_to_all(piece, line, split_axis=0, concat_axis=0, tiled=True)]
    ppermute x0 -> x42, waiting for transfers between devices: none -> 222 us  [exchange(): parts[piece] = lax.ppermute(parts[piece], line, pairs_of_piece)]
    ppermute x0 -> x42, starting transfers between devices: none -> 102 us  [exchange(): parts[piece] = lax.ppermute(parts[piece], line, pairs_of_piece)]
    ppermute x1, waiting for transfers between devices: 3.73 us -> 103 us  [shards(): mine = mine + lax.ppermute(total[turn], 'freq', ring)]
    ppermute x8 -> x6, waiting for transfers between devices: 100 us -> 56.6 us  [shards(): coefs.append(lax.ppermute(sent[turn], 'freq', ring))]
    pallas_call x8 -> x12, Pallas kernels: 28.7 us -> 72.1 us  [the longest x6 44.6 us: prepare(): pl.pallas_call(functools.partial(prepare_kernel, count=count), grid_spec=...]
    unnamed x47 -> x36, local copies, waits for them, and re-layouts: 43.9 us -> 6 us
    all_to_all x8 -> x0, starting transfers between devices: 37.1 us -> none  [shards(): lax.all_to_all(piece, line, split_axis=0, concat_axis=0, tiled=True)]
  transfers between devices with their start and end apart: 20 -> 52, of which waited for: 16 -> 24; matrix products, arithmetic and copies ran while one was open for 10% -> 3% of each run, Pallas kernels for 5% -> 7%
where the time goes in v2:
time: 619 us; the launch traced here: 611 us
  waiting for transfers between devices  389 us (63%)
  starting transfers between devices  111 us (18%)
  Pallas kernels  83.7 us (14%)
  other arithmetic  16 us (3%)
  local copies, waits for them, and re-layouts  8.95 us (1%)
    ppermute x42, waiting for transfers between devices, exchange(): parts[piece] = lax.ppermute(parts[piece], line, pairs_of_piece)  222 us
    ppermute x1, waiting for transfers between devices, shards(): mine = mine + lax.ppermute(total[turn], 'freq', ring)  103 us
    ppermute x42, starting transfers between devices, exchange(): parts[piece] = lax.ppermute(parts[piece], line, pairs_of_piece)  102 us
    ppermute x6, waiting for transfers between devices, shards(): coefs.append(lax.ppermute(sent[turn], 'freq', ring))  56.6 us
    pallas_call x6, Pallas kernels, prepare(): pl.pallas_call(functools.partial(prepare_kernel, count=count), grid_spec=...  44.6 us
    pallas_call x6, Pallas kernels, spectra(): pl.pallas_call(functools.partial(spectra_kernel, count=count, members=mem...  27.4 us
  transfers between devices with their start and end apart: 52, of which 24 were waited for; matrix products, arithmetic and copies ran while one was open for 3% of the time, Pallas kernels for 7%

profile of v2, /device:TPU:0, one launch (start us, length us, event | category | flops | bytes accessed | tf_op | source)
XLA Modules:
  0.0 610.8 jit_solution(14226917617579927609)
XLA Ops:
  33.6 10.1 %fusion.4 = (f32[16,8,1,8,512]{4,3,2,1,0:T(8,128)}, f32[16,8,1,8,512]{4,3,2,1,0:T(8,128)}) fusion(s32[16,512]{1,0:T(8,128)S(1)} %fusion.5, s32[8,8]{1,0:T(8,128)S(1)} %mul.90), kind=kLoop, calls=%fused_computation.12 | loop fusion | flops 7864320 | bytes 4227328 | tf_op jit(solution)/shard_map/cos | solution.py:32
  49.5 10.0 %collective-permute-done.4.refs_5_ = bf16[256,512]{1,0:T(8,128)(2,1)} collective-permute-done((bf16[256,512]{1,0:T(8,128)(2,1)}, bf16[256,512]{1,0:T(8,128)(2,1)}, u32[]{:S(2)}, u32[]{:S(2)}) %collective-permute-start.4) | collective-permute-done | bytes 262176 | tf_op jit(solution)/shard_map/ppermute | solution.py:337
  59.5 13.7 %collective-permute-start.12 = (bf16[256,512]{1,0:T(8,128)(2,1)S(1)}, bf16[256,512]{1,0:T(8,128)(2,1)S(1)}, u32[]{:S(2)}, u32[]{:S(2)}) collective-permute-start(bf16[256,512]{1,0:T(8,128)(2,1)S(1)} %get-tuple-element.96), channel_id=1, source_target_pairs={{0,12},{1,13},{4,8},{5,9},{8,4},{9,5},{12,0},{13,1},{2,14},{3,15},... | collective-permute-start | bytes 786440 | tf_op jit(solution)/shard_map/ppermute | solution.py:337
  82.7 16.9 %collective-permute-done.10.refs_4_ = bf16[256,512]{1,0:T(8,128)(2,1)S(1)} collective-permute-done((bf16[256,512]{1,0:T(8,128)(2,1)S(1)}, bf16[256,512]{1,0:T(8,128)(2,1)S(1)}, u32[]{:S(2)}, u32[]{:S(2)}) %collective-permute-start.10) | collective-permute-done | bytes 262176 | tf_op jit(solution)/shard_map/ppermute | solution.py:337
  107.3 8.8 %prepare.9 = (bf16[256,1024]{1,0:T(8,128)(2,1)S(1)}, bf16[256,1024]{1,0:T(8,128)(2,1)S(1)}, bf16[256,1024]{1,0:T(8,128)(2,1)S(1)}, bf16[256,1024]{1,0:T(8,128)(2...) custom-call(s32[1]{0:T(128)} %bitcast.1.line_ref, ...), custom_call_target="tpu_custom_call" | custom-call | bytes 8388608 | tf_op jit(solution)/shard_map/prepare/pallas_call | solution.py:52
  116.9 11.3 %collective-permute-start.22 = (bf16[256,1024]{1,0:T(8,128)(2,1)S(1)}, bf16[256,1024]{1,0:T(8,128)(2,1)S(1)}, u32[]{:S(2)}, u32[]{:S(2)}) collective-permute-start(bf16[256,1024]{1,0:T(8,128)(2,1)S(1)} %get-tuple-element.114), channel_id=1, source_target_pairs={{0,4},{1,5},{4,0},{5,1},{8,12},{9,13},{12,8},{13,9},{2,6},{3,7},{6... | collective-permute-start | bytes 1572872 | tf_op jit(solution)/shard_map/ppermute | solution.py:337
  128.2 8.9 %prepare.8 = (bf16[256,1024]{1,0:T(8,128)(2,1)S(1)}, bf16[256,1024]{1,0:T(8,128)(2,1)S(1)}, bf16[256,1024]{1,0:T(8,128)(2,1)S(1)}, bf16[256,1024]{1,0:T(8,128)(2...) custom-call(s32[1]{0:T(128)} %bitcast.1.line_ref, ...), custom_call_target="tpu_custom_call" | custom-call | bytes 8388608 | tf_op jit(solution)/shard_map/prepare/pallas_call | solution.py:52
  144.2 29.9 %collective-permute-done.15.refs_2_ = bf16[256,1024]{1,0:T(8,128)(2,1)S(1)} collective-permute-done((bf16[256,1024]{1,0:T(8,128)(2,1)S(1)}, bf16[256,1024]{1,0:T(8,128)(2,1)S(1)}, u32[]{:S(2)}, u32[]{:S(2)}) %collective-permute-start.15) | collective-permute-done | bytes 524320 | tf_op jit(solution)/shard_map/ppermute | solution.py:337
  174.7 10.1 %collective-permute-done.16.refs_3_ = bf16[256,1024]{1,0:T(8,128)(2,1)S(1)} collective-permute-done((bf16[256,1024]{1,0:T(8,128)(2,1)S(1)}, bf16[256,1024]{1,0:T(8,128)(2,1)S(1)}, u32[]{:S(2)}, u32[]{:S(2)}) %collective-permute-start.16) | collective-permute-done | bytes 524320 | tf_op jit(solution)/shard_map/ppermute | solution.py:337
  188.3 11.6 %collective-permute-done.19.refs_6_ = bf16[256,1024]{1,0:T(8,128)(2,1)S(1)} collective-permute-done((bf16[256,1024]{1,0:T(8,128)(2,1)S(1)}, bf16[256,1024]{1,0:T(8,128)(2,1)S(1)}, u32[]{:S(2)}, u32[]{:S(2)}) %collective-permute-start.19) | collective-permute-done | bytes 524320 | tf_op jit(solution)/shard_map/ppermute | solution.py:337
  199.9 12.6 %collective-permute-start.26 = (bf16[256,1024]{1,0:T(8,128)(2,1)S(1)}, bf16[256,1024]{1,0:T(8,128)(2,1)S(1)}, u32[]{:S(2)}, u32[]{:S(2)}) collective-permute-start(bf16[256,1024]{1,0:T(8,128)(2,1)S(1)} %get-tuple-element.118), channel_id=1, source_target_pairs={{0,12},{1,13},{4,8},{5,9},{8,4},{9,5},{12,0},{13,1},{2,14},{3,15},... | collective-permute-start | bytes 1572872 | tf_op jit(solution)/shard_map/ppermute | solution.py:337
  221.3 68.3 %collective-permute-done.24.refs_4_ = bf16[256,1024]{1,0:T(8,128)(2,1)S(1)} collective-permute-done((bf16[256,1024]{1,0:T(8,128)(2,1)S(1)}, bf16[256,1024]{1,0:T(8,128)(2,1)S(1)}, u32[]{:S(2)}, u32[]{:S(2)}) %collective-permute-start.24) | collective-permute-done | bytes 524320 | tf_op jit(solution)/shard_map/ppermute | solution.py:337
  289.6 10.1 %collective-permute-done.25.refs_5_ = bf16[256,1024]{1,0:T(8,128)(2,1)S(1)} collective-permute-done((bf16[256,1024]{1,0:T(8,128)(2,1)S(1)}, bf16[256,1024]{1,0:T(8,128)(2,1)S(1)}, u32[]{:S(2)}, u32[]{:S(2)}) %collective-permute-start.25) | collective-permute-done | bytes 524320 | tf_op jit(solution)/shard_map/ppermute | solution.py:337
  305.8 7.2 %prepare.11 = (bf16[256,512]{1,0:T(8,128)(2,1)S(1)}, bf16[256,512]{1,0:T(8,128)(2,1)S(1)}, bf16[256,512]{1,0:T(8,128)(2,1)S(1)}, bf16[256,512]{1,0:T(8,128)(2,1)...) custom-call(s32[1]{0:T(128)} %bitcast.1.line_ref, ...), custom_call_target="tpu_custom_call" | custom-call | bytes 4194304 | tf_op jit(solution)/shard_map/prepare/pallas_call | solution.py:52
  314.0 22.5 %collective-permute-start.36 = (bf16[256,512]{1,0:T(8,128)(2,1)S(1)}, bf16[256,512]{1,0:T(8,128)(2,1)S(1)}, u32[]{:S(2)}, u32[]{:S(2)}) collective-permute-start(bf16[256,512]{1,0:T(8,128)(2,1)S(1)} %get-tuple-element.134), channel_id=1, source_target_pairs={{0,4},{1,5},{4,0},{5,1},{8,12},{9,13},{12,8},{13,9},{2,6},{3,7},{6... | collective-permute-start | bytes 786440 | tf_op jit(solution)/shard_map/ppermute | solution.py:337
  339.4 6.7 %prepare.10 = (bf16[256,512]{1,0:T(8,128)(2,1)S(1)}, bf16[256,512]{1,0:T(8,128)(2,1)S(1)}, bf16[256,512]{1,0:T(8,128)(2,1)S(1)}, bf16[256,512]{1,0:T(8,128)(2,1)...) custom-call(s32[1]{0:T(128)} %bitcast.1.line_ref, ...), custom_call_target="tpu_custom_call" | custom-call | bytes 4194304 | tf_op jit(solution)/shard_map/prepare/pallas_call | solution.py:52
  346.4 7.7 %collective-permute-done.36.refs_2_ = bf16[256,512]{1,0:T(8,128)(2,1)S(1)} collective-permute-done((bf16[256,512]{1,0:T(8,128)(2,1)S(1)}, bf16[256,512]{1,0:T(8,128)(2,1)S(1)}, u32[]{:S(2)}, u32[]{:S(2)}) %collective-permute-start.36) | collective-permute-done | bytes 262176 | tf_op jit(solution)/shard_map/ppermute | solution.py:337
  365.5 11.0 %collective-permute-done.29.refs_2_ = bf16[256,512]{1,0:T(8,128)(2,1)S(1)} collective-permute-done((bf16[256,512]{1,0:T(8,128)(2,1)S(1)}, bf16[256,512]{1,0:T(8,128)(2,1)S(1)}, u32[]{:S(2)}, u32[]{:S(2)}) %collective-permute-start.29) | collective-permute-done | bytes 262176 | tf_op jit(solution)/shard_map/ppermute | solution.py:337
  384.9 23.3 %collective-permute-done.32.refs_5_ = bf16[256,512]{1,0:T(8,128)(2,1)S(1)} collective-permute-done((bf16[256,512]{1,0:T(8,128)(2,1)S(1)}, bf16[256,512]{1,0:T(8,128)(2,1)S(1)}, u32[]{:S(2)}, u32[]{:S(2)}) %collective-permute-start.32) | collective-permute-done | bytes 262176 | tf_op jit(solution)/shard_map/ppermute | solution.py:337
  421.9 102.6 %collective-permute-done.42 = f32[128,128]{1,0:T(8,128)S(1)} collective-permute-done((f32[128,128]{1,0:T(8,128)S(1)}, f32[128,128]{1,0:T(8,128)S(1)}, u32[]{:S(2)}, u32[]{:S(2)}) %collective-permute-start.42) | collective-permute-done | bytes 65568 | tf_op jit(solution)/shard_map/ppermute | solution.py:355
  544.1 13.3 %collective-permute-done.46.refs_1_ = bf16[16,64,512]{2,1,0:T(8,128)(2,1)} collective-permute-done((bf16[16,64,512]{2,1,0:T(8,128)(2,1)}, bf16[16,64,512]{2,1,0:T(8,128)(2,1)}, u32[]{:S(2)}, u32[]{:S(2)}) %collective-permute-start.46) | collective-permute-done | bytes 1048608 | tf_op jit(solution)/shard_map/ppermute | solution.py:347
  557.5 22.5 %collective-permute-done.51.refs_11_ = bf16[16,64,512]{2,1,0:T(8,128)(2,1)} collective-permute-done((bf16[16,64,512]{2,1,0:T(8,128)(2,1)}, bf16[16,64,512]{2,1,0:T(8,128)(2,1)}, u32[]{:S(2)}, u32[]{:S(2)}) %collective-permute-start.51) | collective-permute-done | bytes 1048608 | tf_op jit(solution)/shard_map/ppermute | solution.py:347
  580.0 20.8 %collective-permute-done.50.refs_9_ = bf16[16,64,512]{2,1,0:T(8,128)(2,1)} collective-permute-done((bf16[16,64,512]{2,1,0:T(8,128)(2,1)}, bf16[16,64,512]{2,1,0:T(8,128)(2,1)}, u32[]{:S(2)}, u32[]{:S(2)}) %collective-permute-start.50) | collective-permute-done | bytes 1048608 | tf_op jit(solution)/shard_map/ppermute | solution.py:347
  603.5 6.8 %modes.1 = f32[2,32,8,1024]{3,2,1,0:T(8,128)} custom-call(s32[1]{0:T(128)} %bitcast.member_ref, bf16[4,16,256]{2,1,0:T(8,128)(2,1)S(1)} %copy-done.5, f32[4,8,128]{2,1,0:T(8,128)S(1)} %copy-done.6, bf16[16,64,512]{2,1,0:T(8,128)(2,1)S(1)} %get-tuple-element.143.refs_0_, bf16[16,64,512]{2,1,0:T(8,128)(2,1)} %collective-permute-done.46.refs_1_, ...), custom_call_target="tpu_custom_call" | custom-call | tf_op jit(solution)/shard_map/modes/pallas_call | solution.py:277
  (156 shorter events, 141.8 us)
Async XLA Ops:
  33.6 39.6 %collective-permute-start.6 = (bf16[256,512]{1,0:T(8,128)(2,1)S(1)}, bf16[256,512]{1,0:T(8,128)(2,1)}, u32[]{:S(2)}, u32[]{:S(2)}) collective-permute-start(bf16[256,512]{1,0:T(8,128)(2,1)S(1)} %get-tuple-element.86), channel_id=1, source_target_pairs={{0,13},{1,12},{4,9},{5,8},{8,5},{9,4},{12,1},{13,0},{2,15},{3,14},... | collective-permute-start | bytes 786440 | tf_op jit(solution)/shard_map/ppermute | solution.py:337
  45.3 37.4 %collective-permute-start.9 = (bf16[256,512]{1,0:T(8,128)(2,1)S(1)}, bf16[256,512]{1,0:T(8,128)(2,1)S(1)}, u32[]{:S(2)}, u32[]{:S(2)}) collective-permute-start(bf16[256,512]{1,0:T(8,128)(2,1)S(1)} %get-tuple-element.93), channel_id=1, source_target_pairs={{0,5},{1,4},{4,1},{5,0},{8,13},{9,12},{12,9},{13,8},{2,7},{3,6},{6... | collective-permute-start | bytes 786440 | tf_op jit(solution)/shard_map/ppermute | solution.py:337
  45.4 54.2 %collective-permute-start.10 = (bf16[256,512]{1,0:T(8,128)(2,1)S(1)}, bf16[256,512]{1,0:T(8,128)(2,1)S(1)}, u32[]{:S(2)}, u32[]{:S(2)}) collective-permute-start(bf16[256,512]{1,0:T(8,128)(2,1)S(1)} %get-tuple-element.94), channel_id=1, source_target_pairs={{0,8},{1,9},{4,12},{5,13},{8,0},{9,1},{12,4},{13,5},{2,10},{3,11},... | collective-permute-start | bytes 786440 | tf_op jit(solution)/shard_map/ppermute | solution.py:337
  59.5 44.8 %collective-permute-start.11 = (bf16[256,512]{1,0:T(8,128)(2,1)S(1)}, bf16[256,512]{1,0:T(8,128)(2,1)S(1)}, u32[]{:S(2)}, u32[]{:S(2)}) collective-permute-start(bf16[256,512]{1,0:T(8,128)(2,1)S(1)} %get-tuple-element.95), channel_id=1, source_target_pairs={{0,9},{1,8},{4,13},{5,12},{8,1},{9,0},{12,5},{13,4},{2,11},{3,10},... | collective-permute-start | bytes 786440 | tf_op jit(solution)/shard_map/ppermute | solution.py:337
  59.5 44.8 %collective-permute-start.12 = (bf16[256,512]{1,0:T(8,128)(2,1)S(1)}, bf16[256,512]{1,0:T(8,128)(2,1)S(1)}, u32[]{:S(2)}, u32[]{:S(2)}) collective-permute-start(bf16[256,512]{1,0:T(8,128)(2,1)S(1)} %get-tuple-element.96), channel_id=1, source_target_pairs={{0,12},{1,13},{4,8},{5,9},{8,4},{9,5},{12,0},{13,1},{2,14},{3,15},... | collective-permute-start | bytes 786440 | tf_op jit(solution)/shard_map/ppermute | solution.py:337
  137.2 37.0 %collective-permute-start.15 = (bf16[256,1024]{1,0:T(8,128)(2,1)S(1)}, bf16[256,1024]{1,0:T(8,128)(2,1)S(1)}, u32[]{:S(2)}, u32[]{:S(2)}) collective-permute-start(bf16[256,1024]{1,0:T(8,128)(2,1)S(1)} %get-tuple-element.103), channel_id=1, source_target_pairs={{0,4},{1,5},{4,0},{5,1},{8,12},{9,13},{12,8},{13,9},{2,6},{3,7},{6... | collective-permute-start | bytes 1572872 | tf_op jit(solution)/shard_map/ppermute | solution.py:337
  137.4 47.4 %collective-permute-start.16 = (bf16[256,1024]{1,0:T(8,128)(2,1)S(1)}, bf16[256,1024]{1,0:T(8,128)(2,1)S(1)}, u32[]{:S(2)}, u32[]{:S(2)}) collective-permute-start(bf16[256,1024]{1,0:T(8,128)(2,1)S(1)} %get-tuple-element.104), channel_id=1, source_target_pairs={{0,5},{1,4},{4,1},{5,0},{8,13},{9,12},{12,9},{13,8},{2,7},{3,6},{6... | collective-permute-start | bytes 1572872 | tf_op jit(solution)/shard_map/ppermute | solution.py:337
  139.0 45.8 %collective-permute-start.17 = (bf16[256,1024]{1,0:T(8,128)(2,1)S(1)}, bf16[256,1024]{1,0:T(8,128)(2,1)S(1)}, u32[]{:S(2)}, u32[]{:S(2)}) collective-permute-start(bf16[256,1024]{1,0:T(8,128)(2,1)S(1)} %get-tuple-element.105), channel_id=1, source_target_pairs={{0,8},{1,9},{4,12},{5,13},{8,0},{9,1},{12,4},{13,5},{2,10},{3,11},... | collective-permute-start | bytes 1572872 | tf_op jit(solution)/shard_map/ppermute | solution.py:337
  140.7 46.2 %collective-permute-start.18 = (bf16[256,1024]{1,0:T(8,128)(2,1)S(1)}, bf16[256,1024]{1,0:T(8,128)(2,1)S(1)}, u32[]{:S(2)}, u32[]{:S(2)}) collective-permute-start(bf16[256,1024]{1,0:T(8,128)(2,1)S(1)} %get-tuple-element.106), channel_id=1, source_target_pairs={{0,9},{1,8},{4,13},{5,12},{8,1},{9,0},{12,5},{13,4},{2,11},{3,10},... | collective-permute-start | bytes 1572872 | tf_op jit(solution)/shard_map/ppermute | solution.py:337
  142.2 57.8 %collective-permute-start.19 = (bf16[256,1024]{1,0:T(8,128)(2,1)S(1)}, bf16[256,1024]{1,0:T(8,128)(2,1)S(1)}, u32[]{:S(2)}, u32[]{:S(2)}) collective-permute-start(bf16[256,1024]{1,0:T(8,128)(2,1)S(1)} %get-tuple-element.107), channel_id=1, source_target_pairs={{0,12},{1,13},{4,8},{5,9},{8,4},{9,5},{12,0},{13,1},{2,14},{3,15},... | collective-permute-start | bytes 1572872 | tf_op jit(solution)/shard_map/ppermute | solution.py:337
  174.2 38.3 %collective-permute-start.20 = (bf16[256,1024]{1,0:T(8,128)(2,1)S(1)}, bf16[256,1024]{1,0:T(8,128)(2,1)S(1)}, u32[]{:S(2)}, u32[]{:S(2)}) collective-permute-start(bf16[256,1024]{1,0:T(8,128)(2,1)S(1)} %get-tuple-element.108), channel_id=1, source_target_pairs={{0,13},{1,12},{4,9},{5,8},{8,5},{9,4},{12,1},{13,0},{2,15},{3,14},... | collective-permute-start | bytes 1572872 | tf_op jit(solution)/shard_map/ppermute | solution.py:337
  184.8 104.8 %collective-permute-start.24 = (bf16[256,1024]{1,0:T(8,128)(2,1)S(1)}, bf16[256,1024]{1,0:T(8,128)(2,1)S(1)}, u32[]{:S(2)}, u32[]{:S(2)}) collective-permute-start(bf16[256,1024]{1,0:T(8,128)(2,1)S(1)} %get-tuple-element.116), channel_id=1, source_target_pairs={{0,8},{1,9},{4,12},{5,13},{8,0},{9,1},{12,4},{13,5},{2,10},{3,11},... | collective-permute-start | bytes 1572872 | tf_op jit(solution)/shard_map/ppermute | solution.py:337
  186.9 112.8 %collective-permute-start.25 = (bf16[256,1024]{1,0:T(8,128)(2,1)S(1)}, bf16[256,1024]{1,0:T(8,128)(2,1)S(1)}, u32[]{:S(2)}, u32[]{:S(2)}) collective-permute-start(bf16[256,1024]{1,0:T(8,128)(2,1)S(1)} %get-tuple-element.117), channel_id=1, source_target_pairs={{0,9},{1,8},{4,13},{5,12},{8,1},{9,0},{12,5},{13,4},{2,11},{3,10},... | collective-permute-start | bytes 1572872 | tf_op jit(solution)/shard_map/ppermute | solution.py:337
  199.9 99.8 %collective-permute-start.26 = (bf16[256,1024]{1,0:T(8,128)(2,1)S(1)}, bf16[256,1024]{1,0:T(8,128)(2,1)S(1)}, u32[]{:S(2)}, u32[]{:S(2)}) collective-permute-start(bf16[256,1024]{1,0:T(8,128)(2,1)S(1)} %get-tuple-element.118), channel_id=1, source_target_pairs={{0,12},{1,13},{4,8},{5,9},{8,4},{9,5},{12,0},{13,1},{2,14},{3,15},... | collective-permute-start | bytes 1572872 | tf_op jit(solution)/shard_map/ppermute | solution.py:337
  212.5 87.2 %collective-permute-start.27 = (bf16[256,1024]{1,0:T(8,128)(2,1)S(1)}, bf16[256,1024]{1,0:T(8,128)(2,1)S(1)}, u32[]{:S(2)}, u32[]{:S(2)}) collective-permute-start(bf16[256,1024]{1,0:T(8,128)(2,1)S(1)} %get-tuple-element.119), channel_id=1, source_target_pairs={{0,13},{1,12},{4,9},{5,8},{8,5},{9,4},{12,1},{13,0},{2,15},{3,14},... | collective-permute-start | bytes 1572872 | tf_op jit(solution)/shard_map/ppermute | solution.py:337
  314.0 40.0 %collective-permute-start.36 = (bf16[256,512]{1,0:T(8,128)(2,1)S(1)}, bf16[256,512]{1,0:T(8,128)(2,1)S(1)}, u32[]{:S(2)}, u32[]{:S(2)}) collective-permute-start(bf16[256,512]{1,0:T(8,128)(2,1)S(1)} %get-tuple-element.134), channel_id=1, source_target_pairs={{0,4},{1,5},{4,0},{5,1},{8,12},{9,13},{12,8},{13,9},{2,6},{3,7},{6... | collective-permute-start | bytes 786440 | tf_op jit(solution)/shard_map/ppermute | solution.py:337
  362.5 45.7 %collective-permute-start.32 = (bf16[256,512]{1,0:T(8,128)(2,1)S(1)}, bf16[256,512]{1,0:T(8,128)(2,1)S(1)}, u32[]{:S(2)}, u32[]{:S(2)}) collective-permute-start(bf16[256,512]{1,0:T(8,128)(2,1)S(1)} %get-tuple-element.127), channel_id=1, source_target_pairs={{0,9},{1,8},{4,13},{5,12},{8,1},{9,0},{12,5},{13,4},{2,11},{3,10},... | collective-permute-start | bytes 786440 | tf_op jit(solution)/shard_map/ppermute | solution.py:337
  362.9 46.8 %collective-permute-start.33 = (bf16[256,512]{1,0:T(8,128)(2,1)S(1)}, bf16[256,512]{1,0:T(8,128)(2,1)S(1)}, u32[]{:S(2)}, u32[]{:S(2)}) collective-permute-start(bf16[256,512]{1,0:T(8,128)(2,1)S(1)} %get-tuple-element.128), channel_id=1, source_target_pairs={{0,12},{1,13},{4,8},{5,9},{8,4},{9,5},{12,0},{13,1},{2,14},{3,15},... | collective-permute-start | bytes 786440 | tf_op jit(solution)/shard_map/ppermute | solution.py:337
  408.2 124.4 %collective-permute-start.47 = (bf16[16,64,512]{2,1,0:T(8,128)(2,1)S(1)}, bf16[16,64,512]{2,1,0:T(8,128)(2,1)S(1)}, u32[]{:S(2)}, u32[]{:S(2)}) collective-permute-start(bf16[16,64,512]{2,1,0:T(8,128)(2,1)S(1)} %get-tuple-element.146), channel_id=1, source_target_pairs={{0,2},{2,0},{1,3},{3,1},{4,6},{6,4},{5,7},{7,5},{8,10},{10,8},{9,1... | collective-permute-start | bytes 3145736 | tf_op jit(solution)/shard_map/ppermute | solution.py:347
  409.7 191.1 %collective-permute-start.49 = (bf16[16,64,1024]{2,1,0:T(8,128)(2,1)}, bf16[16,64,1024]{2,1,0:T(8,128)(2,1)}, u32[]{:S(2)}, u32[]{:S(2)}) collective-permute-start(bf16[16,64,1024]{2,1,0:T(8,128)(2,1)} %get-tuple-element.150), channel_id=1, source_target_pairs={{0,2},{2,0},{1,3},{3,1},{4,6},{6,4},{5,7},{7,5},{8,10},{10,8},{9,1... | collective-permute-start | bytes 6291464 | tf_op jit(solution)/shard_map/ppermute | solution.py:347
  410.2 190.5 %collective-permute-start.48 = (bf16[16,64,1024]{2,1,0:T(8,128)(2,1)}, bf16[16,64,1024]{2,1,0:T(8,128)(2,1)}, u32[]{:S(2)}, u32[]{:S(2)}) collective-permute-start(bf16[16,64,1024]{2,1,0:T(8,128)(2,1)} %get-tuple-element.148), channel_id=1, source_target_pairs={{0,2},{2,0},{1,3},{3,1},{4,6},{6,4},{5,7},{7,5},{8,10},{10,8},{9,1... | collective-permute-start | bytes 6291464 | tf_op jit(solution)/shard_map/ppermute | solution.py:347
  421.4 103.1 %collective-permute-start.42 = (f32[128,128]{1,0:T(8,128)S(1)}, f32[128,128]{1,0:T(8,128)S(1)}, u32[]{:S(2)}, u32[]{:S(2)}) collective-permute-start(f32[128,128]{1,0:T(8,128)S(1)} %slice_bitcast_fusion), channel_id=1, source_target_pairs={{0,2},{2,0},{1,3},{3,1},{4,6},{6,4},{5,7},{7,5},{8,10},{10,8},{9,1... | collective-permute-start | bytes 196616 | tf_op jit(solution)/shard_map/ppermute | solution.py:355
  532.6 47.4 %collective-permute-start.51 = (bf16[16,64,512]{2,1,0:T(8,128)(2,1)}, bf16[16,64,512]{2,1,0:T(8,128)(2,1)}, u32[]{:S(2)}, u32[]{:S(2)}) collective-permute-start(bf16[16,64,512]{2,1,0:T(8,128)(2,1)} %get-tuple-element.154), channel_id=1, source_target_pairs={{0,2},{2,0},{1,3},{3,1},{4,6},{6,4},{5,7},{7,5},{8,10},{10,8},{9,1... | collective-permute-start | bytes 3145736 | tf_op jit(solution)/shard_map/ppermute | solution.py:347
  535.8 65.0 %collective-permute-start.50 = (bf16[16,64,512]{2,1,0:T(8,128)(2,1)}, bf16[16,64,512]{2,1,0:T(8,128)(2,1)}, u32[]{:S(2)}, u32[]{:S(2)}) collective-permute-start(bf16[16,64,512]{2,1,0:T(8,128)(2,1)} %get-tuple-element.152), channel_id=1, source_target_pairs={{0,2},{2,0},{1,3},{3,1},{4,6},{6,4},{5,7},{7,5},{8,10},{10,8},{9,1... | collective-permute-start | bytes 3145736 | tf_op jit(solution)/shard_map/ppermute | solution.py:347
  (46 other events, 816.0 us)

commit v3 on v1

--- a/solution.py
+++ b/solution.py
@@ -13,6 +13,10 @@
 SPAN = 2 * NFFT
 LANES = 128
 SUBLANES = 8
+SHORT = pl.CostEstimate(flops=1, bytes_accessed=1, transcendentals=0)
+PREPARE_ROWS = 64
+PREPARE_PIECES = 8
+AHEAD = 2
 GROUP_ROWS = 2 * SUBLANES
 MIB = 1 << 20
 
@@ -32,13 +36,61 @@
     return table.astype(jnp.bfloat16).reshape(offsets.shape[0] // 2, -1, SPAN)
 
 
-def spectra_kernel(window_start, history, basis, total_in, *outs, members):
-    coefs = outs[:members]
-    total_out = outs[members]
+def prepare_kernel(ticket_ref, *refs, units):
+    del ticket_ref
+    sources, target = refs[:-1], refs[-1]
+    points = units * LANES
+    for number, source in enumerate(sources):
+        piece, unit = divmod(number, units)
+        for plane in range(source.shape[1]):
+            first = plane * points + unit * LANES
+            target[piece, :, first : first + LANES] = source[:, plane, :]
+
+
+def prepare(ticket, series, offset, points, count):
+    snap_rows, slab_rows, plane = series.shape
+    first, stride, units = offset // LANES, plane // count // LANES, points // LANES
+    step_rows = min(snap_rows, PREPARE_ROWS)
+    together = min(count, PREPARE_PIECES)
+
+    def source_map(piece, unit):
+        return lambda part, step, ticket_ref: (
+            step,
+            0,
+            (part * together + piece) * stride + first + unit,
+        )
+
+    return pl.pallas_call(
+        functools.partial(prepare_kernel, units=units),
+        grid_spec=pltpu.PrefetchScalarGridSpec(
+            num_scalar_prefetch=1,
+            grid=(count // together, snap_rows // step_rows),
+            in_specs=[
+                pl.BlockSpec((step_rows, slab_rows, LANES), source_map(piece, unit))
+                for piece in range(together)
+                for unit in range(units)
+            ],
+            out_specs=pl.BlockSpec(
+                (together, step_rows, slab_rows * points),
+                lambda part, step, ticket_ref: (part, step, 0),
+            ),
+        ),
+        out_shape=jax.ShapeDtypeStruct((count, snap_rows, slab_rows * points), series.dtype),
+        compiler_params=pltpu.CompilerParams(vmem_limit_bytes=40 * MIB),
+        cost_estimate=SHORT,
+        name="prepare",
+    )(ticket, *([series] * (together * units)))
+
+
+def spectra_kernel(ticket_ref, window_start, history, basis, total_in, *refs, members, unroll):
+    del ticket_ref
+    coefs = refs[:members]
+    total_out = refs[members]
     rows = coefs[0].shape[1]
     pairs = basis.shape[0]
     width = history.shape[1]
-    for pair in range(pairs):
+
+    def transform(pair, carry):
         start = pl.multiple_of(window_start[pair], 16)
         segment = history[pl.ds(start, SPAN), :]
         both = jnp.dot(basis[pair], segment, preferred_element_type=jnp.float32)
@@ -47,25 +99,34 @@
             for member in range(members):
                 first = (half * members + member) * rows
                 coefs[member][2 * pair + half] = both[first : first + rows]
-    lane = lax.broadcasted_iota(jnp.int32, (2 * pairs * SUBLANES, LANES), 1)
-    sub = lax.broadcasted_iota(jnp.int32, (2 * pairs * SUBLANES, LANES), 0) % SUBLANES
+        return carry
+
+    lax.fori_loop(0, pairs, transform, 0, unroll=unroll)
+    packed_rows = 2 * pairs * SUBLANES
+    lane = lax.broadcasted_iota(jnp.int32, (packed_rows, LANES), 1)
+    sub = lax.broadcasted_iota(jnp.int32, (packed_rows, LANES), 0) % SUBLANES
     place = (lane - sub) & (LANES - 1)
     for member in range(members):
-        packed = [jnp.zeros((2 * pairs * SUBLANES, LANES), jnp.float32) for _ in range(2)]
-        for group in range(rows // GROUP_ROWS):
-            tile = coefs[member][:, group * GROUP_ROWS : (group + 1) * GROUP_ROWS, :]
+
+        def add_group(group, packed):
+            first = pl.multiple_of(group * GROUP_ROWS, GROUP_ROWS)
+            tile = coefs[member][:, pl.ds(first, GROUP_ROWS), :]
             tile = tile.reshape(2 * pairs * GROUP_ROWS, width)
             gram = lax.dot_general(
                 tile, tile, (((1,), (1,)), ((), ())), preferred_element_type=jnp.float32
             )
             gram = gram.reshape(2 * pairs, 2, SUBLANES, 2 * LANES)
+            packed = list(packed)
             for c in range(2):
                 for high in range(2):
                     shift = group + 4 * high
                     part = gram[:, c, :, high * LANES : (high + 1) * LANES]
-                    part = part.reshape(2 * pairs * SUBLANES, LANES)
-                    part = pltpu.roll(part, shift, 1) if shift else part
+                    part = pltpu.roll(part.reshape(packed_rows, LANES), shift, 1)
                     packed[c] = jnp.where(place % 8 == shift, part, packed[c])
+            return tuple(packed)
+
+        empty = jnp.zeros((packed_rows, LANES), jnp.float32)
+        packed = lax.fori_loop(0, rows // GROUP_ROWS, add_group, (empty, empty), unroll=unroll)
         swapped = jnp.where(
             (place // 8) % 2 == 0,
             pltpu.roll(packed[1], LANES - 8, 1),
@@ -74,25 +135,22 @@
         total_out[member] = total_in[member] + (packed[0] + swapped)
 
 
-def spectra(window_start, history, basis, total, members):
+def spectra(ticket, window_start, history, basis, total, members, unroll):
     width = history.shape[1]
     blocks = 2 * basis.shape[0]
     rows = basis.shape[1] // 2 // members
+    smem = pl.BlockSpec(memory_space=pltpu.SMEM)
     vmem = pl.BlockSpec(memory_space=pltpu.VMEM)
     outs = [jax.ShapeDtypeStruct((blocks, rows, width), jnp.bfloat16)] * members
     return pl.pallas_call(
-        functools.partial(spectra_kernel, members=members),
+        functools.partial(spectra_kernel, members=members, unroll=unroll),
         out_shape=outs + [jax.ShapeDtypeStruct(total.shape, jnp.float32)],
-        in_specs=[pl.BlockSpec(memory_space=pltpu.SMEM), vmem, vmem, vmem],
+        in_specs=[smem, smem, vmem, vmem, vmem],
         out_specs=[vmem] * (members + 1),
         compiler_params=pltpu.CompilerParams(vmem_limit_bytes=40 * MIB),
-        cost_estimate=pl.CostEstimate(
-            flops=2 * blocks * members * rows * width * (SPAN + 256),
-            bytes_accessed=2 * (history.size + basis.size + blocks * members * rows * width),
-            transcendentals=0,
-        ),
+        cost_estimate=SHORT,
         name="spectra",
-    )(window_start, history, basis, total)
+    )(ticket, window_start, history, basis, total)
 
 
 def power_kernel(total, mix, scale, spectrum, *, blocks, norm_scale):
@@ -169,29 +227,36 @@
     )(total)
 
 
-def modes_kernel(member_ref, mix, scale, *refs, chunks, members):
+def modes_kernel(member_ref, mix, scale, *refs, chunks, members, offset):
     coefs = refs[: chunks * members]
-    out, buffer, sems = refs[chunks * members :]
+    out = refs[chunks * members + (1 if offset else 0)]
+    scratch = refs[-2 * chunks - 2 :]
+    buffers, results = scratch[:chunks], scratch[chunks : 2 * chunks]
+    sems, out_sems = scratch[2 * chunks :]
     member = member_ref[0]
     copies = []
     for chunk in range(chunks):
         for turn in range(members):
             slot = lax.rem(member + members - turn, members)
             copy = pltpu.make_async_copy(
-                coefs[chunk * members + turn], buffer.at[chunk, slot], sems.at[chunk, turn]
+                coefs[chunk * members + turn], buffers[chunk].at[slot], sems.at[chunk, turn]
             )
             copy.start()
             copies.append(copy)
-    width = coefs[0].shape[2]
-    padded = coefs[0].shape[0]
     planes = out.shape[2] // members
-    points = width // planes
+    out_copies = []
+    done = offset
     for chunk in range(chunks):
         for turn in range(members):
             copies[chunk * members + turn].wait()
-        for slot in range(members):
-            for group in range(mix.shape[0]):
-                tile = buffer[chunk, slot, :, group * GROUP_ROWS : (group + 1) * GROUP_ROWS, :]
+        padded, width = buffers[chunk].shape[1], buffers[chunk].shape[3]
+        points = width // planes
+
+        def one_group(group, carry):
+            first = pl.multiple_of(group * GROUP_ROWS, GROUP_ROWS)
+            factor = jnp.tile(scale[group], (1, points // LANES))
+            for slot in range(members):
+                tile = buffers[chunk][slot, :, pl.ds(first, GROUP_ROWS), :]
                 tile = tile.reshape(padded * GROUP_ROWS, width)
                 raw = jnp.dot(mix[group], tile, preferred_element_type=jnp.float32)
                 for e in range(2):
@@ -199,33 +264,57 @@
                         part = raw[
                             e * SUBLANES : (e + 1) * SUBLANES, plane * points : (plane + 1) * points
                         ]
-                        out[
-                            e,
-                            group * SUBLANES : (group + 1) * SUBLANES,
-                            slot * planes + plane,
-                            chunk * points : (chunk + 1) * points,
-                        ] = part * jnp.tile(scale[group], (1, points // LANES))
-
-
-def project(member, mix, scale, coefs, members, planes, points):
+                        target = pl.ds(pl.multiple_of(group * SUBLANES, SUBLANES), SUBLANES)
+                        results[chunk][e, target, slot * planes + plane, :] = part * factor
+            return carry
+
+        lax.fori_loop(0, mix.shape[0], one_group, 0)
+        copy = pltpu.make_async_copy(
+            results[chunk], out.at[:, :, :, pl.ds(done, points)], out_sems.at[chunk]
+        )
+        copy.start()
+        out_copies.append(copy)
+        done += points
+    for copy in out_copies:
+        copy.wait()
+
+
+def project(member, mix, scale, coefs, members, planes, points, offset, before):
     chunks = len(coefs) // members
     groups = mix.shape[0]
     vmem = pl.BlockSpec(memory_space=pltpu.VMEM)
+    hbm = pl.BlockSpec(memory_space=pl.ANY)
+    extra = [] if before is None else [before]
+    sizes = [part.shape[2] // planes for part in coefs[::members]]
     return pl.pallas_call(
-        functools.partial(modes_kernel, chunks=chunks, members=members),
+        functools.partial(modes_kernel, chunks=chunks, members=members, offset=offset),
         out_shape=jax.ShapeDtypeStruct(
             (2, groups * SUBLANES, members * planes, points), jnp.float32
         ),
         in_specs=[pl.BlockSpec(memory_space=pltpu.SMEM), vmem, vmem]
-        + [pl.BlockSpec(memory_space=pl.ANY)] * len(coefs),
-        out_specs=vmem,
+        + [hbm] * (len(coefs) + len(extra)),
+        out_specs=hbm,
+        input_output_aliases={3 + len(coefs): 0} if extra else {},
         scratch_shapes=[
-            pltpu.VMEM((chunks, members) + coefs[0].shape, jnp.bfloat16),
-            pltpu.SemaphoreType.DMA((chunks, members)),
-        ],
+            pltpu.VMEM((members,) + part.shape, jnp.bfloat16) for part in coefs[::members]
+        ]
+        + [
+            pltpu.VMEM((2, groups * SUBLANES, members * planes, size), jnp.float32)
+            for size in sizes
+        ]
+        + [pltpu.SemaphoreType.DMA((chunks, members)), pltpu.SemaphoreType.DMA((chunks,))],
         compiler_params=pltpu.CompilerParams(vmem_limit_bytes=48 * MIB),
+        cost_estimate=SHORT,
         name="modes",
-    )(member, mix, scale, *coefs)
+    )(member, mix, scale, *coefs, *extra)
+
+
+def chunk_sizes(width):
+    if width % (8 * LANES):
+        return [LANES] * (width // LANES)
+    quarter = width // (4 * LANES) * LANES
+    last = quarter // 2
+    return [quarter, width - 2 * quarter - last, quarter, last]
 
 
 def butterfly_sum(value, axes, count):
@@ -244,8 +333,6 @@
     members = lax.axis_size("freq")
     member = lax.axis_index("freq")
     width = plane // group_count
-    chunk_points = LANES
-    chunks = width // chunk_points
     blocks = block_start.shape[0]
     pairs = (blocks + 1) // 2
     frames = snap_rows * group_count
@@ -256,30 +343,61 @@
     window_start = jnp.minimum(starts[::2] // 16 * 16, frames - SPAN)
     basis = shifted_basis(freq_order, starts - jnp.repeat(window_start, 2), blocks)
 
-    tiles = series.reshape(snap_rows, slab_rows, group_count, chunks, chunk_points)
     total = jnp.zeros((members, 2 * pairs * SUBLANES, LANES), jnp.float32)
-    coefs = []
-    for chunk in range(chunks):
-        piece = jnp.transpose(tiles[:, :, :, chunk, :], (2, 0, 1, 3))
-        piece = piece.reshape(group_count, snap_rows, slab_rows * chunk_points)
-        history = lax.all_to_all(piece, line, split_axis=0, concat_axis=0, tiled=True)
-        history = history.reshape(frames, slab_rows * chunk_points)
-        *sent, total = spectra(window_start, history, basis, total, members)
-        coefs.append(sent[0])
+    sizes = chunk_sizes(width)
+    offsets = [sum(sizes[:chunk]) for chunk in range(len(sizes))]
+    coefs, histories, ticket = [], [], jnp.zeros((1,), jnp.int32)
+
+    prepared = []
+
+    def get_ready(chunk, ticket):
+        parts = prepare(ticket, series, offsets[chunk], sizes[chunk], group_count)
+        ticket, parts = lax.optimization_barrier((ticket, parts))
+        prepared.append(parts)
+        return ticket
+
+    def exchange(chunk):
+        parts = prepared[chunk]
+        if chunk >= 2:
+            parts, coefs[chunk - 2][1:] = lax.optimization_barrier((parts, coefs[chunk - 2][1:]))
+        history = lax.all_to_all(parts, line, split_axis=0, concat_axis=0, tiled=True)
+        histories.append(history.reshape(frames, -1))
+
+    for chunk in range(min(AHEAD, len(sizes))):
+        ticket = get_ready(chunk, ticket)
+        exchange(chunk)
+    for chunk in range(len(sizes)):
+        last = chunk + 1 == len(sizes)
+        *sent, total = spectra(
+            ticket, window_start, histories[chunk], basis, total, members, last
+        )
+        if chunk + AHEAD < len(sizes):
+            ticket, total = lax.optimization_barrier((ticket, total))
+            ticket = get_ready(chunk + AHEAD, ticket)
+        rings = [[(i, (i + turn) % members) for i in range(members)] for turn in range(members)]
+        if last:
+            others = [lax.ppermute(total[turn], "freq", rings[turn]) for turn in range(1, members)]
+            others, sent[1:] = lax.optimization_barrier((others, sent[1:]))
         for turn in range(1, members):
-            ring = [(i, (i + turn) % members) for i in range(members)]
-            coefs.append(lax.ppermute(sent[turn], "freq", ring))
-
-    mine = total[0]
-    for turn in range(1, members):
-        ring = [(i, (i + turn) % members) for i in range(members)]
-        mine = mine + lax.ppermute(total[turn], "freq", ring)
+            sent[turn] = lax.ppermute(sent[turn], "freq", rings[turn])
+        coefs.append(sent)
+        if chunk + AHEAD < len(sizes):
+            exchange(chunk + AHEAD)
+
+    mine = functools.reduce(jnp.add, others, total[0])
     mine = butterfly_sum(mine, line, group_count)
 
     groups = freq_index.shape[0] // members // SUBLANES
     norm_scale = 1.0 / (blocks * slab_rows * members * plane)
     mix, scale, spectrum = leading_vectors(mine, groups, blocks, norm_scale)
-    modes = project(member.reshape(1), mix, scale, coefs, members, slab_rows, width)
+    modes = None
+    for chunk_range in (range(len(sizes) - 1), range(len(sizes) - 1, len(sizes))):
+        if len(chunk_range):
+            parts = [part for chunk in chunk_range for part in coefs[chunk]]
+            offset = offsets[chunk_range[0]]
+            modes = project(
+                member.reshape(1), mix, scale, parts, members, slab_rows, width, offset, modes
+            )
     return (modes, spectrum[:, :, 0].reshape(-1))
 
 

time: 651 us -> 454 us (0.70)
  waiting for transfers between devices: 433 us -> 300 us
  local copies, waits for them, and re-layouts: 111 us -> 21.1 us
  Pallas kernels: 40.4 us -> 86.6 us
  starting transfers between devices: 50.4 us -> 32.1 us
    all_to_all x8 -> x4, waiting for transfers between devices: 323 us -> 190 us  [exchange(): lax.all_to_all(parts, line, split_axis=0, concat_axis=0, tiled=True)]
    pallas_call x8, Pallas kernels: 28.7 us -> 73.4 us  [the longest x4 37.7 us: prepare(): pl.pallas_call(functools.partial(prepare_kernel, units=units), grid_spec=...]
    transpose x9 -> x0, local copies, waits for them, and re-layouts: 33 us -> none  [shards(): piece = jnp.transpose(tiles[:, :, :, chunk, :], (2, 0, 1, 3))]
    all_to_all x8 -> x0, local copies, waits for them, and re-layouts: 31.4 us -> none  [shards(): lax.all_to_all(piece, line, split_axis=0, concat_axis=0, tiled=True)]
    unnamed x47 -> x28, local copies, waits for them, and re-layouts: 43.9 us -> 18.1 us
    all_to_all x8 -> x4, starting transfers between devices: 37.1 us -> 20.2 us  [exchange(): lax.all_to_all(parts, line, split_axis=0, concat_axis=0, tiled=True)]
    ppermute x9 -> x5, waiting for transfers between devices: 104 us -> 103 us  [the longest x4 97.2 us: shards(): sent[turn] = lax.ppermute(sent[turn], 'freq', rings[turn])]
  transfers between devices with their start and end apart: 20 -> 12, of which waited for: 16 -> 10; matrix products, arithmetic and copies ran while one was open for 10% -> 3% of each run, Pallas kernels for 5% -> 17%
where the time goes in v3:
time: 454 us; the launch traced here: 453 us
  waiting for transfers between devices  300 us (66%)
  Pallas kernels  86.6 us (19%)
  starting transfers between devices  32.1 us (7%)
  local copies, waits for them, and re-layouts  21.1 us (5%)
  other arithmetic  11.9 us (3%)
    all_to_all x4, waiting for transfers between devices, exchange(): lax.all_to_all(parts, line, split_axis=0, concat_axis=0, tiled=True)  190 us
    ppermute x4, waiting for transfers between devices, shards(): sent[turn] = lax.ppermute(sent[turn], 'freq', rings[turn])  97.2 us
    pallas_call x4, Pallas kernels, prepare(): pl.pallas_call(functools.partial(prepare_kernel, units=units), grid_spec=...  37.7 us
    pallas_call x4, Pallas kernels, spectra(): pl.pallas_call(functools.partial(spectra_kernel, members=members, unroll=...  35.7 us
    all_to_all x4, starting transfers between devices, exchange(): lax.all_to_all(parts, line, split_axis=0, concat_axis=0, tiled=True)  20.2 us
    unnamed x28, local copies, waits for them, and re-layouts  18.1 us
  transfers between devices with their start and end apart: 12, of which 10 were waited for; matrix products, arithmetic and copies ran while one was open for 3% of the time, Pallas kernels for 17%

profile of v3, /device:TPU:0, one launch (start us, length us, event | category | flops | bytes accessed | tf_op | source)
XLA Modules:
  0.0 453.1 jit_solution(12524829586876660716)
XLA Ops:
  0.6 9.4 %prepare.4 = bf16[8,256,1024]{2,1,0:T(8,128)(2,1)S(1)} custom-call(s32[1]{0:T(128)} %constant.32.clone.1.ticket_ref, bf16[256,4,8192]{2,1,0:T(4,128)(2,1)} %refs_7_.7, bf16[256,4,8192]{2,1,0:T(4,128)(2,1)} %refs_7_.7, bf16[256,4,8192]{2,1,0:T(4,128)(2,1)} %refs_7_.7, bf16[256,4,8192]{2,1,0:T(4,128)(2,1)} %refs_7_.7, bf16[256,4,8192]{2,1,0:T(4,128)(2,1)} %refs_7_.7, ...), custom_call_target="tpu_custom_call" | custom-call | flops 1 | bytes 1 | tf_op jit(solution)/shard_map/prepare/pallas_call | solution.py:63
  12.0 6.3 %all-to-all-start = ((bf16[8,256,1024]{2,1,0:T(8,128)(2,1)}), bf16[8,256,1024]{2,1,0:T(8,128)(2,1)}, u32[]{:S(2)}, u32[]{:S(2)}) async-start(bf16[8,256,1024]{2,1,0:T(8,128)(2,1)} %copy-done.2), calls=%async_computation | async-start | bytes 8388608 | tf_op jit(solution)/shard_map/all_to_all | solution.py:363
  18.3 13.5 %prepare.5 = bf16[8,256,1536]{2,1,0:T(8,128)(2,1)S(1)} custom-call(s32[1]{0:T(128)} %constant.32.clone.1.ticket_ref, bf16[256,4,8192]{2,1,0:T(4,128)(2,1)} %refs_7_.7, bf16[256,4,8192]{2,1,0:T(4,128)(2,1)} %refs_7_.7, bf16[256,4,8192]{2,1,0:T(4,128)(2,1)} %refs_7_.7, bf16[256,4,8192]{2,1,0:T(4,128)(2,1)} %refs_7_.7, bf16[256,4,8192]{2,1,0:T(4,128)(2,1)} %refs_7_.7, ...), custom_call_target="tpu_custom_call" | custom-call | flops 1 | bytes 1 | tf_op jit(solution)/shard_map/prepare/pallas_call | solution.py:63
  34.5 77.9 %all-to-all-done = bf16[8,256,1024]{2,1,0:T(8,128)(2,1)} async-done(((bf16[8,256,1024]{2,1,0:T(8,128)(2,1)}), bf16[8,256,1024]{2,1,0:T(8,128)(2,1)}, u32[]{:S(2)}, u32[]{:S(2)}) %all-to-all-start) | async-done | bytes 4194336 | tf_op jit(solution)/shard_map/all_to_all | solution.py:363
  112.4 4.9 %all-to-all-start.1 = ((bf16[8,256,1536]{2,1,0:T(8,128)(2,1)}), bf16[8,256,1536]{2,1,0:T(8,128)(2,1)}, u32[]{:S(2)}, u32[]{:S(2)}) async-start(bf16[8,256,1536]{2,1,0:T(8,128)(2,1)} %copy-done), calls=%async_computation.1 | async-start | bytes 12582912 | tf_op jit(solution)/shard_map/all_to_all | solution.py:363
  122.1 8.2 %fusion.4 = (f32[16,8,1,8,512]{4,3,2,1,0:T(8,128)S(1)}, f32[16,8,1,8,512]{4,3,2,1,0:T(8,128)S(1)}) fusion(s32[16,512]{1,0:T(8,128)S(1)} %fusion.5, s32[8,8]{1,0:T(8,128)S(1)} %mul.86), kind=kLoop, calls=%fused_computation.12 | loop fusion | flops 7864320 | bytes 4227328 | tf_op jit(solution)/shard_map/cos | solution.py:35
  131.0 9.2 %spectra.4 = (bf16[16,64,1024]{2,1,0:T(8,128)(2,1)S(1)}, bf16[16,64,1024]{2,1,0:T(8,128)(2,1)S(1)}, f32[2,128,128]{2,1,0:T(8,128)S(1)}) custom-call(s32[1]{0:T(128)} %constant.32.clone.1.ticket_ref, s32[8]{0:T(128)S(1)} %multiply_minimum_fusion.window_start, bf16[2048,1024]{1,0:T(8,128)(2,1)} %bitcast.1.history, bf16[8,256,512]{2,1,0:T(8,128)(2,1)S(1)} %bitcast.12, ...), custom_call_target="tpu_custom_call" | custom-call | flops 1 | bytes 1 | tf_op jit(solution)/shard_map/spectra/pallas_call | solution.py:145
  143.0 9.6 %prepare.6 = bf16[8,256,1024]{2,1,0:T(8,128)(2,1)S(1)} custom-call(s32[1]{0:T(128)} %constant.32.clone.1.ticket_ref, bf16[256,4,8192]{2,1,0:T(4,128)(2,1)} %refs_7_.7, bf16[256,4,8192]{2,1,0:T(4,128)(2,1)} %refs_7_.7, bf16[256,4,8192]{2,1,0:T(4,128)(2,1)} %refs_7_.7, bf16[256,4,8192]{2,1,0:T(4,128)(2,1)} %refs_7_.7, bf16[256,4,8192]{2,1,0:T(4,128)(2,1)} %refs_7_.7, ...), custom_call_target="tpu_custom_call" | custom-call | flops 1 | bytes 1 | tf_op jit(solution)/shard_map/prepare/pallas_call | solution.py:63
  154.5 34.7 %collective-permute-done.1.refs_1_ = bf16[16,64,1024]{2,1,0:T(8,128)(2,1)S(1)} collective-permute-done((bf16[16,64,1024]{2,1,0:T(8,128)(2,1)S(1)}, bf16[16,64,1024]{2,1,0:T(8,128)(2,1)S(1)}, u32[]{:S(2)}, u32[]{:S(2)}) %collective-permute-start.1) | collective-permute-done | bytes 2097184 | tf_op jit(solution)/shard_map/ppermute | solution.py:382
  190.5 65.6 %all-to-all-done.1 = bf16[8,256,1536]{2,1,0:T(8,128)(2,1)} async-done(((bf16[8,256,1536]{2,1,0:T(8,128)(2,1)}), bf16[8,256,1536]{2,1,0:T(8,128)(2,1)}, u32[]{:S(2)}, u32[]{:S(2)}) %all-to-all-start.1) | async-done | bytes 6291488 | tf_op jit(solution)/shard_map/all_to_all | solution.py:363
  256.1 4.6 %all-to-all-start.3 = ((bf16[8,256,1024]{2,1,0:T(8,128)(2,1)}), bf16[8,256,1024]{2,1,0:T(8,128)(2,1)}, u32[]{:S(2)}, u32[]{:S(2)}) async-start(bf16[8,256,1024]{2,1,0:T(8,128)(2,1)} %copy-done.1), calls=%async_computation.3 | async-start | bytes 8388608 | tf_op jit(solution)/shard_map/all_to_all | solution.py:363
  260.7 11.4 %spectra.5 = (bf16[16,64,1536]{2,1,0:T(8,128)(2,1)S(1)}, bf16[16,64,1536]{2,1,0:T(8,128)(2,1)S(1)}, f32[2,128,128]{2,1,0:T(8,128)S(1)}) custom-call(s32[1]{0:T(128)} %constant.32.clone.1.ticket_ref, s32[8]{0:T(128)S(1)} %multiply_minimum_fusion.window_start, bf16[2048,1536]{1,0:T(8,128)(2,1)} %bitcast.4.history, bf16[8,256,512]{2,1,0:T(8,128)(2,1)S(1)} %bitcast.13, ...), custom_call_target="tpu_custom_call" | custom-call | flops 1 | bytes 1 | tf_op jit(solution)/shard_map/spectra/pallas_call | solution.py:145
  275.3 5.2 %prepare.7 = bf16[8,256,512]{2,1,0:T(8,128)(2,1)S(1)} custom-call(s32[1]{0:T(128)} %constant.32.clone.1.ticket_ref, bf16[256,4,8192]{2,1,0:T(4,128)(2,1)} %refs_7_.7, bf16[256,4,8192]{2,1,0:T(4,128)(2,1)} %refs_7_.7, bf16[256,4,8192]{2,1,0:T(4,128)(2,1)} %refs_7_.7, bf16[256,4,8192]{2,1,0:T(4,128)(2,1)} %refs_7_.7, bf16[256,4,8192]{2,1,0:T(4,128)(2,1)} %refs_7_.7, ...), custom_call_target="tpu_custom_call" | custom-call | flops 1 | bytes 1 | tf_op jit(solution)/shard_map/prepare/pallas_call | solution.py:63
  281.8 62.5 %collective-permute-done.refs_3_ = bf16[16,64,1536]{2,1,0:T(8,128)(2,1)} collective-permute-done((bf16[16,64,1536]{2,1,0:T(8,128)(2,1)S(1)}, bf16[16,64,1536]{2,1,0:T(8,128)(2,1)}, u32[]{:S(2)}, u32[]{:S(2)}) %collective-permute-start) | collective-permute-done | bytes 3145760 | tf_op jit(solution)/shard_map/ppermute | solution.py:382
  344.2 10.5 %all-to-all-done.3 = bf16[8,256,1024]{2,1,0:T(8,128)(2,1)} async-done(((bf16[8,256,1024]{2,1,0:T(8,128)(2,1)}), bf16[8,256,1024]{2,1,0:T(8,128)(2,1)}, u32[]{:S(2)}, u32[]{:S(2)}) %all-to-all-start.3) | async-done | bytes 4194336 | tf_op jit(solution)/shard_map/all_to_all | solution.py:363
  354.7 4.4 all-to-all-start.2
  359.1 10.5 %spectra.6 = (bf16[16,64,1024]{2,1,0:T(8,128)(2,1)S(1)}, bf16[16,64,1024]{2,1,0:T(8,128)(2,1)}, f32[2,128,128]{2,1,0:T(8,128)S(1)}) custom-call(s32[1]{0:T(128)} %constant.32.clone.1.ticket_ref, s32[8]{0:T(128)S(1)} %multiply_minimum_fusion.window_start, bf16[2048,1024]{1,0:T(8,128)(2,1)} %bitcast.6.history, bf16[8,256,512]{2,1,0:T(8,128)(2,1)S(1)} %bitcast.14, ...), custom_call_target="tpu_custom_call" | custom-call | flops 1 | bytes 1 | tf_op jit(solution)/shard_map/spectra/pallas_call | solution.py:145
  372.5 35.7 %all-to-all-done.2 = bf16[8,256,512]{2,1,0:T(8,128)(2,1)} async-done(((bf16[8,256,512]{2,1,0:T(8,128)(2,1)}), bf16[8,256,512]{2,1,0:T(8,128)(2,1)}, u32[]{:S(2)}, u32[]{:S(2)}) %all-to-all-start.2) | async-done | bytes 2097184 | tf_op jit(solution)/shard_map/all_to_all | solution.py:363
  408.2 4.6 %spectra.7 = (bf16[16,64,512]{2,1,0:T(8,128)(2,1)S(1)}, bf16[16,64,512]{2,1,0:T(8,128)(2,1)}, f32[2,128,128]{2,1,0:T(8,128)S(1)}) custom-call(s32[1]{0:T(128)} %constant.32.clone.1.ticket_ref, s32[8]{0:T(128)S(1)} %multiply_minimum_fusion.window_start, bf16[2048,512]{1,0:T(8,128)(2,1)} %bitcast.5.history, bf16[8,256,512]{2,1,0:T(8,128)(2,1)S(1)} %bitcast.15, ...), custom_call_target="tpu_custom_call" | custom-call | flops 1 | bytes 1 | tf_op jit(solution)/shard_map/spectra/pallas_call | solution.py:145
  414.3 6.2 %collective-permute-done.2 = f32[128,128]{1,0:T(8,128)S(1)} collective-permute-done((f32[128,128]{1,0:T(8,128)S(1)}, f32[128,128]{1,0:T(8,128)S(1)}, u32[]{:S(2)}, u32[]{:S(2)}) %collective-permute-start.2) | collective-permute-done | bytes 65568 | tf_op jit(solution)/shard_map/ppermute | solution.py:379
  427.7 2.6 collective-permute-start.5
  430.3 2.7 collective-permute-done.5
  433.7 4.9 %power.1 = (bf16[4,16,256]{2,1,0:T(8,128)(2,1)}, f32[4,8,128]{2,1,0:T(8,128)}, f32[4,8,128]{2,1,0:T(8,128)}) custom-call(f32[128,128]{1,0:T(8,128)} %add.74.total), custom_call_target="tpu_custom_call" | custom-call | tf_op jit(solution)/shard_map/power/pallas_call | solution.py:217
  444.6 6.6 %modes.2.refs_2_ = f32[2,32,8,1024]{3,2,1,0:T(8,128)} custom-call(s32[1]{0:T(128)} %bitcast.member_ref, bf16[4,16,256]{2,1,0:T(8,128)(2,1)S(1)} %copy-done.10, f32[4,8,128]{2,1,0:T(8,128)S(1)} %copy-done.11, bf16[16,64,1024]{2,1,0:T(8,128)(2,1)S(1)} %copy-done.6, bf16[16,64,1024]{2,1,0:T(8,128)(2,1)S(1)} %copy-done.8, bf16[16,64,1536]{2,1,0:T(8,128)(2,1)} %copy-done.4, ...), custom_call_target="tpu_custom_call" | custom-call | flops 1 | bytes 1 | tf_op jit(solution)/shard_map/modes/pallas_call | solution.py:289
  (65 shorter events, 39.6 us)
Async XLA Ops:
  10.0 2.0 copy-start.2
  12.0 100.4 %all-to-all-start = ((bf16[8,256,1024]{2,1,0:T(8,128)(2,1)}), bf16[8,256,1024]{2,1,0:T(8,128)(2,1)}, u32[]{:S(2)}, u32[]{:S(2)}) async-start(bf16[8,256,1024]{2,1,0:T(8,128)(2,1)} %copy-done.2), calls=%async_computation | async-start | bytes 8388608 | tf_op jit(solution)/shard_map/all_to_all | solution.py:363
  31.8 2.6 copy-start
  34.5 84.2 %copy-start.12 = (s32[15]{0:T(128)S(1)}, s32[15]{0:T(128)}, u32[]{:S(2)}) copy-start(s32[15]{0:T(128)} %param.4) | copy-start | bytes 184
  34.5 85.7 %copy-start.13 = (s32[64]{0:T(128)S(1)}, s32[64]{0:T(128)}, u32[]{:S(2)}) copy-start(s32[64]{0:T(128)} %param.5) | copy-start | bytes 772
  112.4 143.7 %all-to-all-start.1 = ((bf16[8,256,1536]{2,1,0:T(8,128)(2,1)}), bf16[8,256,1536]{2,1,0:T(8,128)(2,1)}, u32[]{:S(2)}, u32[]{:S(2)}) async-start(bf16[8,256,1536]{2,1,0:T(8,128)(2,1)} %copy-done), calls=%async_computation.1 | async-start | bytes 12582912 | tf_op jit(solution)/shard_map/all_to_all | solution.py:363
  140.2 1.4 copy-start.5
  141.5 47.7 %collective-permute-start.1 = (bf16[16,64,1024]{2,1,0:T(8,128)(2,1)S(1)}, bf16[16,64,1024]{2,1,0:T(8,128)(2,1)S(1)}, u32[]{:S(2)}, u32[]{:S(2)}) collective-permute-start(bf16[16,64,1024]{2,1,0:T(8,128)(2,1)S(1)} %get-tuple-element.50), channel_id=1, source_target_pairs={{0,2},{2,0},{1,3},{3,1},{4,6},{6,4},{5,7},{7,5},{8,10},{10,8},{9,1... | collective-permute-start | bytes 6291464 | tf_op jit(solution)/shard_map/ppermute | solution.py:382
  152.6 2.0 copy-start.1
  189.2 1.3 copy-start.7
  256.1 98.6 %all-to-all-start.3 = ((bf16[8,256,1024]{2,1,0:T(8,128)(2,1)}), bf16[8,256,1024]{2,1,0:T(8,128)(2,1)}, u32[]{:S(2)}, u32[]{:S(2)}) async-start(bf16[8,256,1024]{2,1,0:T(8,128)(2,1)} %copy-done.1), calls=%async_computation.3 | async-start | bytes 8388608 | tf_op jit(solution)/shard_map/all_to_all | solution.py:363
  272.1 1.6 copy-start.4
  273.8 70.5 %collective-permute-start = (bf16[16,64,1536]{2,1,0:T(8,128)(2,1)S(1)}, bf16[16,64,1536]{2,1,0:T(8,128)(2,1)}, u32[]{:S(2)}, u32[]{:S(2)}) collective-permute-start(bf16[16,64,1536]{2,1,0:T(8,128)(2,1)S(1)} %get-tuple-element.47), channel_id=1, source_target_pairs={{0,2},{2,0},{1,3},{3,1},{4,6},{6,4},{5,7},{7,5},{8,10},{10,8},{9,1... | collective-permute-start | bytes 9437192 | tf_op jit(solution)/shard_map/ppermute | solution.py:382
  280.5 1.3 copy-start.3
  354.7 53.4 %all-to-all-start.2 = ((bf16[8,256,512]{2,1,0:T(8,128)(2,1)}), bf16[8,256,512]{2,1,0:T(8,128)(2,1)}, u32[]{:S(2)}, u32[]{:S(2)}) async-start(bf16[8,256,512]{2,1,0:T(8,128)(2,1)} %copy-done.3), calls=%async_computation.2 | async-start | bytes 4194304 | tf_op jit(solution)/shard_map/all_to_all | solution.py:363
  369.6 1.4 copy-start.9
  371.0 69.0 %collective-permute-start.7 = (bf16[16,64,1024]{2,1,0:T(8,128)(2,1)}, bf16[16,64,1024]{2,1,0:T(8,128)(2,1)}, u32[]{:S(2)}, u32[]{:S(2)}) collective-permute-start(bf16[16,64,1024]{2,1,0:T(8,128)(2,1)} %get-tuple-element.66), channel_id=1, source_target_pairs={{0,2},{2,0},{1,3},{3,1},{4,6},{6,4},{5,7},{7,5},{8,10},{10,8},{9,1... | collective-permute-start | bytes 6291464 | tf_op jit(solution)/shard_map/ppermute | solution.py:382
  412.8 7.7 %collective-permute-start.2 = (f32[128,128]{1,0:T(8,128)S(1)}, f32[128,128]{1,0:T(8,128)S(1)}, u32[]{:S(2)}, u32[]{:S(2)}) collective-permute-start(f32[128,128]{1,0:T(8,128)S(1)} %slice_bitcast_fusion), channel_id=1, source_target_pairs={{0,2},{2,0},{1,3},{3,1},{4,6},{6,4},{5,7},{7,5},{8,10},{10,8},{9,1... | collective-permute-start | bytes 196616 | tf_op jit(solution)/shard_map/ppermute | solution.py:379
  420.5 30.7 %collective-permute-start.6 = (bf16[16,64,512]{2,1,0:T(8,128)(2,1)}, bf16[16,64,512]{2,1,0:T(8,128)(2,1)S(1)}, u32[]{:S(2)}, u32[]{:S(2)}) collective-permute-start(bf16[16,64,512]{2,1,0:T(8,128)(2,1)} %get-tuple-element.60), channel_id=1, source_target_pairs={{0,2},{2,0},{1,3},{3,1},{4,6},{6,4},{5,7},{7,5},{8,10},{10,8},{9,1... | collective-permute-start | bytes 3145736 | tf_op jit(solution)/shard_map/ppermute | solution.py:382
  422.0 1.3 collective-permute-start.3
  423.3 4.3 collective-permute-start.4
  427.7 5.4 %collective-permute-start.5 = (f32[128,128]{1,0:T(8,128)S(1)}, f32[128,128]{1,0:T(8,128)S(1)}, u32[]{:S(2)}, u32[]{:S(2)}) collective-permute-start(f32[128,128]{1,0:T(8,128)S(1)} %add.73), channel_id=1, source_target_pairs={{0,8},{1,9},{4,12},{5,13},{8,0},{9,1},{12,4},{13,5},{2,10},{3,11},... | collective-permute-start | bytes 196616 | tf_op jit(solution)/shard_map/ppermute | solution.py:324
  439.9 1.6 copy-start.6
  441.5 1.6 copy-start.8
  (2 other events, 1.5 us)

commit v4 on v3

--- a/solution.py
+++ b/solution.py
@@ -15,6 +15,7 @@
 SUBLANES = 8
 SHORT = pl.CostEstimate(flops=1, bytes_accessed=1, transcendentals=0)
 PREPARE_ROWS = 64
+UNROLL_MODES = 2
 PREPARE_PIECES = 8
 AHEAD = 2
 GROUP_ROWS = 2 * SUBLANES
@@ -42,9 +43,10 @@
     points = units * LANES
     for number, source in enumerate(sources):
         piece, unit = divmod(number, units)
+        by_plane = jnp.transpose(source[...], (1, 0, 2))
         for plane in range(source.shape[1]):
             first = plane * points + unit * LANES
-            target[piece, :, first : first + LANES] = source[:, plane, :]
+            target[piece, :, first : first + LANES] = by_plane[plane]
 
 
 def prepare(ticket, series, offset, points, count):
@@ -75,7 +77,7 @@
                 lambda part, step, ticket_ref: (part, step, 0),
             ),
         ),
-        out_shape=jax.ShapeDtypeStruct((count, snap_rows, slab_rows * points), series.dtype),
+        out_shape=pltpu.HBM((count, snap_rows, slab_rows * points), series.dtype),
         compiler_params=pltpu.CompilerParams(vmem_limit_bytes=40 * MIB),
         cost_estimate=SHORT,
         name="prepare",
@@ -84,21 +86,46 @@
 
 def spectra_kernel(ticket_ref, window_start, history, basis, total_in, *refs, members, unroll):
     del ticket_ref
-    coefs = refs[:members]
-    total_out = refs[members]
+    coefs_out = refs[:members]
+    total_out, held, *coefs, in_sems, out_sems = refs[members:]
     rows = coefs[0].shape[1]
     pairs = basis.shape[0]
     width = history.shape[1]
+    parts = history.shape[0] // NFFT
+
+    def arrival(part):
+        rows_of_part = pl.ds(part * NFFT, NFFT)
+        return pltpu.make_async_copy(
+            history.at[rows_of_part], held.at[rows_of_part], in_sems.at[part]
+        )
+
+    def departure(member, pair):
+        blocks_of_pair = pl.ds(2 * pair, 2)
+        return pltpu.make_async_copy(
+            coefs[member].at[blocks_of_pair],
+            coefs_out[member].at[blocks_of_pair],
+            out_sems.at[member, pair],
+        )
+
+    for part in range(parts):
+        arrival(part).start()
+    for part in range(min(2, parts)):
+        arrival(part).wait()
 
     def transform(pair, carry):
+        @pl.when(pair + 2 < parts)
+        def _():
+            arrival(pair + 2).wait()
+
         start = pl.multiple_of(window_start[pair], 16)
-        segment = history[pl.ds(start, SPAN), :]
+        segment = held[pl.ds(start, SPAN), :]
         both = jnp.dot(basis[pair], segment, preferred_element_type=jnp.float32)
         both = both.astype(jnp.bfloat16)
-        for half in range(2):
-            for member in range(members):
+        for member in reversed(range(members)):
+            for half in range(2):
                 first = (half * members + member) * rows
                 coefs[member][2 * pair + half] = both[first : first + rows]
+            departure(member, pair).start()
         return carry
 
     lax.fori_loop(0, pairs, transform, 0, unroll=unroll)
@@ -133,27 +160,38 @@
             -pltpu.roll(packed[1], 8, 1),
         )
         total_out[member] = total_in[member] + (packed[0] + swapped)
+    for member in range(members):
+        for pair in range(pairs):
+            departure(member, pair).wait()
 
 
 def spectra(ticket, window_start, history, basis, total, members, unroll):
-    width = history.shape[1]
-    blocks = 2 * basis.shape[0]
+    frames, width = history.shape
+    pairs = basis.shape[0]
     rows = basis.shape[1] // 2 // members
     smem = pl.BlockSpec(memory_space=pltpu.SMEM)
     vmem = pl.BlockSpec(memory_space=pltpu.VMEM)
-    outs = [jax.ShapeDtypeStruct((blocks, rows, width), jnp.bfloat16)] * members
+    hbm = pl.BlockSpec(memory_space=pltpu.HBM)
+    shape = (2 * pairs, rows, width)
     return pl.pallas_call(
         functools.partial(spectra_kernel, members=members, unroll=unroll),
-        out_shape=outs + [jax.ShapeDtypeStruct(total.shape, jnp.float32)],
-        in_specs=[smem, smem, vmem, vmem, vmem],
-        out_specs=[vmem] * (members + 1),
+        out_shape=[pltpu.HBM(shape, jnp.bfloat16)] * members
+        + [jax.ShapeDtypeStruct(total.shape, jnp.float32)],
+        in_specs=[smem, smem, hbm, vmem, vmem],
+        out_specs=[hbm] * members + [vmem],
+        scratch_shapes=[pltpu.VMEM((frames, width), history.dtype)]
+        + [pltpu.VMEM(shape, jnp.bfloat16)] * members
+        + [
+            pltpu.SemaphoreType.DMA((frames // NFFT,)),
+            pltpu.SemaphoreType.DMA((members, pairs)),
+        ],
         compiler_params=pltpu.CompilerParams(vmem_limit_bytes=40 * MIB),
         cost_estimate=SHORT,
         name="spectra",
     )(ticket, window_start, history, basis, total)
 
 
-def power_kernel(total, mix, scale, spectrum, *, blocks, norm_scale):
+def leading_vectors(total, mix, scale, spectrum, blocks, norm_scale):
     padded = total.shape[0] // SUBLANES
     cross = total[...].reshape(padded, SUBLANES, LANES) * norm_scale
     shape = (SUBLANES, LANES)
@@ -212,27 +250,16 @@
         spectrum[group] = spread(value, group)
 
 
-def leading_vectors(total, groups, blocks, norm_scale):
-    vmem = pl.BlockSpec(memory_space=pltpu.VMEM)
-    return pl.pallas_call(
-        functools.partial(power_kernel, blocks=blocks, norm_scale=norm_scale),
-        out_shape=[
-            jax.ShapeDtypeStruct((groups, GROUP_ROWS, 2 * LANES), jnp.bfloat16),
-            jax.ShapeDtypeStruct((groups, SUBLANES, LANES), jnp.float32),
-            jax.ShapeDtypeStruct((groups, SUBLANES, LANES), jnp.float32),
-        ],
-        in_specs=[vmem],
-        out_specs=[vmem] * 3,
-        name="power",
-    )(total)
-
-
-def modes_kernel(member_ref, mix, scale, *refs, chunks, members, offset):
-    coefs = refs[: chunks * members]
-    out = refs[chunks * members + (1 if offset else 0)]
-    scratch = refs[-2 * chunks - 2 :]
-    buffers, results = scratch[:chunks], scratch[chunks : 2 * chunks]
-    sems, out_sems = scratch[2 * chunks :]
+def modes_kernel(member_ref, *refs, chunks, members, offset, vectors):
+    taken = 1 if vectors else 2
+    coefs = refs[taken : taken + chunks * members]
+    out, *rest = refs[taken + chunks * members + (1 if offset else 0) :]
+    if vectors:
+        mix, scale, spectrum, *rest = rest
+    else:
+        mix, scale = refs[:2]
+    buffers, results = rest[:chunks], rest[chunks : 2 * chunks]
+    sems, out_sems = rest[2 * chunks :]
     member = member_ref[0]
     copies = []
     for chunk in range(chunks):
@@ -243,6 +270,8 @@
             )
             copy.start()
             copies.append(copy)
+    if vectors:
+        leading_vectors(refs[0], mix, scale, spectrum, **vectors)
     planes = out.shape[2] // members
     out_copies = []
     done = offset
@@ -268,7 +297,7 @@
                         results[chunk][e, target, slot * planes + plane, :] = part * factor
             return carry
 
-        lax.fori_loop(0, mix.shape[0], one_group, 0)
+        lax.fori_loop(0, mix.shape[0], one_group, 0, unroll=UNROLL_MODES)
         copy = pltpu.make_async_copy(
             results[chunk], out.at[:, :, :, pl.ds(done, points)], out_sems.at[chunk]
         )
@@ -279,34 +308,38 @@
         copy.wait()
 
 
-def project(member, mix, scale, coefs, members, planes, points, offset, before):
+def project(member, total_or_vectors, coefs, members, planes, shape, offset, before, vectors):
     chunks = len(coefs) // members
-    groups = mix.shape[0]
+    groups = shape[1] // SUBLANES
     vmem = pl.BlockSpec(memory_space=pltpu.VMEM)
-    hbm = pl.BlockSpec(memory_space=pl.ANY)
+    hbm = pl.BlockSpec(memory_space=pltpu.HBM)
     extra = [] if before is None else [before]
     sizes = [part.shape[2] // planes for part in coefs[::members]]
+    found = [
+        jax.ShapeDtypeStruct((groups, GROUP_ROWS, 2 * LANES), jnp.bfloat16),
+        jax.ShapeDtypeStruct((groups, SUBLANES, LANES), jnp.float32),
+        jax.ShapeDtypeStruct((groups, SUBLANES, LANES), jnp.float32),
+    ]
+    found = found if vectors else []
     return pl.pallas_call(
-        functools.partial(modes_kernel, chunks=chunks, members=members, offset=offset),
-        out_shape=jax.ShapeDtypeStruct(
-            (2, groups * SUBLANES, members * planes, points), jnp.float32
+        functools.partial(
+            modes_kernel, chunks=chunks, members=members, offset=offset, vectors=vectors
         ),
-        in_specs=[pl.BlockSpec(memory_space=pltpu.SMEM), vmem, vmem]
+        out_shape=[pltpu.HBM(shape, jnp.float32)] + found,
+        in_specs=[pl.BlockSpec(memory_space=pltpu.SMEM)]
+        + [vmem] * len(total_or_vectors)
         + [hbm] * (len(coefs) + len(extra)),
-        out_specs=hbm,
-        input_output_aliases={3 + len(coefs): 0} if extra else {},
+        out_specs=[hbm] + [vmem] * len(found),
+        input_output_aliases={1 + len(total_or_vectors) + len(coefs): 0} if extra else {},
         scratch_shapes=[
             pltpu.VMEM((members,) + part.shape, jnp.bfloat16) for part in coefs[::members]
         ]
-        + [
-            pltpu.VMEM((2, groups * SUBLANES, members * planes, size), jnp.float32)
-            for size in sizes
-        ]
+        + [pltpu.VMEM(shape[:3] + (size,), jnp.float32) for size in sizes]
         + [pltpu.SemaphoreType.DMA((chunks, members)), pltpu.SemaphoreType.DMA((chunks,))],
         compiler_params=pltpu.CompilerParams(vmem_limit_bytes=48 * MIB),
         cost_estimate=SHORT,
         name="modes",
-    )(member, mix, scale, *coefs, *extra)
+    )(member, *total_or_vectors, *coefs, *extra)
 
 
 def chunk_sizes(width):
@@ -369,7 +402,7 @@
     for chunk in range(len(sizes)):
         last = chunk + 1 == len(sizes)
         *sent, total = spectra(
-            ticket, window_start, histories[chunk], basis, total, members, last
+            ticket, window_start, histories[chunk], basis, total, members, True if last else 2
         )
         if chunk + AHEAD < len(sizes):
             ticket, total = lax.optimization_barrier((ticket, total))
@@ -389,15 +422,18 @@
 
     groups = freq_index.shape[0] // members // SUBLANES
     norm_scale = 1.0 / (blocks * slab_rows * members * plane)
-    mix, scale, spectrum = leading_vectors(mine, groups, blocks, norm_scale)
-    modes = None
-    for chunk_range in (range(len(sizes) - 1), range(len(sizes) - 1, len(sizes))):
-        if len(chunk_range):
-            parts = [part for chunk in chunk_range for part in coefs[chunk]]
-            offset = offsets[chunk_range[0]]
-            modes = project(
-                member.reshape(1), mix, scale, parts, members, slab_rows, width, offset, modes
-            )
+    shape = (2, groups * SUBLANES, members * slab_rows, width)
+    early = [part for chunk in coefs[: max(1, len(sizes) - 1)] for part in chunk]
+    late = [part for chunk in coefs[max(1, len(sizes) - 1) :] for part in chunk]
+    place = member.reshape(1)
+    vectors = {"blocks": blocks, "norm_scale": norm_scale}
+    modes, mix, scale, spectrum = project(
+        place, [mine], early, members, slab_rows, shape, 0, None, vectors
+    )
+    if late:
+        (modes,) = project(
+            place, [mix, scale], late, members, slab_rows, shape, offsets[-1], modes, None
+        )
     return (modes, spectrum[:, :, 0].reshape(-1))
 
 

time: 454 us -> 439 us (0.967)
  waiting for transfers between devices: 300 us -> 328 us
  Pallas kernels: 86.6 us -> 63.1 us
  local copies, waits for them, and re-layouts: 21.1 us -> 3.66 us
    all_to_all x4, waiting for transfers between devices: 190 us -> 207 us  [exchange(): lax.all_to_all(parts, line, split_axis=0, concat_axis=0, tiled=True)]
    pallas_call x4, Pallas kernels: 37.7 us -> 20.4 us  [prepare(): pl.pallas_call(functools.partial(prepare_kernel, units=units), grid_spec=...]
    unnamed x28 -> x12, local copies, waits for them, and re-layouts: 18.1 us -> 1.41 us
    ppermute x4, waiting for transfers between devices: 97.2 us -> 108 us  [shards(): sent[turn] = lax.ppermute(sent[turn], 'freq', rings[turn])]
    pallas_call x1 -> x0, Pallas kernels: 4.85 us -> none  [leading_vectors(): pl.pallas_call(functools.partial(power_kernel, blocks=blocks, norm_scale=...]
  transfers between devices with their start and end apart: 12 -> 12, of which waited for: 10 -> 11; matrix products, arithmetic and copies ran while one was open for 3% -> 3% of each run, Pallas kernels for 17% -> 13%
where the time goes in v4:
time: 439 us; the launch traced here: 437 us
  waiting for transfers between devices  328 us (75%)
  Pallas kernels  63.1 us (14%)
  starting transfers between devices  30 us (7%)
  other arithmetic  11.3 us (3%)
    all_to_all x4, waiting for transfers between devices, exchange(): lax.all_to_all(parts, line, split_axis=0, concat_axis=0, tiled=True)  207 us
    ppermute x4, waiting for transfers between devices, shards(): sent[turn] = lax.ppermute(sent[turn], 'freq', rings[turn])  108 us
    pallas_call x4, Pallas kernels, spectra(): pl.pallas_call(functools.partial(spectra_kernel, members=members, unroll=...  32.7 us
    pallas_call x4, Pallas kernels, prepare(): pl.pallas_call(functools.partial(prepare_kernel, units=units), grid_spec=...  20.4 us
    all_to_all x4, starting transfers between devices, exchange(): lax.all_to_all(parts, line, split_axis=0, concat_axis=0, tiled=True)  20.2 us
    pallas_call x2, Pallas kernels, project(): pl.pallas_call(functools.partial(modes_kernel, chunks=chunks, members=mem...  10 us
    ppermute x3, waiting for transfers between devices, butterfly_sum(): value = value + lax.ppermute(value, axes, pairs)  9.41 us
  transfers between devices with their start and end apart: 12, of which 11 were waited for; matrix products, arithmetic and copies ran while one was open for 3% of the time, Pallas kernels for 13%

profile of v4, /device:TPU:0, one launch (start us, length us, event | category | flops | bytes accessed | tf_op | source)
XLA Modules:
  0.0 437.3 jit_solution(2082401034095387361)
XLA Ops:
  0.6 5.1 %prepare.4 = bf16[8,256,1024]{2,1,0:T(8,128)(2,1)} custom-call(s32[1]{0:T(128)} %constant.32.clone.1.ticket_ref, bf16[256,4,8192]{2,1,0:T(4,128)(2,1)} %refs_7_.7, bf16[256,4,8192]{2,1,0:T(4,128)(2,1)} %refs_7_.7, bf16[256,4,8192]{2,1,0:T(4,128)(2,1)} %refs_7_.7, bf16[256,4,8192]{2,1,0:T(4,128)(2,1)} %refs_7_.7, bf16[256,4,8192]{2,1,0:T(4,128)(2,1)} %refs_7_.7, ...), custom_call_target="tpu_custom_call" | custom-call | flops 1 | bytes 1 | tf_op jit(solution)/shard_map/prepare/pallas_call | solution.py:65
  5.7 6.3 %all-to-all-start = ((bf16[8,256,1024]{2,1,0:T(8,128)(2,1)}), bf16[8,256,1024]{2,1,0:T(8,128)(2,1)}, u32[]{:S(2)}, u32[]{:S(2)}) async-start(bf16[8,256,1024]{2,1,0:T(8,128)(2,1)} %prepare.4), calls=%async_computation | async-start | bytes 8388608 | tf_op jit(solution)/shard_map/all_to_all | solution.py:396
  12.0 6.4 %prepare.5 = bf16[8,256,1536]{2,1,0:T(8,128)(2,1)} custom-call(s32[1]{0:T(128)} %constant.32.clone.1.ticket_ref, bf16[256,4,8192]{2,1,0:T(4,128)(2,1)} %refs_7_.7, bf16[256,4,8192]{2,1,0:T(4,128)(2,1)} %refs_7_.7, bf16[256,4,8192]{2,1,0:T(4,128)(2,1)} %refs_7_.7, bf16[256,4,8192]{2,1,0:T(4,128)(2,1)} %refs_7_.7, bf16[256,4,8192]{2,1,0:T(4,128)(2,1)} %refs_7_.7, ...), custom_call_target="tpu_custom_call" | custom-call | flops 1 | bytes 1 | tf_op jit(solution)/shard_map/prepare/pallas_call | solution.py:65
  18.4 87.7 %all-to-all-done = bf16[8,256,1024]{2,1,0:T(8,128)(2,1)} async-done(((bf16[8,256,1024]{2,1,0:T(8,128)(2,1)}), bf16[8,256,1024]{2,1,0:T(8,128)(2,1)}, u32[]{:S(2)}, u32[]{:S(2)}) %all-to-all-start) | async-done | bytes 4194336 | tf_op jit(solution)/shard_map/all_to_all | solution.py:396
  106.2 4.8 %all-to-all-start.1 = ((bf16[8,256,1536]{2,1,0:T(8,128)(2,1)}), bf16[8,256,1536]{2,1,0:T(8,128)(2,1)}, u32[]{:S(2)}, u32[]{:S(2)}) async-start(bf16[8,256,1536]{2,1,0:T(8,128)(2,1)} %prepare.5), calls=%async_computation.1 | async-start | bytes 12582912 | tf_op jit(solution)/shard_map/all_to_all | solution.py:396
  115.6 8.2 %fusion.4 = (f32[16,8,1,8,512]{4,3,2,1,0:T(8,128)S(1)}, f32[16,8,1,8,512]{4,3,2,1,0:T(8,128)S(1)}) fusion(s32[16,512]{1,0:T(8,128)S(1)} %fusion.5, s32[8,8]{1,0:T(8,128)S(1)} %mul.86), kind=kLoop, calls=%fused_computation.12 | loop fusion | flops 7864320 | bytes 4227328 | tf_op jit(solution)/shard_map/cos | solution.py:36
  124.5 8.4 %spectra.4 = (bf16[16,64,1024]{2,1,0:T(8,128)(2,1)}, bf16[16,64,1024]{2,1,0:T(8,128)(2,1)}, f32[2,128,128]{2,1,0:T(8,128)S(1)}) custom-call(s32[1]{0:T(128)} %constant.32.clone.1.ticket_ref, s32[8]{0:T(128)S(1)} %multiply_minimum_fusion.window_start, bf16[2048,1024]{1,0:T(8,128)(2,1)} %bitcast.1.history, bf16[8,256,512]{2,1,0:T(8,128)(2,1)S(1)} %bitcast.12, ...), custom_call_target="tpu_custom_call" | custom-call | flops 1 | bytes 1 | tf_op jit(solution)/shard_map/spectra/pallas_call | solution.py:176
  132.9 1.6 collective-permute-start.1
  134.5 5.1 %prepare.6 = bf16[8,256,1024]{2,1,0:T(8,128)(2,1)} custom-call(s32[1]{0:T(128)} %constant.32.clone.1.ticket_ref, bf16[256,4,8192]{2,1,0:T(4,128)(2,1)} %refs_7_.7, bf16[256,4,8192]{2,1,0:T(4,128)(2,1)} %refs_7_.7, bf16[256,4,8192]{2,1,0:T(4,128)(2,1)} %refs_7_.7, bf16[256,4,8192]{2,1,0:T(4,128)(2,1)} %refs_7_.7, bf16[256,4,8192]{2,1,0:T(4,128)(2,1)} %refs_7_.7, ...), custom_call_target="tpu_custom_call" | custom-call | flops 1 | bytes 1 | tf_op jit(solution)/shard_map/prepare/pallas_call | solution.py:65
  139.6 41.5 %collective-permute-done.1.refs_2_ = bf16[16,64,1024]{2,1,0:T(8,128)(2,1)S(1)} collective-permute-done((bf16[16,64,1024]{2,1,0:T(8,128)(2,1)}, bf16[16,64,1024]{2,1,0:T(8,128)(2,1)S(1)}, u32[]{:S(2)}, u32[]{:S(2)}) %collective-permute-start.1) | collective-permute-done | bytes 2097184 | tf_op jit(solution)/shard_map/ppermute | solution.py:415
  182.5 67.4 %all-to-all-done.1 = bf16[8,256,1536]{2,1,0:T(8,128)(2,1)} async-done(((bf16[8,256,1536]{2,1,0:T(8,128)(2,1)}), bf16[8,256,1536]{2,1,0:T(8,128)(2,1)}, u32[]{:S(2)}, u32[]{:S(2)}) %all-to-all-start.1) | async-done | bytes 6291488 | tf_op jit(solution)/shard_map/all_to_all | solution.py:396
  249.9 4.7 %all-to-all-start.3 = ((bf16[8,256,1024]{2,1,0:T(8,128)(2,1)}), bf16[8,256,1024]{2,1,0:T(8,128)(2,1)}, u32[]{:S(2)}, u32[]{:S(2)}) async-start(bf16[8,256,1024]{2,1,0:T(8,128)(2,1)} %prepare.6), calls=%async_computation.3 | async-start | bytes 8388608 | tf_op jit(solution)/shard_map/all_to_all | solution.py:396
  254.6 10.2 %spectra.5 = (bf16[16,64,1536]{2,1,0:T(8,128)(2,1)}, bf16[16,64,1536]{2,1,0:T(8,128)(2,1)}, f32[2,128,128]{2,1,0:T(8,128)S(1)}) custom-call(s32[1]{0:T(128)} %constant.32.clone.1.ticket_ref, s32[8]{0:T(128)S(1)} %multiply_minimum_fusion.window_start, bf16[2048,1536]{1,0:T(8,128)(2,1)} %bitcast.4.history, bf16[8,256,512]{2,1,0:T(8,128)(2,1)S(1)} %bitcast.13, ...), custom_call_target="tpu_custom_call" | custom-call | flops 1 | bytes 1 | tf_op jit(solution)/shard_map/spectra/pallas_call | solution.py:176
  266.4 3.9 prepare.7
  270.3 65.1 %collective-permute-done.refs_4_ = bf16[16,64,1536]{2,1,0:T(8,128)(2,1)} collective-permute-done((bf16[16,64,1536]{2,1,0:T(8,128)(2,1)}, bf16[16,64,1536]{2,1,0:T(8,128)(2,1)}, u32[]{:S(2)}, u32[]{:S(2)}) %collective-permute-start) | collective-permute-done | bytes 3145760 | tf_op jit(solution)/shard_map/ppermute | solution.py:415
  335.4 13.0 %all-to-all-done.3 = bf16[8,256,1024]{2,1,0:T(8,128)(2,1)} async-done(((bf16[8,256,1024]{2,1,0:T(8,128)(2,1)}), bf16[8,256,1024]{2,1,0:T(8,128)(2,1)}, u32[]{:S(2)}, u32[]{:S(2)}) %all-to-all-start.3) | async-done | bytes 4194336 | tf_op jit(solution)/shard_map/all_to_all | solution.py:396
  348.4 4.4 all-to-all-start.2
  352.8 8.4 %spectra.6 = (bf16[16,64,1024]{2,1,0:T(8,128)(2,1)}, bf16[16,64,1024]{2,1,0:T(8,128)(2,1)}, f32[2,128,128]{2,1,0:T(8,128)S(1)}) custom-call(s32[1]{0:T(128)} %constant.32.clone.1.ticket_ref, s32[8]{0:T(128)S(1)} %multiply_minimum_fusion.window_start, bf16[2048,1024]{1,0:T(8,128)(2,1)} %bitcast.6.history, bf16[8,256,512]{2,1,0:T(8,128)(2,1)S(1)} %bitcast.14, ...), custom_call_target="tpu_custom_call" | custom-call | flops 1 | bytes 1 | tf_op jit(solution)/shard_map/spectra/pallas_call | solution.py:176
  362.8 39.1 %all-to-all-done.2 = bf16[8,256,512]{2,1,0:T(8,128)(2,1)} async-done(((bf16[8,256,512]{2,1,0:T(8,128)(2,1)}), bf16[8,256,512]{2,1,0:T(8,128)(2,1)}, u32[]{:S(2)}, u32[]{:S(2)}) %all-to-all-start.2) | async-done | bytes 2097184 | tf_op jit(solution)/shard_map/all_to_all | solution.py:396
  401.9 5.7 %spectra.7 = (bf16[16,64,512]{2,1,0:T(8,128)(2,1)}, bf16[16,64,512]{2,1,0:T(8,128)(2,1)}, f32[2,128,128]{2,1,0:T(8,128)S(1)}) custom-call(s32[1]{0:T(128)} %constant.32.clone.1.ticket_ref, s32[8]{0:T(128)S(1)} %multiply_minimum_fusion.window_start, bf16[2048,512]{1,0:T(8,128)(2,1)} %bitcast.5.history, bf16[8,256,512]{2,1,0:T(8,128)(2,1)S(1)} %bitcast.15, ...), custom_call_target="tpu_custom_call" | custom-call | flops 1 | bytes 1 | tf_op jit(solution)/shard_map/spectra/pallas_call | solution.py:176
  409.2 2.8 collective-permute-done.2
  415.4 3.8 collective-permute-done.4
  420.6 4.4 %collective-permute-done.5 = f32[128,128]{1,0:T(8,128)S(1)} collective-permute-done((f32[128,128]{1,0:T(8,128)S(1)}, f32[128,128]{1,0:T(8,128)S(1)}, u32[]{:S(2)}, u32[]{:S(2)}) %collective-permute-start.5) | collective-permute-done | bytes 65568 | tf_op jit(solution)/shard_map/ppermute | solution.py:357
  425.1 8.6 %modes.2 = (f32[2,32,8,1024]{3,2,1,0:T(8,128)}, bf16[4,16,256]{2,1,0:T(8,128)(2,1)S(1)}, f32[4,8,128]{2,1,0:T(8,128)S(1)}, f32[4,8,128]{2,1,0:T(8,128)S(1)}) custom-call(s32[1]{0:T(128)} %bitcast.member_ref, f32[128,128]{1,0:T(8,128)S(1)} %add.74.refs_0_, bf16[16,64,1024]{2,1,0:T(8,128)(2,1)S(1)} %copy-done, bf16[16,64,1024]{2,1,0:T(8,128)(2,1)S(1)} %copy-done.2, ...), custom_call_target="tpu_custom_call" | custom-call | flops 1 | bytes 1 | tf_op jit(solution)/shard_map/modes/pallas_call | solution.py:324
  (48 shorter events, 19.0 us)
Async XLA Ops:
  5.7 100.5 %all-to-all-start = ((bf16[8,256,1024]{2,1,0:T(8,128)(2,1)}), bf16[8,256,1024]{2,1,0:T(8,128)(2,1)}, u32[]{:S(2)}, u32[]{:S(2)}) async-start(bf16[8,256,1024]{2,1,0:T(8,128)(2,1)} %prepare.4), calls=%async_computation | async-start | bytes 8388608 | tf_op jit(solution)/shard_map/all_to_all | solution.py:396
  18.4 93.9 %copy-start.4 = (s32[15]{0:T(128)S(1)}, s32[15]{0:T(128)}, u32[]{:S(2)}) copy-start(s32[15]{0:T(128)} %param.4) | copy-start | bytes 184
  18.4 95.3 %copy-start.5 = (s32[64]{0:T(128)S(1)}, s32[64]{0:T(128)}, u32[]{:S(2)}) copy-start(s32[64]{0:T(128)} %param.5) | copy-start | bytes 772
  106.2 143.7 %all-to-all-start.1 = ((bf16[8,256,1536]{2,1,0:T(8,128)(2,1)}), bf16[8,256,1536]{2,1,0:T(8,128)(2,1)}, u32[]{:S(2)}, u32[]{:S(2)}) async-start(bf16[8,256,1536]{2,1,0:T(8,128)(2,1)} %prepare.5), calls=%async_computation.1 | async-start | bytes 12582912 | tf_op jit(solution)/shard_map/all_to_all | solution.py:396
  132.9 48.2 %collective-permute-start.1 = (bf16[16,64,1024]{2,1,0:T(8,128)(2,1)}, bf16[16,64,1024]{2,1,0:T(8,128)(2,1)S(1)}, u32[]{:S(2)}, u32[]{:S(2)}) collective-permute-start(bf16[16,64,1024]{2,1,0:T(8,128)(2,1)} %get-tuple-element.51), channel_id=1, source_target_pairs={{0,2},{2,0},{1,3},{3,1},{4,6},{6,4},{5,7},{7,5},{8,10},{10,8},{9,1... | collective-permute-start | bytes 6291464 | tf_op jit(solution)/shard_map/ppermute | solution.py:415
  181.1 1.4 copy-start.1
  249.9 98.6 %all-to-all-start.3 = ((bf16[8,256,1024]{2,1,0:T(8,128)(2,1)}), bf16[8,256,1024]{2,1,0:T(8,128)(2,1)}, u32[]{:S(2)}, u32[]{:S(2)}) async-start(bf16[8,256,1024]{2,1,0:T(8,128)(2,1)} %prepare.6), calls=%async_computation.3 | async-start | bytes 8388608 | tf_op jit(solution)/shard_map/all_to_all | solution.py:396
  264.8 70.6 %collective-permute-start = (bf16[16,64,1536]{2,1,0:T(8,128)(2,1)}, bf16[16,64,1536]{2,1,0:T(8,128)(2,1)}, u32[]{:S(2)}, u32[]{:S(2)}) collective-permute-start(bf16[16,64,1536]{2,1,0:T(8,128)(2,1)} %get-tuple-element.48), channel_id=1, source_target_pairs={{0,2},{2,0},{1,3},{3,1},{4,6},{6,4},{5,7},{7,5},{8,10},{10,8},{9,1... | collective-permute-start | bytes 9437192 | tf_op jit(solution)/shard_map/ppermute | solution.py:415
  348.4 53.4 %all-to-all-start.2 = ((bf16[8,256,512]{2,1,0:T(8,128)(2,1)}), bf16[8,256,512]{2,1,0:T(8,128)(2,1)}, u32[]{:S(2)}, u32[]{:S(2)}) async-start(bf16[8,256,512]{2,1,0:T(8,128)(2,1)} %prepare.7), calls=%async_computation.2 | async-start | bytes 4194304 | tf_op jit(solution)/shard_map/all_to_all | solution.py:396
  361.2 63.8 %collective-permute-start.6 = (bf16[16,64,1024]{2,1,0:T(8,128)(2,1)}, bf16[16,64,1024]{2,1,0:T(8,128)(2,1)}, u32[]{:S(2)}, u32[]{:S(2)}) collective-permute-start(bf16[16,64,1024]{2,1,0:T(8,128)(2,1)} %get-tuple-element.63), channel_id=1, source_target_pairs={{0,2},{2,0},{1,3},{3,1},{4,6},{6,4},{5,7},{7,5},{8,10},{10,8},{9,1... | collective-permute-start | bytes 6291464 | tf_op jit(solution)/shard_map/ppermute | solution.py:415
  401.9 23.2 %copy-start = (bf16[16,64,1024]{2,1,0:T(8,128)(2,1)S(1)}, bf16[16,64,1024]{2,1,0:T(8,128)(2,1)}, u32[]{:S(2)}) copy-start(bf16[16,64,1024]{2,1,0:T(8,128)(2,1)} %get-tuple-element.58.refs_1_) | copy-start | bytes 6291460
  401.9 23.2 %copy-start.2 = (bf16[16,64,1024]{2,1,0:T(8,128)(2,1)S(1)}, bf16[16,64,1024]{2,1,0:T(8,128)(2,1)}, u32[]{:S(2)}) copy-start(bf16[16,64,1024]{2,1,0:T(8,128)(2,1)} %copy-done.1) | copy-start | bytes 6291460
  407.6 4.3 collective-permute-start.2
  412.0 23.8 %collective-permute-start.7 = (bf16[16,64,512]{2,1,0:T(8,128)(2,1)}, bf16[16,64,512]{2,1,0:T(8,128)(2,1)S(1)}, u32[]{:S(2)}, u32[]{:S(2)}) collective-permute-start(bf16[16,64,512]{2,1,0:T(8,128)(2,1)} %get-tuple-element.67), channel_id=1, source_target_pairs={{0,2},{2,0},{1,3},{3,1},{4,6},{6,4},{5,7},{7,5},{8,10},{10,8},{9,1... | collective-permute-start | bytes 3145736 | tf_op jit(solution)/shard_map/ppermute | solution.py:415
  413.5 1.3 collective-permute-start.3
  414.8 4.3 collective-permute-start.4
  419.1 5.9 %collective-permute-start.5 = (f32[128,128]{1,0:T(8,128)S(1)}, f32[128,128]{1,0:T(8,128)S(1)}, u32[]{:S(2)}, u32[]{:S(2)}) collective-permute-start(f32[128,128]{1,0:T(8,128)S(1)} %add.73), channel_id=1, source_target_pairs={{0,8},{1,9},{4,12},{5,13},{8,0},{9,1},{12,4},{13,5},{2,10},{3,11},... | collective-permute-start | bytes 196616 | tf_op jit(solution)/shard_map/ppermute | solution.py:357
  425.0 10.7 %copy-start.3 = (bf16[16,64,512]{2,1,0:T(8,128)(2,1)S(1)}, bf16[16,64,512]{2,1,0:T(8,128)(2,1)}, u32[]{:S(2)}) copy-start(bf16[16,64,512]{2,1,0:T(8,128)(2,1)} %get-tuple-element.66.refs_2_) | copy-start | bytes 3145732

commit v5 on v4

--- a/solution.py
+++ b/solution.py
@@ -99,8 +99,8 @@
             history.at[rows_of_part], held.at[rows_of_part], in_sems.at[part]
         )
 
-    def departure(member, pair):
-        blocks_of_pair = pl.ds(2 * pair, 2)
+    def departure(member, pair, count=2):
+        blocks_of_pair = pl.ds(2 * pair, count)
         return pltpu.make_async_copy(
             coefs[member].at[blocks_of_pair],
             coefs_out[member].at[blocks_of_pair],
@@ -112,7 +112,7 @@
     for part in range(min(2, parts)):
         arrival(part).wait()
 
-    def transform(pair, carry):
+    def transform(pair, carry, kept):
         @pl.when(pair + 2 < parts)
         def _():
             arrival(pair + 2).wait()
@@ -125,10 +125,12 @@
             for half in range(2):
                 first = (half * members + member) * rows
                 coefs[member][2 * pair + half] = both[first : first + rows]
-            departure(member, pair).start()
+            departure(member, pair, kept).start()
         return carry
 
-    lax.fori_loop(0, pairs, transform, 0, unroll=unroll)
+    last_count = coefs_out[0].shape[0] - 2 * (pairs - 1)
+    lax.fori_loop(0, pairs - 1, functools.partial(transform, kept=2), 0, unroll=unroll)
+    transform(pairs - 1, 0, last_count)
     packed_rows = 2 * pairs * SUBLANES
     lane = lax.broadcasted_iota(jnp.int32, (packed_rows, LANES), 1)
     sub = lax.broadcasted_iota(jnp.int32, (packed_rows, LANES), 0) % SUBLANES
@@ -162,10 +164,10 @@
         total_out[member] = total_in[member] + (packed[0] + swapped)
     for member in range(members):
         for pair in range(pairs):
-            departure(member, pair).wait()
-
-
-def spectra(ticket, window_start, history, basis, total, members, unroll):
+            departure(member, pair, 2 if pair + 1 < pairs else last_count).wait()
+
+
+def spectra(ticket, window_start, history, basis, total, blocks, members, unroll):
     frames, width = history.shape
     pairs = basis.shape[0]
     rows = basis.shape[1] // 2 // members
@@ -175,7 +177,7 @@
     shape = (2 * pairs, rows, width)
     return pl.pallas_call(
         functools.partial(spectra_kernel, members=members, unroll=unroll),
-        out_shape=[pltpu.HBM(shape, jnp.bfloat16)] * members
+        out_shape=[pltpu.HBM((blocks,) + shape[1:], jnp.bfloat16)] * members
         + [jax.ShapeDtypeStruct(total.shape, jnp.float32)],
         in_specs=[smem, smem, hbm, vmem, vmem],
         out_specs=[hbm] * members + [vmem],
@@ -265,11 +267,16 @@
     for chunk in range(chunks):
         for turn in range(members):
             slot = lax.rem(member + members - turn, members)
+            source = coefs[chunk * members + turn]
             copy = pltpu.make_async_copy(
-                coefs[chunk * members + turn], buffers[chunk].at[slot], sems.at[chunk, turn]
+                source, buffers[chunk].at[slot, pl.ds(0, source.shape[0])], sems.at[chunk, turn]
             )
             copy.start()
             copies.append(copy)
+    blocks = coefs[0].shape[0]
+    for buffer in buffers:
+        if blocks < buffer.shape[1]:
+            buffer[:, blocks:] = jnp.zeros_like(buffer[:, blocks:])
     if vectors:
         leading_vectors(refs[0], mix, scale, spectrum, **vectors)
     planes = out.shape[2] // members
@@ -332,7 +339,8 @@
         out_specs=[hbm] + [vmem] * len(found),
         input_output_aliases={1 + len(total_or_vectors) + len(coefs): 0} if extra else {},
         scratch_shapes=[
-            pltpu.VMEM((members,) + part.shape, jnp.bfloat16) for part in coefs[::members]
+            pltpu.VMEM((members, (part.shape[0] + 1) // 2 * 2) + part.shape[1:], jnp.bfloat16)
+            for part in coefs[::members]
         ]
         + [pltpu.VMEM(shape[:3] + (size,), jnp.float32) for size in sizes]
         + [pltpu.SemaphoreType.DMA((chunks, members)), pltpu.SemaphoreType.DMA((chunks,))],
@@ -351,11 +359,18 @@
 
 
 def butterfly_sum(value, axes, count):
-    step = 1
+    def from_distance(distance):
+        return lax.ppermute(value, axes, [(i, i ^ distance) for i in range(count)])
+
+    value = value + from_distance(1) if count > 1 else value
+    step = 2
     while step < count:
-        pairs = [(i, i ^ step) for i in range(count)]
-        value = value + lax.ppermute(value, axes, pairs)
-        step *= 2
+        if 2 * step < count:
+            near, far, both = (from_distance(n * step) for n in (1, 2, 3))
+            value = (value + near) + (far + both)
+        else:
+            value = value + from_distance(step)
+        step *= 4
     return value
 
 
@@ -402,7 +417,14 @@
     for chunk in range(len(sizes)):
         last = chunk + 1 == len(sizes)
         *sent, total = spectra(
-            ticket, window_start, histories[chunk], basis, total, members, True if last else 2
+            ticket,
+            window_start,
+            histories[chunk],
+            basis,
+            total,
+            blocks,
+            members,
+            True if last else 2,
         )
         if chunk + AHEAD < len(sizes):
             ticket, total = lax.optimization_barrier((ticket, total))

time: 439 us -> 438 us (level)
  waiting for transfers between devices: 328 us -> 323 us
    ppermute x4, waiting for transfers between devices: 108 us -> 100 us  [shards(): sent[turn] = lax.ppermute(sent[turn], 'freq', rings[turn])]
    all_to_all x4, waiting for transfers between devices: 207 us -> 215 us  [exchange(): lax.all_to_all(parts, line, split_axis=0, concat_axis=0, tiled=True)]
    ppermute x3 -> x4, waiting for transfers between devices: 9.41 us -> 5.62 us  [from_distance(): return lax.ppermute(value, axes, [(i, i ^ distance) for i in range(count)])]
  transfers between devices with their start and end apart: 12 -> 13, of which waited for: 11 -> 11; matrix products, arithmetic and copies ran while one was open for 3% -> 3% of each run, Pallas kernels for 13% -> 13%
where the time goes in v5:
time: 438 us; the launch traced here: 436 us
  waiting for transfers between devices  323 us (74%)
  Pallas kernels  62.5 us (14%)
  starting transfers between devices  32.3 us (7%)
  other arithmetic  11.3 us (3%)
  local copies, waits for them, and re-layouts  5.16 us (1%)
    all_to_all x4, waiting for transfers between devices, exchange(): lax.all_to_all(parts, line, split_axis=0, concat_axis=0, tiled=True)  215 us
    ppermute x4, waiting for transfers between devices, shards(): sent[turn] = lax.ppermute(sent[turn], 'freq', rings[turn])  100 us
    pallas_call x4, Pallas kernels, spectra(): pl.pallas_call(functools.partial(spectra_kernel, members=members, unroll=...  32.3 us
    pallas_call x4, Pallas kernels, prepare(): pl.pallas_call(functools.partial(prepare_kernel, units=units), grid_spec=...  20.4 us
    all_to_all x4, starting transfers between devices, exchange(): lax.all_to_all(parts, line, split_axis=0, concat_axis=0, tiled=True)  20 us
    pallas_call x2, Pallas kernels, project(): pl.pallas_call(functools.partial(modes_kernel, chunks=chunks, members=mem...  9.76 us
  transfers between devices with their start and end apart: 13, of which 11 were waited for; matrix products, arithmetic and copies ran while one was open for 3% of the time, Pallas kernels for 13%

profile of v5, /device:TPU:0, one launch (start us, length us, event | category | flops | bytes accessed | tf_op | source)
XLA Modules:
  0.0 436.3 jit_solution(9601397638140978058)
XLA Ops:
  0.6 5.0 %prepare.4 = bf16[8,256,1024]{2,1,0:T(8,128)(2,1)} custom-call(s32[1]{0:T(128)} %constant.32.clone.1.ticket_ref, bf16[256,4,8192]{2,1,0:T(4,128)(2,1)} %refs_7_.7, bf16[256,4,8192]{2,1,0:T(4,128)(2,1)} %refs_7_.7, bf16[256,4,8192]{2,1,0:T(4,128)(2,1)} %refs_7_.7, bf16[256,4,8192]{2,1,0:T(4,128)(2,1)} %refs_7_.7, bf16[256,4,8192]{2,1,0:T(4,128)(2,1)} %refs_7_.7, ...), custom_call_target="tpu_custom_call" | custom-call | flops 1 | bytes 1 | tf_op jit(solution)/shard_map/prepare/pallas_call | solution.py:65
  5.7 6.3 %all-to-all-start = ((bf16[8,256,1024]{2,1,0:T(8,128)(2,1)}), bf16[8,256,1024]{2,1,0:T(8,128)(2,1)}, u32[]{:S(2)}, u32[]{:S(2)}) async-start(bf16[8,256,1024]{2,1,0:T(8,128)(2,1)} %prepare.4), calls=%async_computation | async-start | bytes 8388608 | tf_op jit(solution)/shard_map/all_to_all | solution.py:411
  12.0 6.4 %prepare.5 = bf16[8,256,1536]{2,1,0:T(8,128)(2,1)} custom-call(s32[1]{0:T(128)} %constant.32.clone.1.ticket_ref, bf16[256,4,8192]{2,1,0:T(4,128)(2,1)} %refs_7_.7, bf16[256,4,8192]{2,1,0:T(4,128)(2,1)} %refs_7_.7, bf16[256,4,8192]{2,1,0:T(4,128)(2,1)} %refs_7_.7, bf16[256,4,8192]{2,1,0:T(4,128)(2,1)} %refs_7_.7, bf16[256,4,8192]{2,1,0:T(4,128)(2,1)} %refs_7_.7, ...), custom_call_target="tpu_custom_call" | custom-call | flops 1 | bytes 1 | tf_op jit(solution)/shard_map/prepare/pallas_call | solution.py:65
  18.4 87.7 %all-to-all-done = bf16[8,256,1024]{2,1,0:T(8,128)(2,1)} async-done(((bf16[8,256,1024]{2,1,0:T(8,128)(2,1)}), bf16[8,256,1024]{2,1,0:T(8,128)(2,1)}, u32[]{:S(2)}, u32[]{:S(2)}) %all-to-all-start) | async-done | bytes 4194336 | tf_op jit(solution)/shard_map/all_to_all | solution.py:411
  106.1 4.7 %all-to-all-start.1 = ((bf16[8,256,1536]{2,1,0:T(8,128)(2,1)}), bf16[8,256,1536]{2,1,0:T(8,128)(2,1)}, u32[]{:S(2)}, u32[]{:S(2)}) async-start(bf16[8,256,1536]{2,1,0:T(8,128)(2,1)} %prepare.5), calls=%async_computation.1 | async-start | bytes 12582912 | tf_op jit(solution)/shard_map/all_to_all | solution.py:411
  115.6 8.2 %fusion.4 = (f32[16,8,1,8,512]{4,3,2,1,0:T(8,128)S(1)}, f32[16,8,1,8,512]{4,3,2,1,0:T(8,128)S(1)}) fusion(s32[16,512]{1,0:T(8,128)S(1)} %fusion.5, s32[8,8]{1,0:T(8,128)S(1)} %mul.86), kind=kLoop, calls=%fused_computation.12 | loop fusion | flops 7864320 | bytes 4227328 | tf_op jit(solution)/shard_map/cos | solution.py:36
  124.5 8.4 %spectra.4 = (bf16[15,64,1024]{2,1,0:T(8,128)(2,1)}, bf16[15,64,1024]{2,1,0:T(8,128)(2,1)}, f32[2,128,128]{2,1,0:T(8,128)S(1)}) custom-call(s32[1]{0:T(128)} %constant.32.clone.1.ticket_ref, s32[8]{0:T(128)S(1)} %multiply_minimum_fusion.window_start, bf16[2048,1024]{1,0:T(8,128)(2,1)} %bitcast.1.history, bf16[8,256,512]{2,1,0:T(8,128)(2,1)S(1)} %bitcast.12, ...), custom_call_target="tpu_custom_call" | custom-call | flops 1 | bytes 1 | tf_op jit(solution)/shard_map/spectra/pallas_call | solution.py:178
  134.5 5.1 %prepare.6 = bf16[8,256,1024]{2,1,0:T(8,128)(2,1)} custom-call(s32[1]{0:T(128)} %constant.32.clone.1.ticket_ref, bf16[256,4,8192]{2,1,0:T(4,128)(2,1)} %refs_7_.7, bf16[256,4,8192]{2,1,0:T(4,128)(2,1)} %refs_7_.7, bf16[256,4,8192]{2,1,0:T(4,128)(2,1)} %refs_7_.7, bf16[256,4,8192]{2,1,0:T(4,128)(2,1)} %refs_7_.7, bf16[256,4,8192]{2,1,0:T(4,128)(2,1)} %refs_7_.7, ...), custom_call_target="tpu_custom_call" | custom-call | flops 1 | bytes 1 | tf_op jit(solution)/shard_map/prepare/pallas_call | solution.py:65
  139.5 38.7 %collective-permute-done.1.refs_2_ = bf16[15,64,1024]{2,1,0:T(8,128)(2,1)S(1)} collective-permute-done((bf16[15,64,1024]{2,1,0:T(8,128)(2,1)}, bf16[15,64,1024]{2,1,0:T(8,128)(2,1)S(1)}, u32[]{:S(2)}, u32[]{:S(2)}) %collective-permute-start.1) | collective-permute-done | bytes 1966112 | tf_op jit(solution)/shard_map/ppermute | solution.py:437
  179.6 70.2 %all-to-all-done.1 = bf16[8,256,1536]{2,1,0:T(8,128)(2,1)} async-done(((bf16[8,256,1536]{2,1,0:T(8,128)(2,1)}), bf16[8,256,1536]{2,1,0:T(8,128)(2,1)}, u32[]{:S(2)}, u32[]{:S(2)}) %all-to-all-start.1) | async-done | bytes 6291488 | tf_op jit(solution)/shard_map/all_to_all | solution.py:411
  249.8 4.6 %all-to-all-start.3 = ((bf16[8,256,1024]{2,1,0:T(8,128)(2,1)}), bf16[8,256,1024]{2,1,0:T(8,128)(2,1)}, u32[]{:S(2)}, u32[]{:S(2)}) async-start(bf16[8,256,1024]{2,1,0:T(8,128)(2,1)} %prepare.6), calls=%async_computation.3 | async-start | bytes 8388608 | tf_op jit(solution)/shard_map/all_to_all | solution.py:411
  254.4 10.0 %spectra.5 = (bf16[15,64,1536]{2,1,0:T(8,128)(2,1)}, bf16[15,64,1536]{2,1,0:T(8,128)(2,1)}, f32[2,128,128]{2,1,0:T(8,128)S(1)}) custom-call(s32[1]{0:T(128)} %constant.32.clone.1.ticket_ref, s32[8]{0:T(128)S(1)} %multiply_minimum_fusion.window_start, bf16[2048,1536]{1,0:T(8,128)(2,1)} %bitcast.4.history, bf16[8,256,512]{2,1,0:T(8,128)(2,1)S(1)} %bitcast.13, ...), custom_call_target="tpu_custom_call" | custom-call | flops 1 | bytes 1 | tf_op jit(solution)/shard_map/spectra/pallas_call | solution.py:178
  266.0 3.9 prepare.7
  269.9 61.1 %collective-permute-done.refs_4_ = bf16[15,64,1536]{2,1,0:T(8,128)(2,1)} collective-permute-done((bf16[15,64,1536]{2,1,0:T(8,128)(2,1)}, bf16[15,64,1536]{2,1,0:T(8,128)(2,1)}, u32[]{:S(2)}, u32[]{:S(2)}) %collective-permute-start) | collective-permute-done | bytes 2949152 | tf_op jit(solution)/shard_map/ppermute | solution.py:437
  331.0 17.4 %all-to-all-done.3 = bf16[8,256,1024]{2,1,0:T(8,128)(2,1)} async-done(((bf16[8,256,1024]{2,1,0:T(8,128)(2,1)}), bf16[8,256,1024]{2,1,0:T(8,128)(2,1)}, u32[]{:S(2)}, u32[]{:S(2)}) %all-to-all-start.3) | async-done | bytes 4194336 | tf_op jit(solution)/shard_map/all_to_all | solution.py:411
  348.4 4.4 all-to-all-start.2
  352.8 8.2 %spectra.6 = (bf16[15,64,1024]{2,1,0:T(8,128)(2,1)}, bf16[15,64,1024]{2,1,0:T(8,128)(2,1)}, f32[2,128,128]{2,1,0:T(8,128)S(1)}) custom-call(s32[1]{0:T(128)} %constant.32.clone.1.ticket_ref, s32[8]{0:T(128)S(1)} %multiply_minimum_fusion.window_start, bf16[2048,1024]{1,0:T(8,128)(2,1)} %bitcast.6.history, bf16[8,256,512]{2,1,0:T(8,128)(2,1)S(1)} %bitcast.14, ...), custom_call_target="tpu_custom_call" | custom-call | flops 1 | bytes 1 | tf_op jit(solution)/shard_map/spectra/pallas_call | solution.py:178
  362.6 39.3 %all-to-all-done.2 = bf16[8,256,512]{2,1,0:T(8,128)(2,1)} async-done(((bf16[8,256,512]{2,1,0:T(8,128)(2,1)}), bf16[8,256,512]{2,1,0:T(8,128)(2,1)}, u32[]{:S(2)}, u32[]{:S(2)}) %all-to-all-start.2) | async-done | bytes 2097184 | tf_op jit(solution)/shard_map/all_to_all | solution.py:411
  401.8 5.7 %spectra.7 = (bf16[15,64,512]{2,1,0:T(8,128)(2,1)}, bf16[15,64,512]{2,1,0:T(8,128)(2,1)}, f32[2,128,128]{2,1,0:T(8,128)S(1)}) custom-call(s32[1]{0:T(128)} %constant.32.clone.1.ticket_ref, s32[8]{0:T(128)S(1)} %multiply_minimum_fusion.window_start, bf16[2048,512]{1,0:T(8,128)(2,1)} %bitcast.5.history, bf16[8,256,512]{2,1,0:T(8,128)(2,1)S(1)} %bitcast.15, ...), custom_call_target="tpu_custom_call" | custom-call | flops 1 | bytes 1 | tf_op jit(solution)/shard_map/spectra/pallas_call | solution.py:178
  409.1 2.8 collective-permute-done.2
  416.1 3.1 collective-permute-start.4
  419.2 2.4 collective-permute-done.6
  421.6 2.0 collective-permute-done.5
  425.2 7.9 %modes.2 = (f32[2,32,8,1024]{3,2,1,0:T(8,128)}, bf16[4,16,256]{2,1,0:T(8,128)(2,1)S(1)}, f32[4,8,128]{2,1,0:T(8,128)S(1)}, f32[4,8,128]{2,1,0:T(8,128)S(1)}) custom-call(s32[1]{0:T(128)} %bitcast.member_ref, f32[128,128]{1,0:T(8,128)S(1)} %add_add_fusion.refs_0_, bf16[15,64,1024]{2,1,0:T(8,128)(2,1)S(1)} %copy-done, bf16[15,64,1024]{2,1,0:T(8,128)(2,1)S(1)} %copy-done.2, ...), custom_call_target="tpu_custom_call" | custom-call | flops 1 | bytes 1 | tf_op jit(solution)/shard_map/modes/pallas_call | solution.py:331
  (51 shorter events, 21.0 us)
Async XLA Ops:
  5.7 100.5 %all-to-all-start = ((bf16[8,256,1024]{2,1,0:T(8,128)(2,1)}), bf16[8,256,1024]{2,1,0:T(8,128)(2,1)}, u32[]{:S(2)}, u32[]{:S(2)}) async-start(bf16[8,256,1024]{2,1,0:T(8,128)(2,1)} %prepare.4), calls=%async_computation | async-start | bytes 8388608 | tf_op jit(solution)/shard_map/all_to_all | solution.py:411
  18.4 93.9 %copy-start.5 = (s32[15]{0:T(128)S(1)}, s32[15]{0:T(128)}, u32[]{:S(2)}) copy-start(s32[15]{0:T(128)} %param.4) | copy-start | bytes 184
  18.4 95.3 %copy-start.6 = (s32[64]{0:T(128)S(1)}, s32[64]{0:T(128)}, u32[]{:S(2)}) copy-start(s32[64]{0:T(128)} %param.5) | copy-start | bytes 772
  106.1 143.7 %all-to-all-start.1 = ((bf16[8,256,1536]{2,1,0:T(8,128)(2,1)}), bf16[8,256,1536]{2,1,0:T(8,128)(2,1)}, u32[]{:S(2)}, u32[]{:S(2)}) async-start(bf16[8,256,1536]{2,1,0:T(8,128)(2,1)} %prepare.5), calls=%async_computation.1 | async-start | bytes 12582912 | tf_op jit(solution)/shard_map/all_to_all | solution.py:411
  132.9 45.4 %collective-permute-start.1 = (bf16[15,64,1024]{2,1,0:T(8,128)(2,1)}, bf16[15,64,1024]{2,1,0:T(8,128)(2,1)S(1)}, u32[]{:S(2)}, u32[]{:S(2)}) collective-permute-start(bf16[15,64,1024]{2,1,0:T(8,128)(2,1)} %get-tuple-element.51), channel_id=1, source_target_pairs={{0,2},{2,0},{1,3},{3,1},{4,6},{6,4},{5,7},{7,5},{8,10},{10,8},{9,1... | collective-permute-start | bytes 5898248 | tf_op jit(solution)/shard_map/ppermute | solution.py:437
  178.3 1.3 copy-start.1
  249.8 98.6 %all-to-all-start.3 = ((bf16[8,256,1024]{2,1,0:T(8,128)(2,1)}), bf16[8,256,1024]{2,1,0:T(8,128)(2,1)}, u32[]{:S(2)}, u32[]{:S(2)}) async-start(bf16[8,256,1024]{2,1,0:T(8,128)(2,1)} %prepare.6), calls=%async_computation.3 | async-start | bytes 8388608 | tf_op jit(solution)/shard_map/all_to_all | solution.py:411
  264.4 66.5 %collective-permute-start = (bf16[15,64,1536]{2,1,0:T(8,128)(2,1)}, bf16[15,64,1536]{2,1,0:T(8,128)(2,1)}, u32[]{:S(2)}, u32[]{:S(2)}) collective-permute-start(bf16[15,64,1536]{2,1,0:T(8,128)(2,1)} %get-tuple-element.48), channel_id=1, source_target_pairs={{0,2},{2,0},{1,3},{3,1},{4,6},{6,4},{5,7},{7,5},{8,10},{10,8},{9,1... | collective-permute-start | bytes 8847368 | tf_op jit(solution)/shard_map/ppermute | solution.py:437
  348.4 53.4 %all-to-all-start.2 = ((bf16[8,256,512]{2,1,0:T(8,128)(2,1)}), bf16[8,256,512]{2,1,0:T(8,128)(2,1)}, u32[]{:S(2)}, u32[]{:S(2)}) async-start(bf16[8,256,512]{2,1,0:T(8,128)(2,1)} %prepare.7), calls=%async_computation.2 | async-start | bytes 4194304 | tf_op jit(solution)/shard_map/all_to_all | solution.py:411
  361.0 62.6 %collective-permute-start.7 = (bf16[15,64,1024]{2,1,0:T(8,128)(2,1)}, bf16[15,64,1024]{2,1,0:T(8,128)(2,1)}, u32[]{:S(2)}, u32[]{:S(2)}) collective-permute-start(bf16[15,64,1024]{2,1,0:T(8,128)(2,1)} %get-tuple-element.63), channel_id=1, source_target_pairs={{0,2},{2,0},{1,3},{3,1},{4,6},{6,4},{5,7},{7,5},{8,10},{10,8},{9,1... | collective-permute-start | bytes 5898248 | tf_op jit(solution)/shard_map/ppermute | solution.py:437
  401.8 21.8 %copy-start = (bf16[15,64,1024]{2,1,0:T(8,128)(2,1)S(1)}, bf16[15,64,1024]{2,1,0:T(8,128)(2,1)}, u32[]{:S(2)}) copy-start(bf16[15,64,1024]{2,1,0:T(8,128)(2,1)} %get-tuple-element.58.refs_1_) | copy-start | bytes 5898244
  401.8 21.8 %copy-start.2 = (bf16[15,64,1024]{2,1,0:T(8,128)(2,1)S(1)}, bf16[15,64,1024]{2,1,0:T(8,128)(2,1)}, u32[]{:S(2)}) copy-start(bf16[15,64,1024]{2,1,0:T(8,128)(2,1)} %copy-done.1) | copy-start | bytes 5898244
  407.6 4.3 collective-permute-start.2
  411.9 22.4 %collective-permute-start.8 = (bf16[15,64,512]{2,1,0:T(8,128)(2,1)}, bf16[15,64,512]{2,1,0:T(8,128)(2,1)S(1)}, u32[]{:S(2)}, u32[]{:S(2)}) collective-permute-start(bf16[15,64,512]{2,1,0:T(8,128)(2,1)} %get-tuple-element.67), channel_id=1, source_target_pairs={{0,2},{2,0},{1,3},{3,1},{4,6},{6,4},{5,7},{7,5},{8,10},{10,8},{9,1... | collective-permute-start | bytes 2949128 | tf_op jit(solution)/shard_map/ppermute | solution.py:437
  413.4 1.3 collective-permute-start.3
  414.8 6.9 %collective-permute-start.6 = (f32[128,128]{1,0:T(8,128)S(1)}, f32[128,128]{1,0:T(8,128)S(1)}, u32[]{:S(2)}, u32[]{:S(2)}) collective-permute-start(f32[128,128]{1,0:T(8,128)S(1)} %add.75), channel_id=1, source_target_pairs={{0,12},{1,13},{4,8},{5,9},{8,4},{9,5},{12,0},{13,1},{2,14},{3,15},... | collective-permute-start | bytes 196616 | tf_op jit(solution)/shard_map/ppermute | solution.py:363
  416.1 7.5 %collective-permute-start.5 = (f32[128,128]{1,0:T(8,128)S(1)}, f32[128,128]{1,0:T(8,128)S(1)}, u32[]{:S(2)}, u32[]{:S(2)}) collective-permute-start(f32[128,128]{1,0:T(8,128)S(1)} %add.75), channel_id=1, source_target_pairs={{0,8},{1,9},{4,12},{5,13},{8,0},{9,1},{12,4},{13,5},{2,10},{3,11},... | collective-permute-start | bytes 196616 | tf_op jit(solution)/shard_map/ppermute | solution.py:363
  416.1 7.5 %collective-permute-start.4 = (f32[128,128]{1,0:T(8,128)S(1)}, f32[128,128]{1,0:T(8,128)S(1)}, u32[]{:S(2)}, u32[]{:S(2)}) collective-permute-start(f32[128,128]{1,0:T(8,128)S(1)} %add.75), channel_id=1, source_target_pairs={{0,4},{1,5},{4,0},{5,1},{8,12},{9,13},{12,8},{13,9},{2,6},{3,7},{6... | collective-permute-start | bytes 196616 | tf_op jit(solution)/shard_map/ppermute | solution.py:363
  423.6 1.5 copy-start.3
  425.2 9.1 %copy-start.4 = (bf16[15,64,512]{2,1,0:T(8,128)(2,1)S(1)}, bf16[15,64,512]{2,1,0:T(8,128)(2,1)}, u32[]{:S(2)}) copy-start(bf16[15,64,512]{2,1,0:T(8,128)(2,1)} %get-tuple-element.66.refs_2_) | copy-start | bytes 2949124

commit v6 on v5

--- a/solution.py
+++ b/solution.py
@@ -15,7 +15,7 @@
 SUBLANES = 8
 SHORT = pl.CostEstimate(flops=1, bytes_accessed=1, transcendentals=0)
 PREPARE_ROWS = 64
-UNROLL_MODES = 2
+UNROLL_MODES = 4
 PREPARE_PIECES = 8
 AHEAD = 2
 GROUP_ROWS = 2 * SUBLANES

time: 438 us -> 438 us (level)
  no operation moved by 1% of the time
where the time goes in v6:
time: 438 us; the launch traced here: 436 us
  waiting for transfers between devices  324 us (74%)
  Pallas kernels  61.9 us (14%)
  starting transfers between devices  32.3 us (7%)
  other arithmetic  11.3 us (3%)
  local copies, waits for them, and re-layouts  5.16 us (1%)
    all_to_all x4, waiting for transfers between devices, exchange(): lax.all_to_all(parts, line, split_axis=0, concat_axis=0, tiled=True)  215 us
    ppermute x4, waiting for transfers between devices, shards(): sent[turn] = lax.ppermute(sent[turn], 'freq', rings[turn])  101 us
    pallas_call x4, Pallas kernels, spectra(): pl.pallas_call(functools.partial(spectra_kernel, members=members, unroll=...  32.3 us
    pallas_call x4, Pallas kernels, prepare(): pl.pallas_call(functools.partial(prepare_kernel, units=units), grid_spec=...  20.4 us
    all_to_all x4, starting transfers between devices, exchange(): lax.all_to_all(parts, line, split_axis=0, concat_axis=0, tiled=True)  20 us
    pallas_call x2, Pallas kernels, project(): pl.pallas_call(functools.partial(modes_kernel, chunks=chunks, members=mem...  9.24 us
  transfers between devices with their start and end apart: 13, of which 11 were waited for; matrix products, arithmetic and copies ran while one was open for 3% of the time, Pallas kernels for 13%

profile of v6, /device:TPU:0, one launch (start us, length us, event | category | flops | bytes accessed | tf_op | source)
XLA Modules:
  0.0 436.2 jit_solution(9537920419216657224)
XLA Ops:
  0.6 5.0 %prepare.4 = bf16[8,256,1024]{2,1,0:T(8,128)(2,1)} custom-call(s32[1]{0:T(128)} %constant.32.clone.1.ticket_ref, bf16[256,4,8192]{2,1,0:T(4,128)(2,1)} %refs_7_.7, bf16[256,4,8192]{2,1,0:T(4,128)(2,1)} %refs_7_.7, bf16[256,4,8192]{2,1,0:T(4,128)(2,1)} %refs_7_.7, bf16[256,4,8192]{2,1,0:T(4,128)(2,1)} %refs_7_.7, bf16[256,4,8192]{2,1,0:T(4,128)(2,1)} %refs_7_.7, ...), custom_call_target="tpu_custom_call" | custom-call | flops 1 | bytes 1 | tf_op jit(solution)/shard_map/prepare/pallas_call | solution.py:65
  5.7 6.3 %all-to-all-start = ((bf16[8,256,1024]{2,1,0:T(8,128)(2,1)}), bf16[8,256,1024]{2,1,0:T(8,128)(2,1)}, u32[]{:S(2)}, u32[]{:S(2)}) async-start(bf16[8,256,1024]{2,1,0:T(8,128)(2,1)} %prepare.4), calls=%async_computation | async-start | bytes 8388608 | tf_op jit(solution)/shard_map/all_to_all | solution.py:411
  12.0 6.4 %prepare.5 = bf16[8,256,1536]{2,1,0:T(8,128)(2,1)} custom-call(s32[1]{0:T(128)} %constant.32.clone.1.ticket_ref, bf16[256,4,8192]{2,1,0:T(4,128)(2,1)} %refs_7_.7, bf16[256,4,8192]{2,1,0:T(4,128)(2,1)} %refs_7_.7, bf16[256,4,8192]{2,1,0:T(4,128)(2,1)} %refs_7_.7, bf16[256,4,8192]{2,1,0:T(4,128)(2,1)} %refs_7_.7, bf16[256,4,8192]{2,1,0:T(4,128)(2,1)} %refs_7_.7, ...), custom_call_target="tpu_custom_call" | custom-call | flops 1 | bytes 1 | tf_op jit(solution)/shard_map/prepare/pallas_call | solution.py:65
  18.4 87.7 %all-to-all-done = bf16[8,256,1024]{2,1,0:T(8,128)(2,1)} async-done(((bf16[8,256,1024]{2,1,0:T(8,128)(2,1)}), bf16[8,256,1024]{2,1,0:T(8,128)(2,1)}, u32[]{:S(2)}, u32[]{:S(2)}) %all-to-all-start) | async-done | bytes 4194336 | tf_op jit(solution)/shard_map/all_to_all | solution.py:411
  106.1 4.7 %all-to-all-start.1 = ((bf16[8,256,1536]{2,1,0:T(8,128)(2,1)}), bf16[8,256,1536]{2,1,0:T(8,128)(2,1)}, u32[]{:S(2)}, u32[]{:S(2)}) async-start(bf16[8,256,1536]{2,1,0:T(8,128)(2,1)} %prepare.5), calls=%async_computation.1 | async-start | bytes 12582912 | tf_op jit(solution)/shard_map/all_to_all | solution.py:411
  115.6 8.2 %fusion.4 = (f32[16,8,1,8,512]{4,3,2,1,0:T(8,128)S(1)}, f32[16,8,1,8,512]{4,3,2,1,0:T(8,128)S(1)}) fusion(s32[16,512]{1,0:T(8,128)S(1)} %fusion.5, s32[8,8]{1,0:T(8,128)S(1)} %mul.86), kind=kLoop, calls=%fused_computation.12 | loop fusion | flops 7864320 | bytes 4227328 | tf_op jit(solution)/shard_map/cos | solution.py:36
  124.5 8.4 %spectra.4 = (bf16[15,64,1024]{2,1,0:T(8,128)(2,1)}, bf16[15,64,1024]{2,1,0:T(8,128)(2,1)}, f32[2,128,128]{2,1,0:T(8,128)S(1)}) custom-call(s32[1]{0:T(128)} %constant.32.clone.1.ticket_ref, s32[8]{0:T(128)S(1)} %multiply_minimum_fusion.window_start, bf16[2048,1024]{1,0:T(8,128)(2,1)} %bitcast.1.history, bf16[8,256,512]{2,1,0:T(8,128)(2,1)S(1)} %bitcast.12, ...), custom_call_target="tpu_custom_call" | custom-call | flops 1 | bytes 1 | tf_op jit(solution)/shard_map/spectra/pallas_call | solution.py:178
  134.5 5.1 %prepare.6 = bf16[8,256,1024]{2,1,0:T(8,128)(2,1)} custom-call(s32[1]{0:T(128)} %constant.32.clone.1.ticket_ref, bf16[256,4,8192]{2,1,0:T(4,128)(2,1)} %refs_7_.7, bf16[256,4,8192]{2,1,0:T(4,128)(2,1)} %refs_7_.7, bf16[256,4,8192]{2,1,0:T(4,128)(2,1)} %refs_7_.7, bf16[256,4,8192]{2,1,0:T(4,128)(2,1)} %refs_7_.7, bf16[256,4,8192]{2,1,0:T(4,128)(2,1)} %refs_7_.7, ...), custom_call_target="tpu_custom_call" | custom-call | flops 1 | bytes 1 | tf_op jit(solution)/shard_map/prepare/pallas_call | solution.py:65
  139.5 38.7 %collective-permute-done.1.refs_2_ = bf16[15,64,1024]{2,1,0:T(8,128)(2,1)S(1)} collective-permute-done((bf16[15,64,1024]{2,1,0:T(8,128)(2,1)}, bf16[15,64,1024]{2,1,0:T(8,128)(2,1)S(1)}, u32[]{:S(2)}, u32[]{:S(2)}) %collective-permute-start.1) | collective-permute-done | bytes 1966112 | tf_op jit(solution)/shard_map/ppermute | solution.py:437
  179.6 70.2 %all-to-all-done.1 = bf16[8,256,1536]{2,1,0:T(8,128)(2,1)} async-done(((bf16[8,256,1536]{2,1,0:T(8,128)(2,1)}), bf16[8,256,1536]{2,1,0:T(8,128)(2,1)}, u32[]{:S(2)}, u32[]{:S(2)}) %all-to-all-start.1) | async-done | bytes 6291488 | tf_op jit(solution)/shard_map/all_to_all | solution.py:411
  249.8 4.6 %all-to-all-start.3 = ((bf16[8,256,1024]{2,1,0:T(8,128)(2,1)}), bf16[8,256,1024]{2,1,0:T(8,128)(2,1)}, u32[]{:S(2)}, u32[]{:S(2)}) async-start(bf16[8,256,1024]{2,1,0:T(8,128)(2,1)} %prepare.6), calls=%async_computation.3 | async-start | bytes 8388608 | tf_op jit(solution)/shard_map/all_to_all | solution.py:411
  254.4 10.0 %spectra.5 = (bf16[15,64,1536]{2,1,0:T(8,128)(2,1)}, bf16[15,64,1536]{2,1,0:T(8,128)(2,1)}, f32[2,128,128]{2,1,0:T(8,128)S(1)}) custom-call(s32[1]{0:T(128)} %constant.32.clone.1.ticket_ref, s32[8]{0:T(128)S(1)} %multiply_minimum_fusion.window_start, bf16[2048,1536]{1,0:T(8,128)(2,1)} %bitcast.4.history, bf16[8,256,512]{2,1,0:T(8,128)(2,1)S(1)} %bitcast.13, ...), custom_call_target="tpu_custom_call" | custom-call | flops 1 | bytes 1 | tf_op jit(solution)/shard_map/spectra/pallas_call | solution.py:178
  266.0 3.9 prepare.7
  269.9 61.1 %collective-permute-done.refs_4_ = bf16[15,64,1536]{2,1,0:T(8,128)(2,1)} collective-permute-done((bf16[15,64,1536]{2,1,0:T(8,128)(2,1)}, bf16[15,64,1536]{2,1,0:T(8,128)(2,1)}, u32[]{:S(2)}, u32[]{:S(2)}) %collective-permute-start) | collective-permute-done | bytes 2949152 | tf_op jit(solution)/shard_map/ppermute | solution.py:437
  331.0 17.4 %all-to-all-done.3 = bf16[8,256,1024]{2,1,0:T(8,128)(2,1)} async-done(((bf16[8,256,1024]{2,1,0:T(8,128)(2,1)}), bf16[8,256,1024]{2,1,0:T(8,128)(2,1)}, u32[]{:S(2)}, u32[]{:S(2)}) %all-to-all-start.3) | async-done | bytes 4194336 | tf_op jit(solution)/shard_map/all_to_all | solution.py:411
  348.4 4.4 all-to-all-start.2
  352.8 8.2 %spectra.6 = (bf16[15,64,1024]{2,1,0:T(8,128)(2,1)}, bf16[15,64,1024]{2,1,0:T(8,128)(2,1)}, f32[2,128,128]{2,1,0:T(8,128)S(1)}) custom-call(s32[1]{0:T(128)} %constant.32.clone.1.ticket_ref, s32[8]{0:T(128)S(1)} %multiply_minimum_fusion.window_start, bf16[2048,1024]{1,0:T(8,128)(2,1)} %bitcast.6.history, bf16[8,256,512]{2,1,0:T(8,128)(2,1)S(1)} %bitcast.14, ...), custom_call_target="tpu_custom_call" | custom-call | flops 1 | bytes 1 | tf_op jit(solution)/shard_map/spectra/pallas_call | solution.py:178
  362.6 39.3 %all-to-all-done.2 = bf16[8,256,512]{2,1,0:T(8,128)(2,1)} async-done(((bf16[8,256,512]{2,1,0:T(8,128)(2,1)}), bf16[8,256,512]{2,1,0:T(8,128)(2,1)}, u32[]{:S(2)}, u32[]{:S(2)}) %all-to-all-start.2) | async-done | bytes 2097184 | tf_op jit(solution)/shard_map/all_to_all | solution.py:411
  401.8 5.7 %spectra.7 = (bf16[15,64,512]{2,1,0:T(8,128)(2,1)}, bf16[15,64,512]{2,1,0:T(8,128)(2,1)}, f32[2,128,128]{2,1,0:T(8,128)S(1)}) custom-call(s32[1]{0:T(128)} %constant.32.clone.1.ticket_ref, s32[8]{0:T(128)S(1)} %multiply_minimum_fusion.window_start, bf16[2048,512]{1,0:T(8,128)(2,1)} %bitcast.5.history, bf16[8,256,512]{2,1,0:T(8,128)(2,1)S(1)} %bitcast.15, ...), custom_call_target="tpu_custom_call" | custom-call | flops 1 | bytes 1 | tf_op jit(solution)/shard_map/spectra/pallas_call | solution.py:178
  409.1 2.8 collective-permute-done.2
  416.1 3.1 collective-permute-start.4
  419.2 2.4 collective-permute-done.6
  421.6 2.0 collective-permute-done.5
  425.2 7.5 %modes.2 = (f32[2,32,8,1024]{3,2,1,0:T(8,128)}, bf16[4,16,256]{2,1,0:T(8,128)(2,1)S(1)}, f32[4,8,128]{2,1,0:T(8,128)S(1)}, f32[4,8,128]{2,1,0:T(8,128)S(1)}) custom-call(s32[1]{0:T(128)} %bitcast.member_ref, f32[128,128]{1,0:T(8,128)S(1)} %add_add_fusion.refs_0_, bf16[15,64,1024]{2,1,0:T(8,128)(2,1)S(1)} %copy-done, bf16[15,64,1024]{2,1,0:T(8,128)(2,1)S(1)} %copy-done.2, ...), custom_call_target="tpu_custom_call" | custom-call | flops 1 | bytes 1 | tf_op jit(solution)/shard_map/modes/pallas_call | solution.py:331
  (51 shorter events, 21.3 us)
Async XLA Ops:
  5.7 100.5 %all-to-all-start = ((bf16[8,256,1024]{2,1,0:T(8,128)(2,1)}), bf16[8,256,1024]{2,1,0:T(8,128)(2,1)}, u32[]{:S(2)}, u32[]{:S(2)}) async-start(bf16[8,256,1024]{2,1,0:T(8,128)(2,1)} %prepare.4), calls=%async_computation | async-start | bytes 8388608 | tf_op jit(solution)/shard_map/all_to_all | solution.py:411
  18.4 93.9 %copy-start.5 = (s32[15]{0:T(128)S(1)}, s32[15]{0:T(128)}, u32[]{:S(2)}) copy-start(s32[15]{0:T(128)} %param.4) | copy-start | bytes 184
  18.4 95.3 %copy-start.6 = (s32[64]{0:T(128)S(1)}, s32[64]{0:T(128)}, u32[]{:S(2)}) copy-start(s32[64]{0:T(128)} %param.5) | copy-start | bytes 772
  106.1 143.7 %all-to-all-start.1 = ((bf16[8,256,1536]{2,1,0:T(8,128)(2,1)}), bf16[8,256,1536]{2,1,0:T(8,128)(2,1)}, u32[]{:S(2)}, u32[]{:S(2)}) async-start(bf16[8,256,1536]{2,1,0:T(8,128)(2,1)} %prepare.5), calls=%async_computation.1 | async-start | bytes 12582912 | tf_op jit(solution)/shard_map/all_to_all | solution.py:411
  132.9 45.4 %collective-permute-start.1 = (bf16[15,64,1024]{2,1,0:T(8,128)(2,1)}, bf16[15,64,1024]{2,1,0:T(8,128)(2,1)S(1)}, u32[]{:S(2)}, u32[]{:S(2)}) collective-permute-start(bf16[15,64,1024]{2,1,0:T(8,128)(2,1)} %get-tuple-element.51), channel_id=1, source_target_pairs={{0,2},{2,0},{1,3},{3,1},{4,6},{6,4},{5,7},{7,5},{8,10},{10,8},{9,1... | collective-permute-start | bytes 5898248 | tf_op jit(solution)/shard_map/ppermute | solution.py:437
  178.3 1.3 copy-start.1
  249.8 98.6 %all-to-all-start.3 = ((bf16[8,256,1024]{2,1,0:T(8,128)(2,1)}), bf16[8,256,1024]{2,1,0:T(8,128)(2,1)}, u32[]{:S(2)}, u32[]{:S(2)}) async-start(bf16[8,256,1024]{2,1,0:T(8,128)(2,1)} %prepare.6), calls=%async_computation.3 | async-start | bytes 8388608 | tf_op jit(solution)/shard_map/all_to_all | solution.py:411
  264.4 66.5 %collective-permute-start = (bf16[15,64,1536]{2,1,0:T(8,128)(2,1)}, bf16[15,64,1536]{2,1,0:T(8,128)(2,1)}, u32[]{:S(2)}, u32[]{:S(2)}) collective-permute-start(bf16[15,64,1536]{2,1,0:T(8,128)(2,1)} %get-tuple-element.48), channel_id=1, source_target_pairs={{0,2},{2,0},{1,3},{3,1},{4,6},{6,4},{5,7},{7,5},{8,10},{10,8},{9,1... | collective-permute-start | bytes 8847368 | tf_op jit(solution)/shard_map/ppermute | solution.py:437
  348.4 53.4 %all-to-all-start.2 = ((bf16[8,256,512]{2,1,0:T(8,128)(2,1)}), bf16[8,256,512]{2,1,0:T(8,128)(2,1)}, u32[]{:S(2)}, u32[]{:S(2)}) async-start(bf16[8,256,512]{2,1,0:T(8,128)(2,1)} %prepare.7), calls=%async_computation.2 | async-start | bytes 4194304 | tf_op jit(solution)/shard_map/all_to_all | solution.py:411
  361.0 62.6 %collective-permute-start.7 = (bf16[15,64,1024]{2,1,0:T(8,128)(2,1)}, bf16[15,64,1024]{2,1,0:T(8,128)(2,1)}, u32[]{:S(2)}, u32[]{:S(2)}) collective-permute-start(bf16[15,64,1024]{2,1,0:T(8,128)(2,1)} %get-tuple-element.63), channel_id=1, source_target_pairs={{0,2},{2,0},{1,3},{3,1},{4,6},{6,4},{5,7},{7,5},{8,10},{10,8},{9,1... | collective-permute-start | bytes 5898248 | tf_op jit(solution)/shard_map/ppermute | solution.py:437
  401.8 21.8 %copy-start = (bf16[15,64,1024]{2,1,0:T(8,128)(2,1)S(1)}, bf16[15,64,1024]{2,1,0:T(8,128)(2,1)}, u32[]{:S(2)}) copy-start(bf16[15,64,1024]{2,1,0:T(8,128)(2,1)} %get-tuple-element.58.refs_1_) | copy-start | bytes 5898244
  401.8 21.8 %copy-start.2 = (bf16[15,64,1024]{2,1,0:T(8,128)(2,1)S(1)}, bf16[15,64,1024]{2,1,0:T(8,128)(2,1)}, u32[]{:S(2)}) copy-start(bf16[15,64,1024]{2,1,0:T(8,128)(2,1)} %copy-done.1) | copy-start | bytes 5898244
  407.6 4.3 collective-permute-start.2
  411.9 22.4 %collective-permute-start.8 = (bf16[15,64,512]{2,1,0:T(8,128)(2,1)}, bf16[15,64,512]{2,1,0:T(8,128)(2,1)S(1)}, u32[]{:S(2)}, u32[]{:S(2)}) collective-permute-start(bf16[15,64,512]{2,1,0:T(8,128)(2,1)} %get-tuple-element.67), channel_id=1, source_target_pairs={{0,2},{2,0},{1,3},{3,1},{4,6},{6,4},{5,7},{7,5},{8,10},{10,8},{9,1... | collective-permute-start | bytes 2949128 | tf_op jit(solution)/shard_map/ppermute | solution.py:437
  413.4 1.3 collective-permute-start.3
  414.8 6.9 %collective-permute-start.6 = (f32[128,128]{1,0:T(8,128)S(1)}, f32[128,128]{1,0:T(8,128)S(1)}, u32[]{:S(2)}, u32[]{:S(2)}) collective-permute-start(f32[128,128]{1,0:T(8,128)S(1)} %add.75), channel_id=1, source_target_pairs={{0,12},{1,13},{4,8},{5,9},{8,4},{9,5},{12,0},{13,1},{2,14},{3,15},... | collective-permute-start | bytes 196616 | tf_op jit(solution)/shard_map/ppermute | solution.py:363
  416.1 7.5 %collective-permute-start.5 = (f32[128,128]{1,0:T(8,128)S(1)}, f32[128,128]{1,0:T(8,128)S(1)}, u32[]{:S(2)}, u32[]{:S(2)}) collective-permute-start(f32[128,128]{1,0:T(8,128)S(1)} %add.75), channel_id=1, source_target_pairs={{0,8},{1,9},{4,12},{5,13},{8,0},{9,1},{12,4},{13,5},{2,10},{3,11},... | collective-permute-start | bytes 196616 | tf_op jit(solution)/shard_map/ppermute | solution.py:363
  416.1 7.5 %collective-permute-start.4 = (f32[128,128]{1,0:T(8,128)S(1)}, f32[128,128]{1,0:T(8,128)S(1)}, u32[]{:S(2)}, u32[]{:S(2)}) collective-permute-start(f32[128,128]{1,0:T(8,128)S(1)} %add.75), channel_id=1, source_target_pairs={{0,4},{1,5},{4,0},{5,1},{8,12},{9,13},{12,8},{13,9},{2,6},{3,7},{6... | collective-permute-start | bytes 196616 | tf_op jit(solution)/shard_map/ppermute | solution.py:363
  423.6 1.5 copy-start.3
  425.2 9.1 %copy-start.4 = (bf16[15,64,512]{2,1,0:T(8,128)(2,1)S(1)}, bf16[15,64,512]{2,1,0:T(8,128)(2,1)}, u32[]{:S(2)}) copy-start(bf16[15,64,512]{2,1,0:T(8,128)(2,1)} %get-tuple-element.66.refs_2_) | copy-start | bytes 2949124
